TPU v7x, 32 devices: a whole 2x2x4 slice. The times are simulated.
32 devices in a mesh: grp: 4 (over x, core), wide: 8 (over z, y).
Axes of the slice: x: 2, y: 2, z: 4, core: 2. Of those that a mesh axis runs over, the one named last changes fastest.
Arguments:
- tokens: bfloat16 [4096, 768], P(('grp', 'wide')), may hold values from -6 to 6
- frames: bfloat16 [2048, 768], P(('grp', 'wide')), may hold values from -6 to 6
- cotangent: bfloat16 [4096, 768], P(('grp', 'wide')), may hold values from -6 to 6
- item_lengths: int32 [4, 4], P('grp'), may hold values from 1 to 512, 1024 in all within a row
- frame_lengths: int32 [4, 4], P('grp'), may hold values from 1 to 256, 512 in all within a row
- attn_inputs: bfloat16 [768, 2304], P('wide'), may hold values from -0.21875 to 0.21875
- attn_output: bfloat16 [768, 768], P('wide'), may hold values from -1.75 to 1.75
- cross_queries: bfloat16 [768, 768], P('wide'), may hold values from -0.21875 to 0.21875
- cross_memory: bfloat16 [768, 1536], P('wide'), may hold values from -0.21875 to 0.21875
- cross_output: bfloat16 [768, 768], P('wide'), may hold values from -1.75 to 1.75
- mlp_inputs: bfloat16 [768, 3072], P('wide'), may hold values from -0.21875 to 0.21875
- mlp_output: bfloat16 [3072, 768], P('wide'), may hold values from -0.109375 to 0.109375
- norm_gains: bfloat16 [3, 768], P(None, 'wide'), may hold values from 0.5 to 1.5
- bias_rows: bfloat16 [10, 768], P(None, 'wide'), may hold values from -4 to 4
- mlp_bias: bfloat16 [3072], P('wide'), may hold values from -4 to 4
Outputs:
- block_output: bfloat16 [4096, 768], P(('grp', 'wide'))
- grad_tokens: float32 [4096, 768], P(('grp', 'wide'))
- grad_frames: float32 [2048, 768], P(('grp', 'wide'))
- grad_attn_inputs: float32 [768, 2304], P('wide')
- grad_attn_output: float32 [768, 768], P('wide')
- grad_cross_queries: float32 [768, 768], P('wide')
- grad_cross_memory: float32 [768, 1536], P('wide')
- grad_cross_output: float32 [768, 768], P('wide')
- grad_mlp_inputs: float32 [768, 3072], P('wide')
- grad_mlp_output: float32 [3072, 768], P('wide')
- grad_norm_gains: float32 [3, 768], P(None, 'wide')
- grad_bias_rows: float32 [10, 768], P(None, 'wide')
- grad_mlp_bias: float32 [3072], P('wide')
Inputs may be any that keep to these rules, and one draw needn't show every extreme that they name: `item_lengths`: row g gives the lengths of the 4 items packed in order into group g's 1024 token slots; they sum to 1024 and the longest is exactly 512. `frame_lengths`: row g gives the frame counts of the 4 items, laid in the same order over group g's 512 frames; they sum to 512 and the largest is exactly 256.
All inputs are finite; a program needn't handle non-finite values.
Results may differ from a plain program's by a relative error of at most 0.03.
Values may be sent and summed in bfloat16 or wider, within the bound.
No kernel may reach another device: no remote copies, remote signals or barrier semaphores. Data moves between devices by JAX's collectives and lax.ppermute only.
A program may use at most 256 MiB of HBM per device.

v0:
```python
import math

import jax
import jax.numpy as jnp
from jax import lax
from jax.sharding import PartitionSpec as P

HEADS = 12
HEAD_DIM = 64
SPAN = 4


EPSILON = 1e-05
MASKED = -1e30


def shifted(shard, axis, by):
    size = lax.axis_size(axis)
    pairs = [(i, i + by) for i in range(size) if 0 <= i + by < size]
    return lax.ppermute(shard, axis, pairs)


def norm_apply(values, gain, shift):
    centre = jnp.mean(values, axis=-1, keepdims=True)
    centred = values - centre
    spread = jnp.mean(centred * centred, axis=-1, keepdims=True)
    return centred * lax.rsqrt(spread + EPSILON) * gain + shift


def norm_back(values, gain, shift, upstream):
    ignored, pull_back = jax.vjp(norm_apply, values, gain, shift)
    return pull_back(upstream)


def exact_gelu(values):
    return jax.nn.gelu(values, approximate=False)


def split_heads(values):
    return values.reshape(values.shape[0], HEADS, HEAD_DIM)


def merge_heads(values):
    return values.reshape(values.shape[0], HEADS * HEAD_DIM)


def block_length(total_rows):
    length = min(total_rows, 1024)
    while total_rows % length:
        length -= 1
    return length


def project(left_side, right_side):
    return jnp.dot(left_side, right_side, preferred_element_type=jnp.float32)


def project_left(left_side, right_side):
    return lax.dot_general(
        left_side, right_side, (((0,), (0,)), ((), ())), preferred_element_type=jnp.float32
    )


def project_right(left_side, right_side):
    return lax.dot_general(
        left_side, right_side, (((1,), (1,)), ((), ())), preferred_element_type=jnp.float32
    )


def owner_item(positions, ends):
    return jnp.sum((positions[:, None] >= ends[None, :]).astype(jnp.int32), axis=1)


def pack_grads(grad_list, shard_dims, wide_size):
    pieces = []
    for grad_item, split_dim in zip(grad_list, shard_dims):
        pieces.append(jnp.moveaxis(grad_item, split_dim, 0).reshape(wide_size, -1))
    return jnp.concatenate(pieces, axis=1)


def unpack_grads(shard_flat, grad_list, shard_dims, wide_size):
    shards = []
    cursor = 0
    for grad_item, split_dim in zip(grad_list, shard_dims):
        moved_shape = [grad_item.shape[split_dim]] + [
            grad_item.shape[axis_pos] for axis_pos in range(grad_item.ndim) if axis_pos != split_dim
        ]
        local_shape = tuple([moved_shape[0] // wide_size] + moved_shape[1:])
        part_len = math.prod(local_shape)
        shards.append(
            jnp.moveaxis(shard_flat[cursor : cursor + part_len].reshape(local_shape), 0, split_dim)
        )
        cursor += part_len
    return shards


def per_device(
    tokens,
    frames,
    cotangent,
    item_lengths,
    frame_lengths,
    attn_inputs,
    attn_output,
    cross_queries,
    cross_memory,
    cross_output,
    mlp_inputs,
    mlp_output,
    norm_gains,
    bias_rows,
    mlp_bias,
):
    model_width = tokens.shape[1]
    tok_rows = tokens.shape[0]
    frame_rows = frames.shape[0]
    scale_factor = HEAD_DIM ** (-0.5)
    wide_size = lax.axis_size("wide")
    wide_index = lax.axis_index("wide")
    gathered = (
        lax.all_gather(attn_inputs, "wide", axis=0, tiled=True),
        lax.all_gather(attn_output, "wide", axis=0, tiled=True),
        lax.all_gather(cross_queries, "wide", axis=0, tiled=True),
        lax.all_gather(cross_memory, "wide", axis=0, tiled=True),
        lax.all_gather(cross_output, "wide", axis=0, tiled=True),
        lax.all_gather(mlp_inputs, "wide", axis=0, tiled=True),
        lax.all_gather(mlp_output, "wide", axis=0, tiled=True),
        lax.all_gather(norm_gains, "wide", axis=1, tiled=True),
        lax.all_gather(bias_rows, "wide", axis=1, tiled=True),
        lax.all_gather(mlp_bias, "wide", axis=0, tiled=True),
    )
    (
        w_inputs,
        w_output,
        w_cross_q,
        w_memory,
        w_cross_out,
        w_mlp_in,
        w_mlp_out,
        gains_low,
        biases_low,
        mlp_bias_low,
    ) = gathered
    gain_rows = gains_low.astype(jnp.float32)
    biases = biases_low.astype(jnp.float32)
    hidden_bias = mlp_bias_low.astype(jnp.float32)
    zero_row = jnp.zeros((model_width,), jnp.float32)
    lengths = item_lengths[0]
    item_ends = jnp.cumsum(lengths)
    item_starts = item_ends - lengths
    item_ids = jnp.arange(lengths.shape[0], dtype=jnp.int32)
    token_pos = wide_index * tok_rows + jnp.arange(tok_rows, dtype=jnp.int32)
    token_item = owner_item(token_pos, item_ends)
    token_first = jnp.sum(
        jnp.where(token_item[:, None] == item_ids[None, :], item_starts[None, :], 0), axis=1
    )
    inputs = tokens.astype(jnp.float32)
    normed_one_low = norm_apply(inputs, gain_rows[0], biases[0]).astype(jnp.bfloat16)
    projected = (
        project(normed_one_low, w_inputs) + jnp.concatenate([biases[3], zero_row, biases[4]])
    ).astype(jnp.bfloat16)
    query_low = projected[:, :model_width]
    memory_own = projected[:, model_width:]
    earlier = []
    for offset in range(SPAN, 0, -1):
        earlier.append(shifted(memory_own, "wide", offset))
    memory_all = jnp.concatenate(earlier + [memory_own], axis=0)
    key_pos = jnp.concatenate([token_pos - offset * tok_rows for offset in range(SPAN, -1, -1)])
    self_mask = (key_pos[None, :] >= token_first[:, None]) & (
        key_pos[None, :] <= token_pos[:, None]
    )
    queries = split_heads(query_low)
    keys_all = split_heads(memory_all[:, :model_width])
    values_all = split_heads(memory_all[:, model_width:])
    self_scores = (
        jnp.einsum("ihd,jhd->hij", queries, keys_all, preferred_element_type=jnp.float32)
        * scale_factor
    )
    self_probs = jax.nn.softmax(jnp.where(self_mask[None], self_scores, MASKED), axis=-1)
    self_probs_low = self_probs.astype(jnp.bfloat16)
    attended_low = merge_heads(
        jnp.einsum("hij,jhd->ihd", self_probs_low, values_all, preferred_element_type=jnp.float32)
    ).astype(jnp.bfloat16)
    after_one = inputs + project(attended_low, w_output) + biases[5]
    normed_two_low = norm_apply(after_one, gain_rows[1], biases[1]).astype(jnp.bfloat16)
    cross_low = (project(normed_two_low, w_cross_q) + biases[6]).astype(jnp.bfloat16)
    memory_bias = jnp.concatenate([zero_row, biases[7]])
    own_memory = (project(frames, w_memory) + memory_bias).astype(jnp.bfloat16)
    frame_memory = lax.all_gather(own_memory, "wide", axis=0, tiled=True)
    group_frames = frame_memory.shape[0]
    frame_counts = frame_lengths[0]
    frame_ends = jnp.cumsum(frame_counts)
    frame_starts = frame_ends - frame_counts
    frame_block = block_length(group_frames)
    window_low = jnp.sum(jnp.where(item_ids == token_item[0], frame_starts, 0))
    window_high = jnp.sum(jnp.where(item_ids == token_item[tok_rows - 1], frame_ends, 0))
    block_first = window_low // frame_block
    block_end = (window_high + frame_block - 1) // frame_block
    cross_heads = split_heads(cross_low)

    def frame_piece(block_number):
        start = (block_number * frame_block).astype(jnp.int32)
        memory_block = lax.dynamic_slice_in_dim(frame_memory, start, frame_block, 0)
        positions = start + jnp.arange(frame_block, dtype=jnp.int32)
        return (memory_block, owner_item(positions, frame_ends))

    def cross_scores(memory_block, item_block):
        key_heads = split_heads(memory_block[:, :model_width])
        raw_scores = (
            jnp.einsum("ihd,jhd->hij", cross_heads, key_heads, preferred_element_type=jnp.float32)
            * scale_factor
        )
        return jnp.where((token_item[:, None] == item_block[None, :])[None], raw_scores, MASKED)

    def running_total(block_number, carried):
        running_top, running_sum = carried
        memory_block, item_block = frame_piece(block_number)
        scores = cross_scores(memory_block, item_block)
        new_top = jnp.maximum(running_top, jnp.max(scores, axis=-1))
        running_sum = running_sum * jnp.exp(running_top - new_top) + jnp.sum(
            jnp.exp(scores - new_top[:, :, None]), axis=-1
        )
        return (new_top, running_sum)

    start_carry = (
        jnp.full((HEADS, tok_rows), MASKED, jnp.float32),
        jnp.zeros((HEADS, tok_rows), jnp.float32),
    )
    final_top, final_sum = lax.fori_loop(block_first, block_end, running_total, start_carry)
    log_total = final_top + jnp.log(final_sum)

    def cross_weights(memory_block, item_block):
        return jnp.exp(cross_scores(memory_block, item_block) - log_total[:, :, None])

    def weighted_sum(block_number, carried):
        memory_block, item_block = frame_piece(block_number)
        weights = cross_weights(memory_block, item_block).astype(jnp.bfloat16)
        values = split_heads(memory_block[:, model_width:])
        return carried + jnp.einsum(
            "hij,jhd->ihd", weights, values, preferred_element_type=jnp.float32
        )

    cross_sum = lax.fori_loop(
        block_first, block_end, weighted_sum, jnp.zeros((tok_rows, HEADS, HEAD_DIM), jnp.float32)
    )
    cross_att_low = merge_heads(cross_sum).astype(jnp.bfloat16)
    after_two = after_one + project(cross_att_low, w_cross_out) + biases[8]
    normed_three_low = norm_apply(after_two, gain_rows[2], biases[2]).astype(jnp.bfloat16)
    pre_act = project(normed_three_low, w_mlp_in) + hidden_bias
    hidden_low = exact_gelu(pre_act).astype(jnp.bfloat16)
    block_output = (after_two + project(hidden_low, w_mlp_out) + biases[9]).astype(jnp.bfloat16)
    grad_out = cotangent.astype(jnp.float32)
    grad_w_mlp_out = project_left(hidden_low, cotangent)
    grad_bias_mlp_out = jnp.sum(grad_out, axis=0)
    ignored, gelu_back = jax.vjp(exact_gelu, pre_act)
    grad_pre_low = gelu_back(project_right(cotangent, w_mlp_out))[0].astype(jnp.bfloat16)
    grad_w_mlp_in = project_left(normed_three_low, grad_pre_low)
    grad_hidden_bias = jnp.sum(grad_pre_low.astype(jnp.float32), axis=0)
    grad_three, grad_gain_three, grad_shift_three = norm_back(
        after_two, gain_rows[2], biases[2], project_right(grad_pre_low, w_mlp_in)
    )
    grad_after_two = grad_out + grad_three
    grad_cross_branch = grad_after_two.astype(jnp.bfloat16)
    grad_w_cross_out = project_left(cross_att_low, grad_cross_branch)
    grad_bias_cross_out = jnp.sum(grad_cross_branch.astype(jnp.float32), axis=0)
    grad_cross_att_low = project_right(grad_cross_branch, w_cross_out).astype(jnp.bfloat16)
    grad_cross_att = split_heads(grad_cross_att_low)

    def cross_delta(block_number, carried):
        memory_block, item_block = frame_piece(block_number)
        weights = cross_weights(memory_block, item_block)
        values = split_heads(memory_block[:, model_width:])
        grad_weights = jnp.einsum(
            "ihd,jhd->hij", grad_cross_att, values, preferred_element_type=jnp.float32
        )
        return carried + jnp.sum(weights * grad_weights, axis=-1)

    delta_cross = lax.fori_loop(
        block_first, block_end, cross_delta, jnp.zeros((HEADS, tok_rows), jnp.float32)
    )

    def query_back(block_number, carried):
        memory_block, item_block = frame_piece(block_number)
        weights = cross_weights(memory_block, item_block)
        key_heads = split_heads(memory_block[:, :model_width])
        values = split_heads(memory_block[:, model_width:])
        grad_weights = jnp.einsum(
            "ihd,jhd->hij", grad_cross_att, values, preferred_element_type=jnp.float32
        )
        grad_scores = (weights * (grad_weights - delta_cross[:, :, None])).astype(jnp.bfloat16)
        return (
            carried
            + jnp.einsum("hij,jhd->ihd", grad_scores, key_heads, preferred_element_type=jnp.float32)
            * scale_factor
        )

    grad_cross_q = lax.fori_loop(
        block_first, block_end, query_back, jnp.zeros((tok_rows, HEADS, HEAD_DIM), jnp.float32)
    )
    query_group, grad_att_group, top_group, delta_group = (
        lax.all_gather(cross_low, "wide", axis=0, tiled=True),
        lax.all_gather(grad_cross_att_low, "wide", axis=0, tiled=True),
        lax.all_gather(log_total.astype(jnp.bfloat16), "wide", axis=1, tiled=True).astype(
            log_total.dtype
        ),
        lax.all_gather(delta_cross.astype(jnp.bfloat16), "wide", axis=1, tiled=True).astype(
            delta_cross.dtype
        ),
    )
    group_tokens = query_group.shape[0]
    token_block = block_length(group_tokens)
    own_rows = lax.dynamic_slice_in_dim(frame_memory, wide_index * frame_rows, frame_rows, 0)
    own_keys = split_heads(own_rows[:, :model_width])
    own_values = split_heads(own_rows[:, model_width:])
    own_pos = wide_index * frame_rows + jnp.arange(frame_rows, dtype=jnp.int32)
    own_item = owner_item(own_pos, frame_ends)
    slot_low = jnp.sum(jnp.where(item_ids == own_item[0], item_starts, 0))
    slot_high = jnp.sum(jnp.where(item_ids == own_item[frame_rows - 1], item_ends, 0))

    def frame_back(block_number, carried):
        grad_keys, grad_values = carried
        start = (block_number * token_block).astype(jnp.int32)
        query_block = split_heads(lax.dynamic_slice_in_dim(query_group, start, token_block, 0))
        grad_block = split_heads(lax.dynamic_slice_in_dim(grad_att_group, start, token_block, 0))
        top_block = lax.dynamic_slice_in_dim(top_group, start, token_block, 1)
        delta_block = lax.dynamic_slice_in_dim(delta_group, start, token_block, 1)
        slot_item = owner_item(start + jnp.arange(token_block, dtype=jnp.int32), item_ends)
        raw_scores = (
            jnp.einsum("ihd,jhd->hij", query_block, own_keys, preferred_element_type=jnp.float32)
            * scale_factor
        )
        scores = jnp.where((slot_item[:, None] == own_item[None, :])[None], raw_scores, MASKED)
        weights = jnp.exp(scores - top_block[:, :, None])
        grad_weights = jnp.einsum(
            "ihd,jhd->hij", grad_block, own_values, preferred_element_type=jnp.float32
        )
        grad_scores = (weights * (grad_weights - delta_block[:, :, None])).astype(jnp.bfloat16)
        grad_keys = (
            grad_keys
            + jnp.einsum(
                "hij,ihd->jhd", grad_scores, query_block, preferred_element_type=jnp.float32
            )
            * scale_factor
        )
        grad_values = grad_values + jnp.einsum(
            "hij,ihd->jhd",
            weights.astype(jnp.bfloat16),
            grad_block,
            preferred_element_type=jnp.float32,
        )
        return (grad_keys, grad_values)

    empty_frames = jnp.zeros((frame_rows, HEADS, HEAD_DIM), jnp.float32)
    grad_keys_own, grad_values_own = lax.fori_loop(
        slot_low // token_block,
        (slot_high + token_block - 1) // token_block,
        frame_back,
        (empty_frames, empty_frames),
    )
    memory_grad_low = jnp.concatenate(
        [merge_heads(grad_keys_own), merge_heads(grad_values_own)], axis=1
    ).astype(jnp.bfloat16)
    grad_w_memory = project_left(frames, memory_grad_low)
    grad_bias_memory = jnp.sum(memory_grad_low[:, model_width:].astype(jnp.float32), axis=0)
    grad_frames = project_right(memory_grad_low, w_memory)
    grad_cross_q_low = merge_heads(grad_cross_q).astype(jnp.bfloat16)
    grad_w_cross_q = project_left(normed_two_low, grad_cross_q_low)
    grad_bias_cross_q = jnp.sum(grad_cross_q_low.astype(jnp.float32), axis=0)
    grad_two, grad_gain_two, grad_shift_two = norm_back(
        after_one, gain_rows[1], biases[1], project_right(grad_cross_q_low, w_cross_q)
    )
    grad_after_one = grad_after_two + grad_two
    grad_self_branch = grad_after_one.astype(jnp.bfloat16)
    grad_w_output = project_left(attended_low, grad_self_branch)
    grad_bias_output = jnp.sum(grad_self_branch.astype(jnp.float32), axis=0)
    grad_attended = split_heads(project_right(grad_self_branch, w_output).astype(jnp.bfloat16))
    grad_probs = jnp.einsum(
        "ihd,jhd->hij", grad_attended, values_all, preferred_element_type=jnp.float32
    )
    delta_self = jnp.sum(self_probs * grad_probs, axis=-1, keepdims=True)
    grad_self_scores = (self_probs * (grad_probs - delta_self)).astype(jnp.bfloat16)
    grad_keys_all = (
        jnp.einsum("hij,ihd->jhd", grad_self_scores, queries, preferred_element_type=jnp.float32)
        * scale_factor
    )
    grad_values_all = jnp.einsum(
        "hij,ihd->jhd", self_probs_low, grad_attended, preferred_element_type=jnp.float32
    )
    grad_queries = (
        jnp.einsum("hij,jhd->ihd", grad_self_scores, keys_all, preferred_element_type=jnp.float32)
        * scale_factor
    )
    self_terms = jnp.concatenate([merge_heads(grad_keys_all), merge_heads(grad_values_all)], axis=1)
    grad_memory_own = self_terms[SPAN * tok_rows :]
    for offset in range(1, SPAN + 1):
        slice_terms = self_terms[(SPAN - offset) * tok_rows : (SPAN - offset + 1) * tok_rows]
        grad_memory_own = grad_memory_own + shifted(
            slice_terms.astype(jnp.bfloat16), "wide", -offset
        ).astype(slice_terms.dtype)
    grad_projected_low = jnp.concatenate(
        [merge_heads(grad_queries), grad_memory_own], axis=1
    ).astype(jnp.bfloat16)
    grad_w_inputs = project_left(normed_one_low, grad_projected_low)
    grad_bias_query = jnp.sum(grad_projected_low[:, :model_width].astype(jnp.float32), axis=0)
    grad_bias_value = jnp.sum(grad_projected_low[:, 2 * model_width :].astype(jnp.float32), axis=0)
    grad_one, grad_gain_one, grad_shift_one = norm_back(
        inputs, gain_rows[0], biases[0], project_right(grad_projected_low, w_inputs)
    )
    grad_tokens = grad_after_one + grad_one
    grad_gains = jnp.stack([grad_gain_one, grad_gain_two, grad_gain_three])
    grad_biases = jnp.stack(
        [
            grad_shift_one,
            grad_shift_two,
            grad_shift_three,
            grad_bias_query,
            grad_bias_value,
            grad_bias_output,
            grad_bias_cross_q,
            grad_bias_memory,
            grad_bias_cross_out,
            grad_bias_mlp_out,
        ]
    )
    grad_list = (
        grad_w_inputs,
        grad_w_output,
        grad_w_cross_q,
        grad_w_memory,
        grad_w_cross_out,
        grad_w_mlp_in,
        grad_w_mlp_out,
        grad_gains,
        grad_biases,
        grad_hidden_bias,
    )
    shard_dims = (0, 0, 0, 0, 0, 0, 0, 1, 1, 0)
    packed = pack_grads(grad_list, shard_dims, wide_size)
    summed = lax.psum_scatter(packed.reshape(-1), "wide", scatter_dimension=0, tiled=True)
    shard_flat = lax.psum(summed.astype(jnp.bfloat16), "grp").astype(jnp.float32)
    shards = unpack_grads(shard_flat, grad_list, shard_dims, wide_size)
    return (
        block_output,
        grad_tokens,
        grad_frames,
        shards[0],
        shards[1],
        shards[2],
        shards[3],
        shards[4],
        shards[5],
        shards[6],
        shards[7],
        shards[8],
        shards[9],
    )


def solution(mesh):
    placed = (
        P(("grp", "wide"), None),
        P(("grp", "wide"), None),
        P(("grp", "wide"), None),
        P("grp", None),
        P("grp", None),
        P("wide", None),
        P("wide", None),
        P("wide", None),
        P("wide", None),
        P("wide", None),
        P("wide", None),
        P("wide", None),
        P(None, "wide"),
        P(None, "wide"),
        P("wide"),
    )
    return jax.shard_map(
        per_device,
        mesh=mesh,
        in_specs=placed,
        out_specs=(
            P(("grp", "wide"), None),
            P(("grp", "wide"), None),
            P(("grp", "wide"), None),
            P("wide", None),
            P("wide", None),
            P("wide", None),
            P("wide", None),
            P("wide", None),
            P("wide", None),
            P("wide", None),
            P(None, "wide"),
            P(None, "wide"),
            P("wide"),
        ),
        check_vma=False,
    )
```

profile of v0, /device:TPU:0, one launch (start us, length us, event | category | flops | bytes accessed | tf_op | source)
XLA Modules:
  0.0 2318.2 jit_solution(15215709621321142536)
XLA Ops:
  10.0 32.8 %all-gather.1 = bf16[8,96,10]{1,2,0:T(8,128)(2,1)S(1)} all-gather(bf16[1,96,10]{1,2,0:T(8,128)(2,1)} %bitcast.267), channel_id=1, replica_groups=mesh['grp'=4,'wide'=8] {'wide'}, dimensions={0}, use_global_device_ids=true | all-gather | bytes 17280 | tf_op jit(solution)/shard_map/all_gather | solution.py:129
  43.6 21.2 all-gather.18.cloned.1.call-done
  64.8 2.9 fusion.37
  69.8 18.3 all-gather
  94.3 35.9 %all-gather.14.cloned.1.call-done = bf16[768,2304]{1,0:T(8,128)(2,1)} async-done(((bf16[96,2304]{1,0:T(8,128)(2,1)}), bf16[768,2304]{1,0:T(8,128)(2,1)}) %all-gather.14.cloned.1.call-update) | async-done | bytes 3538960 | tf_op jit(solution)/shard_map/all_gather | solution.py:121
  130.2 2.7 fusion.35
  133.0 4.0 collective-permute-start
  143.5 34.6 %all-gather.2 = bf16[8,1,384]{2,1,0:T(2,128)(2,1)S(1)} all-gather(bf16[1,1,384]{2,1,0:T(2,128)(2,1)S(1)} %reshape.588), channel_id=1, replica_groups=mesh['grp'=4,'wide'=8] {'wide'}, dimensions={0}, use_global_device_ids=true | all-gather | bytes 6912 | tf_op jit(solution)/shard_map/all_gather | solution.py:130
  181.0 2.2 collective-permute-start.2
  183.2 3.3 collective-permute-start.3
  186.8 2.6 collective-permute-done.1
  189.4 4.2 collective-permute-done.2
  195.9 3.4 fusion.114
  199.3 3.1 convolution_convert_fusion.2
  204.4 24.1 %all-gather.22.cloned.1.call-done = bf16[768,768]{1,0:T(8,128)(2,1)} async-done(((bf16[96,768]{1,0:T(8,128)(2,1)}), bf16[768,768]{1,0:T(8,128)(2,1)}) %all-gather.22.cloned.1.call-update) | async-done | bytes 1179664 | tf_op jit(solution)/shard_map/all_gather | solution.py:123
  231.0 42.9 %all-gather.20.cloned.1.call-done = bf16[512,1536]{1,0:T(8,128)(2,1)} async-done(((bf16[64,1536]{1,0:T(8,128)(2,1)}), bf16[512,1536]{1,0:T(8,128)(2,1)}) %all-gather.20.cloned.1.call-update) | async-done | bytes 1572880 | tf_op jit(solution)/shard_map/all_gather | solution.py:189
  275.7 2.0 while.54
  279.1 3.6 while.55
  279.4 3.3 fusion.226
  283.7 31.8 %all-gather.24.cloned.1.call-done = bf16[768,768]{1,0:T(8,128)(2,1)} async-done(((bf16[96,768]{1,0:T(8,128)(2,1)}), bf16[768,768]{1,0:T(8,128)(2,1)}) %all-gather.24.cloned.1.call-update) | async-done | bytes 1179664 | tf_op jit(solution)/shard_map/all_gather | solution.py:125
  319.4 27.3 %all_gather.57 = bf16[12,1024]{1,0:T(8,128)(2,1)S(1)} all-gather(bf16[12,128]{1,0:T(8,128)(2,1)S(1)} %copy-done.62), channel_id=1, replica_groups=mesh['grp'=4,'wide'=8] {'wide'}, dimensions={1}, use_global_device_ids=true | all-gather | bytes 27648 | tf_op jit(solution)/shard_map/all_gather | solution.py:303
  348.2 47.9 %all-gather.26.cloned.1.call-done = bf16[768,3072]{1,0:T(8,128)(2,1)} async-done(((bf16[96,3072]{1,0:T(8,128)(2,1)}), bf16[768,3072]{1,0:T(8,128)(2,1)}) %all-gather.26.cloned.1.call-update) | async-done | bytes 4718608 | tf_op jit(solution)/shard_map/all_gather | solution.py:126
  396.1 4.3 convolution_add_fusion.1
  400.4 75.5 %all-gather.28.cloned.1.call-done = bf16[3072,768]{1,0:T(8,128)(2,1)} async-done(((bf16[384,768]{1,0:T(8,128)(2,1)}), bf16[3072,768]{1,0:T(8,128)(2,1)}) %all-gather.28.cloned.1.call-update) | async-done | bytes 4718608 | tf_op jit(solution)/shard_map/all_gather | solution.py:127
  476.0 9.2 convert_reduce_fusion.5
  489.6 5.7 while.56
  489.7 2.3 fusion.232
  492.2 3.1 multiply_reduce_fusion.9
  496.2 8.5 while.57
  497.1 2.3 fusion.239
  499.6 4.6 fusion.240
  506.0 2.0 multiply_reduce_fusion.3
  509.6 3.1 multiply_reduce_fusion.1
  526.8 2.1 fusion.96
  528.9 5.1 fusion.97
  534.3 73.5 %all_gather.59 = bf16[12,1024]{1,0:T(8,128)(2,1)S(1)} all-gather(bf16[12,128]{1,0:T(8,128)(2,1)S(1)} %convert_element_type.208), channel_id=1, replica_groups=mesh['grp'=4,'wide'=8] {'wide'}, dimensions={1}, use_global_device_ids=true | all-gather | bytes 27648 | tf_op jit(solution)/shard_map/all_gather | solution.py:306
  608.4 3.5 reshape.560
  611.9 3.5 reshape.561
  615.4 3.5 reshape.563
  618.9 9.0 reshape.564
  628.0 5.0 fusion.122
  633.0 9.0 reshape.565
  648.6 4.2 fusion.73
  652.7 7.1 reshape.559
  659.9 5.5 constant_dynamic-update-slice_fusion.14
  674.7 2.6 copy.129
  677.3 2.6 copy.131
  681.5 9.7 while.58
  681.5 2.1 fusion.248
  683.8 4.3 fusion.249
  688.1 3.1 fusion.250
  694.0 3.0 convolution_bitcast_fusion
  696.9 6.1 copy.135
  703.1 5.3 reshape.562
  708.9 4.1 constant_dynamic-update-slice_fusion.11
  714.6 9.7 constant_dynamic-update-slice_fusion.9
  724.3 3.9 constant_dynamic-update-slice_fusion.8
  733.0 68.0 %reshape.575 = f32[9450240]{0:T(1024)} reshape(f32[8,1181280]{1,0:T(8,128)} %dynamic-update-slice.9) | data formatting | bytes 75601920 | tf_op jit(solution)/shard_map/reshape | solution.py:439
  801.0 1437.3 %all-reduce.6 = bf16[9450240]{0:T(1024)(128)(2,1)} all-reduce(f32[9450240]{0:T(1024)} %reshape.575), channel_id=2, replica_groups=mesh['grp'=4,'wide'=8] {'wide'}, use_global_device_ids=true, to_apply=%region_56.57.clone | all-reduce | flops 9450240 | bytes 56701440
  2238.3 3.6 dynamic-slice.6
  2243.0 4.2 fusion.50
  2249.7 47.3 %all-reduce.5.cloned.1.call-done = bf16[1181280]{0:T(1024)(128)(2,1)} async-done(((bf16[1181280]{0:T(1024)(128)(2,1)}), bf16[1181280]{0:T(1024)(128)(2,1)}) %all-reduce.5.cloned.1.call-update) | async-done | bytes 2362576 | tf_op jit(solution)/shard_map/psum | solution.py:440
  2304.2 2.4 reshape.581
  2306.6 2.4 reshape.582
  (421 shorter events, 96.6 us)
Async XLA Ops:
  7.2 57.6 %copy-start = (bf16[64,768]{1,0:T(8,128)(2,1)S(1)}, bf16[64,768]{1,0:T(8,128)(2,1)}, u32[]{:S(2)}) copy-start(bf16[64,768]{1,0:T(8,128)(2,1)} %param.26) | copy-start | bytes 294916
  7.2 57.6 %all-gather.18.cloned.1.call-start = ((), (), s32[]{:S(2)}) async-start(), calls=%async_computation.2 | async-start | bytes 2654208 | tf_op jit(solution)/shard_map/all_gather | solution.py:124
  7.9 122.2 %all-gather.14.cloned.1.call-start = ((), (), s32[]{:S(2)}) async-start(), calls=%async_computation | async-start | bytes 3981312 | tf_op jit(solution)/shard_map/all_gather | solution.py:121
  8.7 193.7 %all-gather.16.cloned.1.call-start = ((), (), s32[]{:S(2)}) async-start(), calls=%async_computation.1 | async-start | bytes 1327104 | tf_op jit(solution)/shard_map/all_gather | solution.py:122
  9.4 219.1 %all-gather.22.cloned.1.call-start = ((), (), s32[]{:S(2)}) async-start(), calls=%async_computation.4 | async-start | bytes 1327104 | tf_op jit(solution)/shard_map/all_gather | solution.py:123
  10.0 263.9 %all-gather.20.cloned.1.call-start = ((), (), s32[]{:S(2)}) async-start(), calls=%async_computation.3 | async-start | bytes 1769472 | tf_op jit(solution)/shard_map/all_gather | solution.py:189
  43.5 185.0 %copy-start.52 = (f32[768]{0:T(1024)}, f32[768]{0:T(1024)S(1)}, u32[]{:S(2)}) copy-start(f32[768]{0:T(1024)S(1)} %get-tuple-element.573) | copy-start | bytes 9220
  43.5 26.3 %copy-start.88 = (bf16[3,96]{1,0:T(4,128)(2,1)S(1)}, bf16[3,96]{1,0:T(4,128)(2,1)}, u32[]{:S(2)}) copy-start(bf16[3,96]{1,0:T(4,128)(2,1)} %param.37) | copy-start | bytes 1732
  43.5 44.7 %copy-start.96 = (s32[1,4]{1,0:T(1,128)S(1)}, s32[1,4]{1,0:T(1,128)}, u32[]{:S(2)}) copy-start(s32[1,4]{1,0:T(1,128)} %param.28) | copy-start | bytes 52
  43.6 44.9 %copy-start.95 = (s32[1,4]{1,0:T(1,128)S(1)}, s32[1,4]{1,0:T(1,128)}, u32[]{:S(2)}) copy-start(s32[1,4]{1,0:T(1,128)} %param.29) | copy-start | bytes 52
  43.6 50.3 %copy-start.7 = (bf16[128,768]{1,0:T(8,128)(2,1)S(1)}, bf16[128,768]{1,0:T(8,128)(2,1)}, u32[]{:S(2)}) copy-start(bf16[128,768]{1,0:T(8,128)(2,1)} %param.25) | copy-start | bytes 589828
  67.7 247.8 %all-gather.24.cloned.1.call-start = ((), (), s32[]{:S(2)}) async-start(), calls=%async_computation.5 | async-start | bytes 1327104 | tf_op jit(solution)/shard_map/all_gather | solution.py:125
  68.3 327.8 %all-gather.26.cloned.1.call-start = ((), (), s32[]{:S(2)}) async-start(), calls=%async_computation.6 | async-start | bytes 5308416 | tf_op jit(solution)/shard_map/all_gather | solution.py:126
  69.0 407.0 %all-gather.28.cloned.1.call-start = ((), (), s32[]{:S(2)}) async-start(), calls=%async_computation.7 | async-start | bytes 5308416 | tf_op jit(solution)/shard_map/all_gather | solution.py:127
  69.8 605.0 %all-gather.30.cloned.1.call-start = ((), (), s32[]{:S(2)}) async-start(), calls=%async_computation.8 | async-start | bytes 1769472 | tf_op jit(solution)/shard_map/all_gather | solution.py:301
  88.4 44.5 %copy-start.58 = (s32[4,1]{0,1:T(1,128)}, s32[4,1]{0,1:T(1,128)S(1)}, u32[]{:S(2)}) copy-start(s32[4,1]{0,1:T(1,128)S(1)} %reduce-window.13) | copy-start | bytes 52
  89.4 43.5 %copy-start.54 = (s32[64]{0:T(128)}, s32[64]{0:T(128)S(1)}, u32[]{:S(2)}) copy-start(s32[64]{0:T(128)S(1)} %convert_reduce_fusion.14) | copy-start | bytes 772
  94.0 38.9 %copy-start.60 = (f32[128]{0:T(128)}, f32[128]{0:T(128)S(1)}, u32[]{:S(2)}) copy-start(f32[128]{0:T(128)S(1)} %broadcast_multiply_fusion.2) | copy-start | bytes 1540
  94.2 35.9 %copy-start.90 = (f32[128]{0:T(128)}, f32[128]{0:T(128)S(1)}, u32[]{:S(2)}) copy-start(f32[128]{0:T(128)S(1)} %fusion.71) | copy-start | bytes 1540
  94.2 38.7 %copy-start.68 = (f32[128]{0:T(128)}, f32[128]{0:T(128)S(1)}, u32[]{:S(2)}) copy-start(f32[128]{0:T(128)S(1)} %fusion.83) | copy-start | bytes 1540
  130.2 13.3 copy-start.89
  130.2 48.0 %copy-start.97 = (u32[32]{0:T(128)S(1)}, u32[32]{0:T(128)}, u32[]{:S(2)}) copy-start(u32[32]{0:T(128)} %constant.231) | copy-start | bytes 388
  133.0 53.8 %collective-permute-start = (bf16[128,1536]{1,0:T(8,128)(2,1)S(1)}, bf16[128,1536]{1,0:T(8,128)(2,1)S(1)}, u32[]{:S(2)}, u32[]{:S(2)}) collective-permute-start(bf16[128,1536]{1,0:T(8,128)(2,1)S(1)} %slice.203), channel_id=1, source_target_pairs={{0,4},{1,5},{2,6},{3,7},{8,12},{9,13},{10,14},{11,15},{16,20},{17,... | collective-permute-start | bytes 1179656 | tf_op jit(solution)/shard_map/ppermute | solution.py:20
  179.6 9.8 collective-permute-start.1
  181.0 12.6 collective-permute-start.2
  183.2 10.4 collective-permute-start.3
  186.7 9.1 copy-start.47
  202.4 27.8 %copy-start.49 = (bf16[12,64,128]{2,1,0:T(8,128)(2,1)}, bf16[12,64,128]{2,1,0:T(8,128)(2,1)S(1)}, u32[]{:S(2)}) copy-start(bf16[12,64,128]{2,1,0:T(8,128)(2,1)S(1)} %convolution_convert_fusion.2) | copy-start | bytes 589828
  204.2 26.8 %copy-start.3 = (f32[128,768]{1,0:T(8,128)}, f32[128,768]{1,0:T(8,128)S(1)}, u32[]{:S(2)}) copy-start(f32[128,768]{1,0:T(8,128)S(1)} %get-tuple-element.724) | copy-start | bytes 1179652
  204.2 71.4 %copy-start.66 = (f32[128]{0:T(128)}, f32[128]{0:T(128)S(1)}, u32[]{:S(2)}) copy-start(f32[128]{0:T(128)S(1)} %broadcast_multiply_fusion.1) | copy-start | bytes 1540
  204.4 71.2 %copy-start.92 = (f32[128]{0:T(128)}, f32[128]{0:T(128)S(1)}, u32[]{:S(2)}) copy-start(f32[128]{0:T(128)S(1)} %multiply_reduce_fusion.7) | copy-start | bytes 1540
  204.4 71.2 %copy-start.82 = (f32[128]{0:T(128)}, f32[128]{0:T(128)S(1)}, u32[]{:S(2)}) copy-start(f32[128]{0:T(128)S(1)} %fusion.84) | copy-start | bytes 1540
  230.9 446.4 %all-gather.32.cloned.1.call-start = ((), (), s32[]{:S(2)}) async-start(), calls=%async_computation.9 | async-start | bytes 1769472 | tf_op jit(solution)/shard_map/all_gather | solution.py:302
  283.7 63.8 %copy-start.34 = (bf16[128,12,64]{0,2,1:T(8,128)(2,1)}, bf16[128,12,64]{0,2,1:T(8,128)(2,1)S(1)}, u32[]{:S(2)}) copy-start(bf16[128,12,64]{0,2,1:T(8,128)(2,1)S(1)} %convert_element_type.186) | copy-start | bytes 589828
  283.7 35.7 %copy-start.62 = (bf16[12,128]{1,0:T(8,128)(2,1)S(1)}, bf16[12,128]{1,0:T(8,128)(2,1)}, u32[]{:S(2)}) copy-start(bf16[12,128]{1,0:T(8,128)(2,1)} %get-tuple-element.689) | copy-start | bytes 9220
  317.3 211.6 %copy-start.1 = (f32[128,768]{1,0:T(8,128)}, f32[128,768]{1,0:T(8,128)S(1)}, u32[]{:S(2)}) copy-start(f32[128,768]{1,0:T(8,128)S(1)} %get-tuple-element.726) | copy-start | bytes 1179652
  317.3 169.8 %copy-start.56 = (f32[128]{0:T(128)}, f32[128]{0:T(128)S(1)}, u32[]{:S(2)}) copy-start(f32[128]{0:T(128)S(1)} %broadcast_multiply_fusion) | copy-start | bytes 1540
  317.5 169.6 %copy-start.64 = (f32[128]{0:T(128)}, f32[128]{0:T(128)S(1)}, u32[]{:S(2)}) copy-start(f32[128]{0:T(128)S(1)} %fusion.85) | copy-start | bytes 1540
  396.1 79.9 %copy-start.31 = (bf16[128,768]{1,0:T(8,128)(2,1)S(1)}, bf16[128,768]{1,0:T(8,128)(2,1)}, u32[]{:S(2)}) copy-start(bf16[128,768]{1,0:T(8,128)(2,1)} %param.27) | copy-start | bytes 589828
  476.0 9.2 copy-start.5
  496.2 9.8 copy-start.4
  508.5 16.3 copy-start.17
  516.4 6.6 copy-start.35
  516.4 6.6 copy-start.37
  517.6 7.2 copy-start.50
  517.6 129.0 %collective-permute-start.7 = (bf16[128,1536]{0,1:T(8,128)(2,1)}, bf16[128,1536]{0,1:T(8,128)(2,1)}, u32[]{:S(2)}, u32[]{:S(2)}) collective-permute-start(bf16[128,1536]{0,1:T(8,128)(2,1)} %get-tuple-element.709), channel_id=1, source_target_pairs={{4,0},{5,1},{6,2},{7,3},{12,8},{13,9},{14,10},{15,11},{20,16},{21,... | collective-permute-start | bytes 1179656 | tf_op jit(solution)/shard_map/ppermute | solution.py:20
  519.1 127.6 %collective-permute-start.6 = (bf16[128,1536]{0,1:T(8,128)(2,1)}, bf16[128,1536]{0,1:T(8,128)(2,1)}, u32[]{:S(2)}, u32[]{:S(2)}) collective-permute-start(bf16[128,1536]{0,1:T(8,128)(2,1)} %get-tuple-element.710), channel_id=1, source_target_pairs={{3,0},{4,1},{5,2},{6,3},{7,4},{11,8},{12,9},{13,10},{14,11},{15,12... | collective-permute-start | bytes 1179656 | tf_op jit(solution)/shard_map/ppermute | solution.py:20
  520.4 126.3 %collective-permute-start.5 = (bf16[128,1536]{0,1:T(8,128)(2,1)}, bf16[128,1536]{0,1:T(8,128)(2,1)}, u32[]{:S(2)}, u32[]{:S(2)}) collective-permute-start(bf16[128,1536]{0,1:T(8,128)(2,1)} %get-tuple-element.711), channel_id=1, source_target_pairs={{2,0},{3,1},{4,2},{5,3},{6,4},{7,5},{10,8},{11,9},{12,10},{13,11},... | collective-permute-start | bytes 1179656 | tf_op jit(solution)/shard_map/ppermute | solution.py:20
  521.7 125.0 %collective-permute-start.4 = (bf16[128,1536]{0,1:T(8,128)(2,1)}, bf16[128,1536]{0,1:T(8,128)(2,1)}, u32[]{:S(2)}, u32[]{:S(2)}) collective-permute-start(bf16[128,1536]{0,1:T(8,128)(2,1)} %get-tuple-element.708), channel_id=1, source_target_pairs={{1,0},{2,1},{3,2},{4,3},{5,4},{6,5},{7,6},{9,8},{10,9},{11,10},{12... | collective-permute-start | bytes 1179656 | tf_op jit(solution)/shard_map/ppermute | solution.py:20
  534.2 93.7 %copy-start.14 = (bf16[128,3072]{1,0:T(8,128)(2,1)}, bf16[128,3072]{1,0:T(8,128)(2,1)S(1)}, u32[]{:S(2)}) copy-start(bf16[128,3072]{1,0:T(8,128)(2,1)S(1)} %multiply_convert_fusion.3) | copy-start | bytes 2359300
  534.3 1762.8 %all-reduce.5.cloned.1.call-start = ((), (), s32[]{:S(2)}) async-start(), calls=%async_computation.10 | async-start | bytes 4726784 | tf_op jit(solution)/shard_map/psum | solution.py:440
  618.9 9.0 copy-start.33
  633.0 9.6 copy-start.23
  659.9 5.5 copy-start.13
  703.0 5.4 copy-start.71
  703.0 5.4 copy-start.72
  703.0 5.4 copy-start.73
  703.0 5.4 copy-start.74
  703.0 5.4 copy-start.75
  703.0 5.4 copy-start.76
  703.0 5.4 copy-start.77
  713.0 11.3 slice-start
  714.6 9.7 slice-start.1
  714.6 9.7 slice-start.2
  (56 other events, 150.5 us)
Sparse Core Ops, SparseCore 0:
  10.2 54.5 all-gather.17
  66.9 63.1 all-gather.13
  132.4 47.9 all-gather.15
  182.3 46.1 all-gather.21
  231.1 42.7 all-gather.19
  275.9 39.4 all-gather.23
  317.6 78.3 all-gather.25
  398.3 77.6 all-gather.27
  478.7 42.5 all-gather.29
  534.4 57.6 all-gather.31
  2242.1 54.8 all-reduce.4
where the time goes:
time: 2330 us; the launch traced here: 2320 us
  blocking collectives  1620 us (70%)
  waiting for transfers between devices  338 us (15%)
  local copies, waits for them, and re-layouts  200 us (9%)
  matrix products  96.8 us (4%)
    unnamed x1, blocking collectives  1440 us
    all_gather x1, waiting for transfers between devices, per_device(): lax.all_gather(mlp_output, 'wide', axis=0, tiled=True)  75.5 us
    all_gather x1, blocking collectives, per_device(): lax.all_gather(delta_cross.astype(jnp.bfloat16), 'wide', axis=1, tiled=True)  73.5 us
    reshape x1, local copies, waits for them, and re-layouts, per_device(): packed.reshape(-1)  68 us
    all_gather x1, waiting for transfers between devices, per_device(): lax.all_gather(mlp_inputs, 'wide', axis=0, tiled=True)  47.9 us
    psum x1, waiting for transfers between devices, per_device(): lax.psum(summed.astype(jnp.bfloat16), 'grp').astype(jnp.float32)  47.3 us
  transfers between devices with their start and end apart: 19, of which 10 were waited for; matrix products, arithmetic and copies ran while one was open for 7% of the time, Pallas kernels for 0%

commit v1 on v0

v1 whole, which is shorter than its diff:
```python
import functools

import jax
import jax.numpy as jnp
from jax import lax
from jax.experimental import pallas as pl
from jax.experimental.pallas import tpu as pltpu
from jax.sharding import PartitionSpec as P

HEADS = 12
HEAD_DIM = 64
LONGEST = 512
EPSILON = 1e-05
MASKED = -1e30
SCALE = HEAD_DIM ** (-0.5)
F32 = jnp.float32
BF16 = jnp.bfloat16
BOTH = ("grp", "wide")
NZ, NY = 4, 2


def dot(left, right):
    return jnp.dot(left, right, preferred_element_type=F32)


def dot_tn(left, right):
    return lax.dot_general(left, right, (((0,), (0,)), ((), ())), preferred_element_type=F32)


def dot_nt(left, right):
    return lax.dot_general(left, right, (((1,), (1,)), ((), ())), preferred_element_type=F32)


def norm_parts(values):
    centre = jnp.mean(values, axis=-1, keepdims=True)
    centred = values - centre
    spread = jnp.mean(centred * centred, axis=-1, keepdims=True)
    inverse = lax.rsqrt(spread + EPSILON)
    return centred * inverse, inverse


def norm_apply(values, gain, shift):
    return norm_parts(values)[0] * gain + shift


def norm_back(values, gain, upstream):
    normal, inverse = norm_parts(values)
    scaled = upstream * gain
    mean_one = jnp.mean(scaled, axis=-1, keepdims=True)
    mean_two = jnp.mean(scaled * normal, axis=-1, keepdims=True)
    grad = inverse * (scaled - mean_one - normal * mean_two)
    return grad, jnp.sum(upstream * normal, axis=0), jnp.sum(upstream, axis=0)


def move(value, wide, dx=0, dc=0, dz=0, dy=0):
    pairs = []
    for x in range(2):
        for c in range(2):
            for z in range(NZ):
                for y in range(NY):
                    source = (x * 2 + c) * wide + z * NY + y
                    target = ((x ^ dx) * 2 + (c ^ dc)) * wide + ((z + dz) % NZ) * NY + (y ^ dy)
                    pairs.append((source, target))
    return lax.ppermute(value, BOTH, pairs)


def shifted(value, wide, by):
    pairs = [(i, i + by) for i in range(wide) if 0 <= i + by < wide]
    return lax.ppermute(value, "wide", pairs)


def pick(value, index, axis):
    return lax.dynamic_index_in_dim(value, index, axis, keepdims=False)


def attention_bias(mode, tok_rows, info_ref, lengths_ref, counts_ref, pos_ref):
    items = lengths_ref.shape[1]
    slot = info_ref[0] * tok_rows + lax.broadcasted_iota(jnp.int32, (tok_rows, 1), 0)
    key = pos_ref[...]
    if mode == "self":
        first = jnp.zeros((tok_rows, 1), jnp.int32)
        start = jnp.int32(0)
        for item in range(items):
            first = jnp.where(slot >= start, start, first)
            start = start + lengths_ref[0, item]
        allowed = (key >= first) & (key <= slot)
    else:
        owner = jnp.zeros((tok_rows, 1), jnp.int32)
        frame_owner = jnp.zeros(key.shape, jnp.int32)
        end = jnp.int32(0)
        frame_end = jnp.int32(0)
        for item in range(items):
            end = end + lengths_ref[0, item]
            frame_end = frame_end + counts_ref[0, item]
            owner = owner + (slot >= end).astype(jnp.int32)
            frame_owner = frame_owner + (key >= frame_end).astype(jnp.int32)
        allowed = owner == frame_owner
    return jnp.where(allowed, 0.0, MASKED).astype(F32)


def softmax_rows(query, keys, bias):
    scores = dot_nt(query, keys) * SCALE + bias
    top = jnp.max(scores, axis=-1, keepdims=True)
    raised = jnp.exp(scores - top)
    return raised / jnp.sum(raised, axis=-1, keepdims=True)


def attention_forward_body(mode, info_ref, lengths_ref, counts_ref, pos_ref, q_ref, kv_ref, out_ref):
    rows, width = q_ref.shape
    bias = attention_bias(mode, rows, info_ref, lengths_ref, counts_ref, pos_ref)
    lane = lax.broadcasted_iota(jnp.int32, (1, 128), 1)

    def pair(number, carry):
        at = pl.ds(pl.multiple_of(number * 128, 128), 128)
        value_at = pl.ds(pl.multiple_of(number * 128 + width, 128), 128)
        query, keys, values = q_ref[:, at], kv_ref[:, at], kv_ref[:, value_at]
        results = []
        for half in range(2):
            keep = (lane // HEAD_DIM == half).astype(BF16)
            probs = softmax_rows(query * keep, keys, bias)
            results.append(dot(probs.astype(BF16), values))
        out_ref[:, at] = jnp.where(lane < HEAD_DIM, results[0], results[1]).astype(BF16)
        return carry

    lax.fori_loop(0, width // 128, pair, 0)


def attention_backward_body(
    mode, info_ref, lengths_ref, counts_ref, pos_ref, q_ref, kv_ref, g_ref, dq_ref, dkv_ref
):
    rows, width = q_ref.shape
    bias = attention_bias(mode, rows, info_ref, lengths_ref, counts_ref, pos_ref)
    lane = lax.broadcasted_iota(jnp.int32, (1, 128), 1)

    def pair(number, carry):
        at = pl.ds(pl.multiple_of(number * 128, 128), 128)
        value_at = pl.ds(pl.multiple_of(number * 128 + width, 128), 128)
        query, keys, values, grads = q_ref[:, at], kv_ref[:, at], kv_ref[:, value_at], g_ref[:, at]
        d_query, d_keys, d_values = [], [], []
        for half in range(2):
            keep = (lane // HEAD_DIM == half).astype(BF16)
            probs = softmax_rows(query * keep, keys, bias)
            d_probs = dot_nt(grads * keep, values)
            delta = jnp.sum(probs * d_probs, axis=-1, keepdims=True)
            d_scores = (probs * (d_probs - delta)).astype(BF16)
            d_query.append(dot(d_scores, keys) * SCALE)
            d_keys.append(dot_tn(d_scores, query) * SCALE)
            d_values.append(dot_tn(probs.astype(BF16), grads))
        first = lane < HEAD_DIM
        dq_ref[:, at] = jnp.where(first, d_query[0], d_query[1]).astype(BF16)
        dkv_ref[:, at] = jnp.where(first, d_keys[0], d_keys[1]).astype(BF16)
        dkv_ref[:, value_at] = jnp.where(first, d_values[0], d_values[1]).astype(BF16)
        return carry

    lax.fori_loop(0, width // 128, pair, 0)


def smem():
    return pl.BlockSpec(memory_space=pltpu.SMEM)


def vmem():
    return pl.BlockSpec(memory_space=pltpu.VMEM)


def attention_forward(mode, info, lengths, counts, positions, query, kv):
    rows, width = query.shape
    count = kv.shape[0]
    return pl.pallas_call(
        functools.partial(attention_forward_body, mode),
        out_shape=jax.ShapeDtypeStruct((rows, width), BF16),
        in_specs=[smem(), smem(), smem(), vmem(), vmem(), vmem()],
        out_specs=vmem(),
        name=mode + "_forward",
        cost_estimate=pl.CostEstimate(
            flops=8 * rows * count * width, bytes_accessed=8 * count * width, transcendentals=rows * count * HEADS
        ),
    )(info, lengths, counts, positions, query, kv)


def attention_backward(mode, info, lengths, counts, positions, query, kv, grads):
    rows, width = query.shape
    count = kv.shape[0]
    return pl.pallas_call(
        functools.partial(attention_backward_body, mode),
        out_shape=(jax.ShapeDtypeStruct((rows, width), BF16), jax.ShapeDtypeStruct(kv.shape, BF16)),
        in_specs=[smem(), smem(), smem(), vmem(), vmem(), vmem(), vmem()],
        out_specs=(vmem(), vmem()),
        name=mode + "_backward",
        cost_estimate=pl.CostEstimate(
            flops=20 * rows * count * width, bytes_accessed=16 * count * width, transcendentals=rows * count * HEADS
        ),
    )(info, lengths, counts, positions, query, kv, grads)


def half_columns(shard, core):
    half = shard.shape[1] // 2
    part = lax.dynamic_slice_in_dim(shard, core * half, half, 1)
    blocks = part.reshape(-1, 96, half)
    return [blocks[i] for i in range(blocks.shape[0])]


def assemble_body(rows, plan, coords_ref, *refs):
    count = len(refs) - len(plan)
    arrays, outs = refs[:count], refs[count:]
    x, c, z, y = coords_ref[0], coords_ref[1], coords_ref[2], coords_ref[3]
    per_core = count // 2
    for number, array in enumerate(arrays):
        core = c ^ (number // per_core)
        local = number % per_core
        row_y = y ^ (local % 2)
        row_x = x ^ (local // 2)

        def step(dz, carry, array=array, core=core, row_y=row_y, row_x=row_x):
            wide = ((z + dz) & (NZ - 1)) * NY + row_y
            cursor = 0
            for out, (blocks, width) in zip(outs, plan):
                half = width // 2
                for block in range(blocks):
                    row = wide * (96 * blocks) + block * 96
                    if rows < 96:
                        row = row + row_x * rows
                    row = pl.multiple_of(row, 16)
                    column = pl.multiple_of(core * half, 128)
                    out[pl.ds(row, rows), pl.ds(column, half)] = array[dz, :, cursor : cursor + half]
                    cursor += half
            return carry

        lax.fori_loop(0, NZ, step, 0)


def gather_weights(shards, coords, wide, use_x):
    x, c, z, y = coords
    own = jnp.concatenate([b for s in shards for b in half_columns(s, c)], axis=1)
    rows = 96
    if use_x:
        rows = 48
        own = lax.dynamic_slice_in_dim(own, x * rows, rows, 0)
    column = jnp.stack([own] + [move(own, wide, dz=-d) for d in range(1, NZ)])
    plane = [column, move(column, wide, dy=1)]
    if use_x:
        plane = plane + [move(v, wide, dx=1) for v in plane]
    arrays = plane + [move(v, wide, dc=1) for v in plane]
    plan = [(s.shape[0] // 96, s.shape[1]) for s in shards]
    return pl.pallas_call(
        functools.partial(assemble_body, rows, plan),
        out_shape=tuple(jax.ShapeDtypeStruct((s.shape[0] * wide, s.shape[1]), BF16) for s in shards),
        in_specs=[smem()] + [vmem()] * len(arrays),
        out_specs=tuple(vmem() for s in shards),
        name="assemble",
        cost_estimate=pl.CostEstimate(
            flops=0, bytes_accessed=sum(4 * s.size * wide for s in shards), transcendentals=0
        ),
    )(jnp.stack(coords).astype(jnp.int32), *arrays)


def scatter_grads(pieces, coords, wide, use_x):
    x, c, z, y = coords

    def joined(parts):
        return parts[0] if len(parts) == 1 else jnp.concatenate(parts, axis=-1)

    if use_x:
        views = [p.reshape(NZ, NY, 2, 48, p.shape[-1]) for p in pieces]
        arrived = move(joined([pick(v, 1 - x, 2) for v in views]), wide, dx=1)
        kept = joined([pick(v, x, 2) for v in views])
        block = (kept.astype(F32) + arrived.astype(F32)).astype(BF16)
        arrived = move(pick(block, 1 - y, 1), wide, dy=1)
        kept = pick(block, y, 1)
    else:
        views = [p.reshape(NZ, NY, 96, p.shape[-1]) for p in pieces]
        arrived = move(joined([pick(v, 1 - y, 1) for v in views]), wide, dy=1)
        kept = joined([pick(v, y, 1) for v in views])
    column = (kept.astype(F32) + arrived.astype(F32)).astype(BF16)
    arrived = [move(pick(column, (z + d) % NZ, 0), wide, dz=d) for d in range(1, NZ)]
    total = pick(column, z, 0).astype(F32)
    for value in arrived:
        total = total + value.astype(F32)
    total = total.astype(BF16)
    other = move(total, wide, dx=1)
    if use_x:
        return jnp.where(x == 0, jnp.concatenate([total, other]), jnp.concatenate([other, total]))
    return (total.astype(F32) + other.astype(F32)).astype(BF16)


def finish_grads(mine, shapes, coords, wide):
    c = coords[1]
    theirs = move(mine, wide, dc=1)
    low = jnp.where(c == 0, mine, theirs)
    high = jnp.where(c == 0, theirs, mine)
    shards, cursor = [], 0
    for rows, width in shapes:
        half = width // 2
        blocks = []
        for block in range(rows // 96):
            at = slice(cursor, cursor + half)
            blocks.append(jnp.concatenate([low[:, at], high[:, at]], axis=1))
            cursor += half
        whole = blocks[0] if len(blocks) == 1 else jnp.concatenate(blocks, axis=0)
        shards.append(whole.astype(F32))
    return shards


def per_device(
    tokens,
    frames,
    cotangent,
    item_lengths,
    frame_lengths,
    attn_inputs,
    attn_output,
    cross_queries,
    cross_memory,
    cross_output,
    mlp_inputs,
    mlp_output,
    norm_gains,
    bias_rows,
    mlp_bias,
):
    width = tokens.shape[1]
    tok_rows = tokens.shape[0]
    frame_rows = frames.shape[0]
    hidden_rows = mlp_output.shape[0]
    wide = lax.axis_size("wide")
    me = lax.axis_index("wide").astype(jnp.int32)
    group = lax.axis_index("grp").astype(jnp.int32)
    span = LONGEST // tok_rows
    fast = wide == NZ * NY
    x, c, z, y = group // 2, group % 2, me // NY, me % NY
    coords = (x, c, z, y)
    part = width // wide

    small = jnp.concatenate([norm_gains.reshape(-1), bias_rows.reshape(-1), mlp_bias])
    window = jnp.concatenate([shifted(tokens, wide, o) for o in range(span, 0, -1)] + [tokens])
    if fast:
        small_rows = -(-small.shape[0] // (16 * width)) * 16
        small = jnp.pad(small, (0, small_rows * width - small.shape[0])).reshape(small_rows, width)
        own = jnp.concatenate([frames, small])
        column = jnp.stack([own] + [move(own, wide, dz=-d) for d in range(1, NZ)])
        plane = jnp.stack([column, move(column, wide, dy=1)])
        all_frames = plane[:, :, :frame_rows].reshape(-1, width)
        number = jnp.arange(wide, dtype=jnp.int32)
        owner = ((z + number % NZ) % NZ) * NY + (y ^ (number // NZ))
        params = plane[:, :, frame_rows:].reshape(NY, NZ, small_rows * width)
        params = jnp.where(y == 0, params, params[::-1])
        params = jnp.roll(params, z, axis=1)
        params = params.transpose(1, 0, 2).reshape(wide, -1)
        w_in, w_out, w_cross_q = gather_weights((attn_inputs, attn_output, cross_queries), coords, wide, False)
        w_memory, w_cross_out = gather_weights((cross_memory, cross_output), coords, wide, True)
        w_mlp_in, w_mlp_out = gather_weights((mlp_inputs, mlp_output), coords, wide, True)
    else:
        gather = functools.partial(lax.all_gather, axis_name="wide", axis=0, tiled=True)
        all_frames = gather(frames)
        owner = jnp.arange(wide, dtype=jnp.int32)
        params = gather(small.reshape(1, -1))
        w_in, w_out, w_cross_q = gather(attn_inputs), gather(attn_output), gather(cross_queries)
        w_memory, w_cross_out = gather(cross_memory), gather(cross_output)
        w_mlp_in, w_mlp_out = gather(mlp_inputs), gather(mlp_output)
    gains = params[:, : 3 * part].reshape(wide, 3, part).transpose(1, 0, 2).reshape(3, width).astype(F32)
    biases = params[:, 3 * part : 13 * part].reshape(wide, 10, part).transpose(1, 0, 2)
    biases = biases.reshape(10, width).astype(F32)
    hidden_bias = params[:, 13 * part : 13 * part + hidden_rows].reshape(-1).astype(F32)
    frame_pos = (owner[:, None] * frame_rows + jnp.arange(frame_rows, dtype=jnp.int32)).reshape(1, -1)
    key_pos = ((me - span) * tok_rows + jnp.arange((span + 1) * tok_rows, dtype=jnp.int32)).reshape(1, -1)
    info = me.reshape(1)
    zero_row = jnp.zeros((width,), F32)

    inputs = tokens.astype(F32)
    normed_window = norm_apply(window.astype(F32), gains[0], biases[0]).astype(BF16)
    normed_one = normed_window[span * tok_rows :]
    query = (dot(normed_one, w_in[:, :width]) + biases[3]).astype(BF16)
    self_kv = (dot(normed_window, w_in[:, width:]) + jnp.concatenate([zero_row, biases[4]])).astype(BF16)
    tables = (info, item_lengths, frame_lengths)
    attended = attention_forward("self", *tables, key_pos, query, self_kv)
    after_one = inputs + dot(attended, w_out) + biases[5]
    normed_two = norm_apply(after_one, gains[1], biases[1]).astype(BF16)
    cross_q = (dot(normed_two, w_cross_q) + biases[6]).astype(BF16)
    memory = (dot(all_frames, w_memory) + jnp.concatenate([zero_row, biases[7]])).astype(BF16)
    cross_att = attention_forward("cross", *tables, frame_pos, cross_q, memory)
    after_two = after_one + dot(cross_att, w_cross_out) + biases[8]
    normed_three = norm_apply(after_two, gains[2], biases[2]).astype(BF16)
    pre_act = dot(normed_three, w_mlp_in) + hidden_bias
    exact_gelu = functools.partial(jax.nn.gelu, approximate=False)
    hidden = exact_gelu(pre_act).astype(BF16)
    block_output = (after_two + dot(hidden, w_mlp_out) + biases[9]).astype(BF16)

    grad_out = cotangent.astype(F32)
    grad_hidden = dot_nt(cotangent, w_mlp_out)
    grad_pre = jax.vjp(exact_gelu, pre_act)[1](grad_hidden)[0].astype(BF16)
    grad_three, gain_three, shift_three = norm_back(after_two, gains[2], dot_nt(grad_pre, w_mlp_in))
    grad_after_two = grad_out + grad_three
    grad_cross_branch = grad_after_two.astype(BF16)
    grad_cross_att = dot_nt(grad_cross_branch, w_cross_out).astype(BF16)
    grad_cross_q, grad_memory = attention_backward(
        "cross", *tables, frame_pos, cross_q, memory, grad_cross_att
    )
    grad_two, gain_two, shift_two = norm_back(after_one, gains[1], dot_nt(grad_cross_q, w_cross_q))
    grad_after_one = grad_after_two + grad_two
    grad_self_branch = grad_after_one.astype(BF16)
    grad_attended = dot_nt(grad_self_branch, w_out).astype(BF16)
    grad_query, grad_kv = attention_backward("self", *tables, key_pos, query, self_kv, grad_attended)

    frame_part = dot_nt(grad_memory, w_memory)
    if fast:
        frame_part = frame_part.astype(BF16).reshape(NY, NZ, frame_rows, width)
        arrived = move(frame_part[1], wide, dy=1)
        line = (frame_part[0].astype(F32) + arrived.astype(F32)).astype(BF16)
        grad_frames = line[0].astype(F32)
        for d in range(1, NZ):
            grad_frames = grad_frames + move(line[d], wide, dz=d).astype(F32)
    else:
        grad_frames = lax.psum_scatter(frame_part, "wide", scatter_dimension=0, tiled=True)

    window_part = dot_nt(grad_kv, w_in[:, width:])
    grad_one = window_part[span * tok_rows :] + dot_nt(grad_query, w_in[:, :width])
    for o in range(1, span + 1):
        block = window_part[(span - o) * tok_rows : (span - o + 1) * tok_rows]
        grad_one = grad_one + shifted(block.astype(BF16), wide, -o).astype(F32)
    grad_first, gain_one, shift_one = norm_back(inputs, gains[0], grad_one)
    grad_tokens = grad_after_one + grad_first

    def total(value):
        return jnp.sum(value.astype(F32), axis=0)

    rows = [
        gain_one,
        gain_two,
        gain_three,
        shift_one,
        shift_two,
        shift_three,
        total(grad_query),
        total(grad_kv[:, width:]),
        total(grad_self_branch),
        total(grad_cross_q),
        total(grad_memory[:, width:]),
        total(grad_cross_branch),
        total(grad_out),
    ]
    pre_total = total(grad_pre)

    if fast:

        def both(value):
            return jnp.concatenate([value, move(value, wide, dc=1)])

        def split(value):
            half = value.shape[1] // 2
            mine = lax.dynamic_slice_in_dim(value, c * half, half, 1)
            theirs = lax.dynamic_slice_in_dim(value, (1 - c) * half, half, 1)
            return jnp.concatenate([mine, move(theirs, wide, dc=1)])

        def weight(left, right):
            grad = dot_tn(left, right).astype(BF16)
            return grad.reshape(wide, -1, 96, grad.shape[1])

        def blocks(grad):
            return [grad[:, i] for i in range(grad.shape[1])]

        half_hidden = weight(both(hidden), split(cotangent))
        half_pre = weight(both(normed_three), split(grad_pre))
        reduced = scatter_grads(blocks(half_pre) + blocks(half_hidden), coords, wide, True)
        g_mlp_in, g_mlp_out = finish_grads(reduced, [mlp_inputs.shape, mlp_output.shape], coords, wide)

        g_cross_out = weight(both(cross_att), split(grad_cross_branch))
        frames_two = both(all_frames)
        g_memory_k = weight(frames_two, split(grad_memory[:, :width]))
        g_memory_v = weight(frames_two, split(grad_memory[:, width:]))
        g_cross_q = weight(both(normed_two), split(grad_cross_q))
        pieces = [p for g in (g_memory_k, g_memory_v, g_cross_out, g_cross_q) for p in blocks(g)]
        reduced = scatter_grads(pieces, coords, wide, False)
        square = (part, width)
        g_memory_k, g_memory_v, g_cross_out, g_cross_q = finish_grads(reduced, [square] * 4, coords, wide)
        g_memory = jnp.concatenate([g_memory_k, g_memory_v], axis=1)

        g_out = weight(both(attended), split(grad_self_branch))
        window_two = both(normed_window)
        g_in_q = weight(both(normed_one), split(grad_query))
        g_in_k = weight(window_two, split(grad_kv[:, :width]))
        g_in_v = weight(window_two, split(grad_kv[:, width:]))
        pieces = [p for g in (g_out, g_in_q, g_in_k, g_in_v) for p in blocks(g)]
        reduced = scatter_grads(pieces, coords, wide, True)
        g_out, g_in_q, g_in_k, g_in_v = finish_grads(reduced, [square] * 4, coords, wide)
        g_in = jnp.concatenate([g_in_q, g_in_k, g_in_v], axis=1)

        small = jnp.concatenate([jnp.stack(rows), pre_total.reshape(-1, width)])
        small = small + move(small, wide, dc=1)
        small = small + move(small, wide, dx=1)
        small = small + move(small, wide, dy=1)
        arrived = [move(small, wide, dz=d) for d in range(1, NZ)]
        small = small + arrived[0] + arrived[1] + arrived[2]
        rows_all = lax.dynamic_slice_in_dim(small[:13], me * part, part, 1)
        g_bias = lax.dynamic_slice_in_dim(small[13:].reshape(-1), me * hidden_rows, hidden_rows, 0)
    else:

        def weight(left, right):
            grad = lax.psum_scatter(dot_tn(left, right), "wide", scatter_dimension=0, tiled=True)
            return lax.psum(grad.astype(BF16), "grp").astype(F32)

        g_in = jnp.concatenate([weight(normed_one, grad_query), weight(normed_window, grad_kv)], axis=1)
        g_out = weight(attended, grad_self_branch)
        g_cross_q = weight(normed_two, grad_cross_q)
        g_memory = weight(all_frames, grad_memory)
        g_cross_out = weight(cross_att, grad_cross_branch)
        g_mlp_in = weight(normed_three, grad_pre)
        g_mlp_out = weight(hidden, cotangent)
        small = lax.psum(jnp.stack(rows), BOTH)
        rows_all = lax.dynamic_slice_in_dim(small, me * part, part, 1)
        g_bias = lax.dynamic_slice_in_dim(lax.psum(pre_total, BOTH), me * hidden_rows, hidden_rows, 0)
    return (
        block_output,
        grad_tokens,
        grad_frames,
        g_in,
        g_out,
        g_cross_q,
        g_memory,
        g_cross_out,
        g_mlp_in,
        g_mlp_out,
        rows_all[:3],
        rows_all[3:],
        g_bias,
    )


def solution(mesh):
    rows = P(BOTH, None)
    weight = P("wide", None)
    columns = P(None, "wide")
    return jax.shard_map(
        per_device,
        mesh=mesh,
        in_specs=(rows,) * 3 + (P("grp", None),) * 2 + (weight,) * 7 + (columns, columns, P("wide")),
        out_specs=(rows,) * 3 + (weight,) * 7 + (columns, columns, P("wide")),
        check_vma=False,
    )
```

time: 2330 us -> 587 us (0.25)
  blocking collectives: 1620 us -> 0 us
  waiting for transfers between devices: 338 us -> 199 us
  starting transfers between devices: 16.5 us -> 136 us
  local copies, waits for them, and re-layouts: 200 us -> 88.6 us
  Pallas kernels: 0 us -> 56.9 us
  matrix products: 96.8 us -> 64.3 us
    unnamed x1 -> x0, blocking collectives: 1440 us -> none
    all_gather x10 -> x0, waiting for transfers between devices: 279 us -> none  [the longest x1 75.5 us: per_device(): lax.all_gather(mlp_output, 'wide', axis=0, tiled=True)]
    ppermute x8 -> x86, waiting for transfers between devices: 6.79 us -> 199 us  [the longest x78 177 us: move(): return lax.ppermute(value, BOTH, pairs)]
    all_gather x5 -> x0, blocking collectives: 186 us -> none  [the longest x1 73.5 us: per_device(): lax.all_gather(delta_cross.astype(jnp.bfloat16), 'wide', axis=1, tiled=True)]
    ppermute x8 -> x86, starting transfers between devices: 16.1 us -> 136 us  [the longest x78 111 us: move(): return lax.ppermute(value, BOTH, pairs)]
    reshape x29 -> x8, local copies, waits for them, and re-layouts: 120 us -> 2.02 us  [the longest x1 0.77 us: per_device(): bias_rows.reshape(-1)]
    pallas_call x0 -> x7, Pallas kernels: none -> 56.9 us  [the longest x2 22.4 us: attention_backward(): pl.pallas_call(functools.partial(attention_backward_body, mode), out_shap...]
    psum x1 -> x0, waiting for transfers between devices: 47.3 us -> none  [per_device(): lax.psum(summed.astype(jnp.bfloat16), 'grp').astype(jnp.float32)]
  transfers between devices with their start and end apart: 19 -> 86, of which waited for: 10 -> 21; matrix products, arithmetic and copies ran while one was open for 7% -> 30% of each run, Pallas kernels for 0% -> 10%
where the time goes in v1:
time: 587 us; the launch traced here: 578 us
  waiting for transfers between devices  199 us (34%)
  starting transfers between devices  136 us (23%)
  local copies, waits for them, and re-layouts  88.6 us (15%)
  matrix products  64.3 us (11%)
  Pallas kernels  56.9 us (10%)
  other arithmetic  30 us (5%)
    ppermute x78, waiting for transfers between devices, move(): return lax.ppermute(value, BOTH, pairs)  177 us
    ppermute x78, starting transfers between devices, move(): return lax.ppermute(value, BOTH, pairs)  111 us
    rev x1, local copies, waits for them, and re-layouts, per_device(): params = jnp.where(y == 0, params, params[::-1])  28.8 us
    dot_general x8, matrix products, dot(): return jnp.dot(left, right, preferred_element_type=F32)  27.2 us
    ppermute x8, starting transfers between devices, shifted(): return lax.ppermute(value, 'wide', pairs)  24.8 us
    pallas_call x2, Pallas kernels, attention_backward(): pl.pallas_call(functools.partial(attention_backward_body, mode), out_shap...  22.4 us
    ppermute x8, waiting for transfers between devices, shifted(): return lax.ppermute(value, 'wide', pairs)  21.5 us
    dot_general x10, matrix products, dot_tn(): lax.dot_general(left, right, (((0,), (0,)), ((), ())), preferred_element_...  19.4 us
  transfers between devices with their start and end apart: 86, of which 21 were waited for; matrix products, arithmetic and copies ran while one was open for 30% of the time, Pallas kernels for 10%

profile of v1, /device:TPU:0, one launch (start us, length us, event | category | flops | bytes accessed | tf_op | source)
XLA Modules:
  0.0 577.8 jit_solution(14419821290987655663)
XLA Ops:
  2.6 5.1 collective-permute-start.14
  12.1 2.9 collective-permute-start.4
  21.9 3.7 collective-permute-start
  28.1 2.7 collective-permute-start.25
  30.8 10.9 %collective-permute-start.26 = (bf16[48,3072]{1,0:T(8,128)(2,1)}, bf16[48,3072]{1,0:T(8,128)(2,1)S(1)}, u32[]{:S(2)}, u32[]{:S(2)}) collective-permute-start(bf16[48,3072]{1,0:T(8,128)(2,1)} %constant_dynamic-slice_fusion.38), channel_id=1, source_target_pairs={{0,2},{1,3},{2,4},{3,5},{4,6},{5,7},{6,0},{7,1},{8,10},{9,11},{10,... | collective-permute-start | bytes 884744 | tf_op jit(solution)/shard_map/ppermute | solution.py:64
  41.7 7.4 %collective-permute-start.1 = (bf16[128,768]{1,0:T(8,128)(2,1)S(1)}, bf16[128,768]{1,0:T(8,128)(2,1)S(1)}, u32[]{:S(2)}, u32[]{:S(2)}) collective-permute-start(bf16[128,768]{1,0:T(8,128)(2,1)S(1)} %copy-done.3), channel_id=1, source_target_pairs={{0,3},{1,4},{2,5},{3,6},{4,7},{8,11},{9,12},{10,13},{11,14},{12,15... | collective-permute-start | bytes 589832 | tf_op jit(solution)/shard_map/ppermute | solution.py:69
  50.2 4.4 collective-permute-start.2
  54.6 4.0 collective-permute-start.3
  58.6 19.3 %collective-permute-start.8 = (bf16[96,1920]{1,0:T(8,128)(2,1)S(1)}, bf16[96,1920]{1,0:T(8,128)(2,1)S(1)}, u32[]{:S(2)}, u32[]{:S(2)}) collective-permute-start(bf16[96,1920]{1,0:T(8,128)(2,1)S(1)} %get-tuple-element.148), channel_id=1, source_target_pairs={{0,6},{1,7},{2,0},{3,1},{4,2},{5,3},{6,4},{7,5},{8,14},{9,15},{10,... | collective-permute-start | bytes 1105928 | tf_op jit(solution)/shard_map/ppermute | solution.py:64
  78.0 12.2 %collective-permute-start.9 = (bf16[96,1920]{1,0:T(8,128)(2,1)S(1)}, bf16[96,1920]{1,0:T(8,128)(2,1)S(1)}, u32[]{:S(2)}, u32[]{:S(2)}) collective-permute-start(bf16[96,1920]{1,0:T(8,128)(2,1)S(1)} %get-tuple-element.148), channel_id=1, source_target_pairs={{0,4},{1,5},{2,6},{3,7},{4,0},{5,1},{6,2},{7,3},{8,12},{9,13},{10,... | collective-permute-start | bytes 1105928 | tf_op jit(solution)/shard_map/ppermute | solution.py:64
  92.1 2.0 collective-permute-start.7
  96.8 16.5 %collective-permute-done.9 = bf16[96,1920]{1,0:T(8,128)(2,1)S(1)} collective-permute-done((bf16[96,1920]{1,0:T(8,128)(2,1)S(1)}, bf16[96,1920]{1,0:T(8,128)(2,1)S(1)}, u32[]{:S(2)}, u32[]{:S(2)}) %collective-permute-start.9) | collective-permute-done | bytes 368672 | tf_op jit(solution)/shard_map/ppermute | solution.py:64
  113.4 4.7 collective-permute-start.27
  120.4 28.8 %rev.3 = bf16[2,4,12288]{2,0,1:T(2,128)(2,1)} reverse(bf16[2,4,12288]{2,0,1:T(2,128)(2,1)S(1)} %copy.47), dimensions={0} | reverse | bytes 393216 | tf_op jit(solution)/shard_map/rev | solution.py:346
  150.8 25.8 %collective-permute-done.11.refs_1_ = bf16[4,96,1920]{2,1,0:T(8,128)(2,1)} collective-permute-done((bf16[4,96,1920]{2,1,0:T(8,128)(2,1)S(1)}, bf16[4,96,1920]{2,1,0:T(8,128)(2,1)}, u32[]{:S(2)}, u32[]{:S(2)}) %collective-permute-start.11) | collective-permute-done | bytes 1474592 | tf_op jit(solution)/shard_map/ppermute | solution.py:64
  181.8 2.0 slice_reduce_fusion
  198.9 2.1 fusion.10
  201.0 1.6 slice.330
  204.0 2.0 pad_maximum_fusion.10
  206.8 4.3 assemble.4
  211.1 4.5 fusion.kv_ref
  216.1 14.5 %collective-permute-done.29.refs_3_ = bf16[4,48,3072]{2,1,0:T(8,128)(2,1)} collective-permute-done((bf16[4,48,3072]{2,1,0:T(8,128)(2,1)}, bf16[4,48,3072]{2,1,0:T(8,128)(2,1)}, u32[]{:S(2)}, u32[]{:S(2)}) %collective-permute-start.29) | collective-permute-done | bytes 1179680 | tf_op jit(solution)/shard_map/ppermute | solution.py:64
  231.2 5.9 %assemble.3 = (bf16[768,2304]{1,0:T(8,128)(2,1)}, bf16[768,768]{1,0:T(8,128)(2,1)}, bf16[768,768]{1,0:T(8,128)(2,1)}) custom-call(s32[4]{0:T(128)} %pad_add_fusion.coords_ref, bf16[4,96,1920]{2,1,0:T(8,128)(2,1)} %copy-done.2, bf16[4,96,1920]{2,1,0:T(8,128)(2,1)} %collective-permute-done.11.refs_1_, bf16[4,96,1920]{2,1,0:T(8,128)(2,1)} %collective-permute-done.12.refs_2_, ...), custom_call_target="tpu_custom_call" | custom-call | bytes 11796480 | tf_op jit(solution)/shard_map/assemble/pallas_call | solution.py:245
  237.0 5.0 add_convert_fusion.1.kv_ref
  242.0 2.4 fusion.25.q_ref
  244.4 8.3 %self_forward.1 = bf16[128,768]{1,0:T(8,128)(2,1)} custom-call(s32[1]{0:T(128)} %bitcast.info_ref, s32[1,4]{1,0:T(1,128)} %lengths_ref.7, s32[1,4]{1,0:T(1,128)} %counts_ref.7, s32[1,640]{1,0:T(1,128)} %iota_add_fusion.1.pos_ref, bf16[128,768]{1,0:T(8,128)(2,1)} %fusion.25.q_ref, bf16[640,1536]{1,0:T(8,128)(2,1)} %add_convert_fusion.1.kv_ref), custom_call_target="tpu_custom_call" | custom-call | flops 503316480 | bytes 3932160 | tf_op jit(solution)/shard_map/self_forward/pallas_call | solution.py:169
  255.6 7.4 %cross_forward.1 = bf16[128,768]{1,0:T(8,128)(2,1)} custom-call(s32[1]{0:T(128)} %bitcast.info_ref, s32[1,4]{1,0:T(1,128)} %lengths_ref.7, s32[1,4]{1,0:T(1,128)} %counts_ref.7, s32[1,512]{1,0:T(1,128)} %add.528.pos_ref, bf16[128,768]{1,0:T(8,128)(2,1)} %fusion.26.q_ref, bf16[512,1536]{1,0:T(8,128)(2,1)} %fusion.kv_ref), custom_call_target="tpu_custom_call" | custom-call | flops 402653184 | bytes 3145728 | tf_op jit(solution)/shard_map/cross_forward/pallas_call | solution.py:169
  266.0 8.6 %assemble.5 = (bf16[768,3072]{1,0:T(8,128)(2,1)}, bf16[3072,768]{1,0:T(8,128)(2,1)}) custom-call(s32[4]{0:T(128)} %pad_add_fusion.coords_ref, bf16[4,48,3072]{2,1,0:T(8,128)(2,1)} %pad_maximum_fusion.5.refs_0_, bf16[4,48,3072]{2,1,0:T(8,128)(2,1)} %collective-permute-done.27.refs_1_, bf16[4,48,3072]{2,1,0:T(8,128)(2,1)} %collective-permute-done.28.refs_2_, ...), custom_call_target="tpu_custom_call" | custom-call | bytes 18874368 | tf_op jit(solution)/shard_map/assemble/pallas_call | solution.py:245
  274.6 7.5 %multiply_convert_fusion = (bf16[128,3072]{1,0:T(8,128)(2,1)}, f32[128,3072]{1,0:T(8,128)S(1)}, f32[128,3072]{1,0:T(8,128)S(1)}) fusion(f32[3072]{0:T(1024)S(1)} %copy-done.71, bf16[128,768]{1,0:T(8,128)(2,1)} %add_convert_fusion.6, bf16[768,3072]{1,0:T(8,128)(2,1)} %get-tuple-element.29), kind=kOutput, calls=%fused_computation.34 | convolution fusion | flops 629932032 | bytes 8859648 | tf_op jit(solution)/shard_map/dot_general | solution.py:23
  282.1 1.9 convert_reduce_fusion.2
  284.5 1.8 multiply_reduce_fusion
  289.2 10.4 %cross_backward.1 = (bf16[128,768]{1,0:T(8,128)(2,1)}, bf16[512,1536]{1,0:T(8,128)(2,1)}) custom-call(s32[1]{0:T(128)} %bitcast.info_ref, s32[1,4]{1,0:T(1,128)} %lengths_ref.7, s32[1,4]{1,0:T(1,128)} %counts_ref.7, s32[1,512]{1,0:T(1,128)} %add.528.pos_ref, bf16[128,768]{1,0:T(8,128)(2,1)} %fusion.26.q_ref, bf16[512,1536]{1,0:T(8,128)(2,1)} %fusion.kv_ref, ...), custom_call_target="tpu_custom_call" | custom-call | flops 1006632960 | bytes 6291456 | tf_op jit(solution)/shard_map/cross_backward/pallas_call | solution.py:184
  299.6 1.7 multiply_reduce_fusion.1
  303.5 12.0 %self_backward.1 = (bf16[128,768]{1,0:T(8,128)(2,1)}, bf16[640,1536]{1,0:T(8,128)(2,1)}) custom-call(s32[1]{0:T(128)} %bitcast.info_ref, s32[1,4]{1,0:T(1,128)} %lengths_ref.7, s32[1,4]{1,0:T(1,128)} %counts_ref.7, s32[1,640]{1,0:T(1,128)} %iota_add_fusion.1.pos_ref, bf16[128,768]{1,0:T(8,128)(2,1)} %fusion.25.q_ref, ...), custom_call_target="tpu_custom_call" | custom-call | flops 1258291200 | bytes 7864320 | tf_op jit(solution)/shard_map/self_backward/pallas_call | solution.py:184
  315.5 5.4 fusion.147
  325.7 2.3 convolution_convert_fusion.2
  336.3 4.1 fusion.24
  357.0 2.8 collective-permute-done.35
  359.8 4.8 collective-permute-done.36
  364.6 13.8 %collective-permute-done.37 = bf16[128,768]{1,0:T(8,128)(2,1)S(1)} collective-permute-done((bf16[128,768]{1,0:T(8,128)(2,1)S(1)}, bf16[128,768]{1,0:T(8,128)(2,1)S(1)}, u32[]{:S(2)}, u32[]{:S(2)}) %collective-permute-start.37) | collective-permute-done | bytes 196640 | tf_op jit(solution)/shard_map/ppermute | solution.py:69
  378.5 2.1 fusion.61
  383.7 2.9 collective-permute-done.81
  387.6 3.4 collective-permute-done.82
  391.7 1.8 convolution_convert_fusion.1
  393.9 2.4 convolution_convert_fusion.6
  397.3 2.4 convolution_convert_fusion.5
  402.4 3.0 collective-permute-done.38
  412.7 2.5 collective-permute-start.40
  415.2 3.0 convolution_convert_fusion.8
  419.3 2.8 convolution_convert_fusion.7
  423.6 2.0 collective-permute-start.63
  427.9 2.4 convolution_convert_fusion
  433.4 18.2 %collective-permute-done.63 = bf16[4,96,1536]{2,1,0:T(8,128)(2,1)S(1)} collective-permute-done((bf16[4,96,1536]{2,1,0:T(8,128)(2,1)S(1)}, bf16[4,96,1536]{2,1,0:T(8,128)(2,1)S(1)}, u32[]{:S(2)}, u32[]{:S(2)}) %collective-permute-start.63) | collective-permute-done | bytes 1179680 | tf_op jit(solution)/shard_map/ppermute | solution.py:64
  453.6 2.8 collective-permute-start.66
  458.2 5.7 collective-permute-done.64
  463.9 11.0 %collective-permute-done.65 = bf16[96,1536]{1,0:T(8,128)(2,1)S(1)} collective-permute-done((bf16[96,1536]{1,0:T(8,128)(2,1)S(1)}, bf16[96,1536]{1,0:T(8,128)(2,1)S(1)}, u32[]{:S(2)}, u32[]{:S(2)}) %collective-permute-start.65) | collective-permute-done | bytes 294944 | tf_op jit(solution)/shard_map/ppermute | solution.py:64
  476.8 8.1 %collective-permute-start.51 = (bf16[48,1536]{1,0:T(8,128)(2,1)S(1)}, bf16[48,1536]{1,0:T(8,128)(2,1)S(1)}, u32[]{:S(2)}, u32[]{:S(2)}) collective-permute-start(bf16[48,1536]{1,0:T(8,128)(2,1)S(1)} %get-tuple-element.131), channel_id=1, source_target_pairs={{0,2},{1,3},{2,4},{3,5},{4,6},{5,7},{6,0},{7,1},{8,10},{9,11},{10,... | collective-permute-start | bytes 442376 | tf_op jit(solution)/shard_map/ppermute | solution.py:64
  484.9 2.4 collective-permute-start.53
  487.3 22.6 %collective-permute-done.67 = bf16[96,1536]{1,0:T(8,128)(2,1)S(1)} collective-permute-done((bf16[96,1536]{1,0:T(8,128)(2,1)S(1)}, bf16[96,1536]{1,0:T(8,128)(2,1)S(1)}, u32[]{:S(2)}, u32[]{:S(2)}) %collective-permute-start.67) | collective-permute-done | bytes 294944 | tf_op jit(solution)/shard_map/ppermute | solution.py:64
  516.7 24.3 %collective-permute-done.74 = bf16[4,48,3072]{2,1,0:T(8,128)(2,1)S(1)} collective-permute-done((bf16[4,48,3072]{2,1,0:T(8,128)(2,1)S(1)}, bf16[4,48,3072]{2,1,0:T(8,128)(2,1)S(1)}, u32[]{:S(2)}, u32[]{:S(2)}) %collective-permute-start.74) | collective-permute-done | bytes 1179680 | tf_op jit(solution)/shard_map/ppermute | solution.py:64
  542.8 2.5 collective-permute-start.77
  545.4 7.9 %collective-permute-done.75 = bf16[48,3072]{1,0:T(8,128)(2,1)S(1)} collective-permute-done((bf16[48,3072]{1,0:T(8,128)(2,1)S(1)}, bf16[48,3072]{1,0:T(8,128)(2,1)S(1)}, u32[]{:S(2)}, u32[]{:S(2)}) %collective-permute-start.75) | collective-permute-done | bytes 294944 | tf_op jit(solution)/shard_map/ppermute | solution.py:64
  553.3 11.1 %collective-permute-done.76 = bf16[48,3072]{1,0:T(8,128)(2,1)S(1)} collective-permute-done((bf16[48,3072]{1,0:T(8,128)(2,1)S(1)}, bf16[48,3072]{1,0:T(8,128)(2,1)S(1)}, u32[]{:S(2)}, u32[]{:S(2)}) %collective-permute-start.76) | collective-permute-done | bytes 294944 | tf_op jit(solution)/shard_map/ppermute | solution.py:64
  565.9 7.0 %collective-permute-done.78 = bf16[48,3072]{1,0:T(8,128)(2,1)S(1)} collective-permute-done((bf16[48,3072]{1,0:T(8,128)(2,1)S(1)}, bf16[48,3072]{1,0:T(8,128)(2,1)S(1)}, u32[]{:S(2)}, u32[]{:S(2)}) %collective-permute-start.78) | collective-permute-done | bytes 294944 | tf_op jit(solution)/shard_map/ppermute | solution.py:64
  (508 shorter events, 132.8 us)
Async XLA Ops:
  2.6 19.2 %collective-permute-start.14 = (bf16[48,1152]{1,0:T(8,128)(2,1)S(1)}, bf16[48,1152]{1,0:T(8,128)(2,1)S(1)}, u32[]{:S(2)}, u32[]{:S(2)}) collective-permute-start(bf16[48,1152]{1,0:T(8,128)(2,1)S(1)} %fusion.112), channel_id=1, source_target_pairs={{0,6},{1,7},{2,0},{3,1},{4,2},{5,3},{6,4},{7,5},{8,14},{9,15},{10,... | collective-permute-start | bytes 331784 | tf_op jit(solution)/shard_map/ppermute | solution.py:64
  7.8 14.1 %collective-permute-start.15 = (bf16[48,1152]{1,0:T(8,128)(2,1)S(1)}, bf16[48,1152]{1,0:T(8,128)(2,1)S(1)}, u32[]{:S(2)}, u32[]{:S(2)}) collective-permute-start(bf16[48,1152]{1,0:T(8,128)(2,1)S(1)} %fusion.112), channel_id=1, source_target_pairs={{0,4},{1,5},{2,6},{3,7},{4,0},{5,1},{6,2},{7,3},{8,12},{9,13},{10,... | collective-permute-start | bytes 331784 | tf_op jit(solution)/shard_map/ppermute | solution.py:64
  7.8 17.8 %collective-permute-start.16 = (bf16[48,1152]{1,0:T(8,128)(2,1)S(1)}, bf16[48,1152]{1,0:T(8,128)(2,1)S(1)}, u32[]{:S(2)}, u32[]{:S(2)}) collective-permute-start(bf16[48,1152]{1,0:T(8,128)(2,1)S(1)} %fusion.112), channel_id=1, source_target_pairs={{0,2},{1,3},{2,4},{3,5},{4,6},{5,7},{6,0},{7,1},{8,10},{9,11},{10,... | collective-permute-start | bytes 331784 | tf_op jit(solution)/shard_map/ppermute | solution.py:64
  12.1 16.0 %collective-permute-start.4 = (bf16[80,768]{1,0:T(8,128)(2,1)S(1)}, bf16[80,768]{1,0:T(8,128)(2,1)}, u32[]{:S(2)}, u32[]{:S(2)}) collective-permute-start(bf16[80,768]{1,0:T(8,128)(2,1)S(1)} %constant_dynamic-update-slice_fusion.5), channel_id=1, source_target_pairs={{0,6},{1,7},{2,0},{3,1},{4,2},{5,3},{6,4},{7,5},{8,14},{9,15},{10,... | collective-permute-start | bytes 368648 | tf_op jit(solution)/shard_map/ppermute | solution.py:64
  14.9 15.9 %collective-permute-start.5 = (bf16[80,768]{1,0:T(8,128)(2,1)S(1)}, bf16[80,768]{1,0:T(8,128)(2,1)}, u32[]{:S(2)}, u32[]{:S(2)}) collective-permute-start(bf16[80,768]{1,0:T(8,128)(2,1)S(1)} %constant_dynamic-update-slice_fusion.5), channel_id=1, source_target_pairs={{0,4},{1,5},{2,6},{3,7},{4,0},{5,1},{6,2},{7,3},{8,12},{9,13},{10,... | collective-permute-start | bytes 368648 | tf_op jit(solution)/shard_map/ppermute | solution.py:64
  21.9 19.8 %collective-permute-start.6 = (bf16[80,768]{1,0:T(8,128)(2,1)S(1)}, bf16[80,768]{1,0:T(8,128)(2,1)S(1)}, u32[]{:S(2)}, u32[]{:S(2)}) collective-permute-start(bf16[80,768]{1,0:T(8,128)(2,1)S(1)} %constant_dynamic-update-slice_fusion.5), channel_id=1, source_target_pairs={{0,2},{1,3},{2,4},{3,5},{4,6},{5,7},{6,0},{7,1},{8,10},{9,11},{10,... | collective-permute-start | bytes 368648 | tf_op jit(solution)/shard_map/ppermute | solution.py:64
  21.9 28.3 %collective-permute-start = (bf16[128,768]{1,0:T(8,128)(2,1)S(1)}, bf16[128,768]{1,0:T(8,128)(2,1)S(1)}, u32[]{:S(2)}, u32[]{:S(2)}) collective-permute-start(bf16[128,768]{1,0:T(8,128)(2,1)S(1)} %copy-done.3), channel_id=1, source_target_pairs={{0,4},{1,5},{2,6},{3,7},{8,12},{9,13},{10,14},{11,15},{16,20},{17,... | collective-permute-start | bytes 589832 | tf_op jit(solution)/shard_map/ppermute | solution.py:69
  25.6 65.3 %collective-permute-start.24 = (bf16[48,3072]{1,0:T(8,128)(2,1)}, bf16[48,3072]{1,0:T(8,128)(2,1)S(1)}, u32[]{:S(2)}, u32[]{:S(2)}) collective-permute-start(bf16[48,3072]{1,0:T(8,128)(2,1)} %constant_dynamic-slice_fusion.38), channel_id=1, source_target_pairs={{0,6},{1,7},{2,0},{3,1},{4,2},{5,3},{6,4},{7,5},{8,14},{9,15},{10,... | collective-permute-start | bytes 884744 | tf_op jit(solution)/shard_map/ppermute | solution.py:64
  28.1 64.0 %collective-permute-start.25 = (bf16[48,3072]{1,0:T(8,128)(2,1)}, bf16[48,3072]{1,0:T(8,128)(2,1)S(1)}, u32[]{:S(2)}, u32[]{:S(2)}) collective-permute-start(bf16[48,3072]{1,0:T(8,128)(2,1)} %constant_dynamic-slice_fusion.38), channel_id=1, source_target_pairs={{0,4},{1,5},{2,6},{3,7},{4,0},{5,1},{6,2},{7,3},{8,12},{9,13},{10,... | collective-permute-start | bytes 884744 | tf_op jit(solution)/shard_map/ppermute | solution.py:64
  30.8 61.3 %collective-permute-start.26 = (bf16[48,3072]{1,0:T(8,128)(2,1)}, bf16[48,3072]{1,0:T(8,128)(2,1)S(1)}, u32[]{:S(2)}, u32[]{:S(2)}) collective-permute-start(bf16[48,3072]{1,0:T(8,128)(2,1)} %constant_dynamic-slice_fusion.38), channel_id=1, source_target_pairs={{0,2},{1,3},{2,4},{3,5},{4,6},{5,7},{6,0},{7,1},{8,10},{9,11},{10,... | collective-permute-start | bytes 884744 | tf_op jit(solution)/shard_map/ppermute | solution.py:64
  41.7 12.9 %collective-permute-start.1 = (bf16[128,768]{1,0:T(8,128)(2,1)S(1)}, bf16[128,768]{1,0:T(8,128)(2,1)S(1)}, u32[]{:S(2)}, u32[]{:S(2)}) collective-permute-start(bf16[128,768]{1,0:T(8,128)(2,1)S(1)} %copy-done.3), channel_id=1, source_target_pairs={{0,3},{1,4},{2,5},{3,6},{4,7},{8,11},{9,12},{10,13},{11,14},{12,15... | collective-permute-start | bytes 589832 | tf_op jit(solution)/shard_map/ppermute | solution.py:69
  54.6 23.4 %collective-permute-start.3 = (bf16[128,768]{1,0:T(8,128)(2,1)S(1)}, bf16[128,768]{1,0:T(8,128)(2,1)S(1)}, u32[]{:S(2)}, u32[]{:S(2)}) collective-permute-start(bf16[128,768]{1,0:T(8,128)(2,1)S(1)} %copy-done.3), channel_id=1, source_target_pairs={{0,1},{1,2},{2,3},{3,4},{4,5},{5,6},{6,7},{8,9},{9,10},{10,11},{11... | collective-permute-start | bytes 589832 | tf_op jit(solution)/shard_map/ppermute | solution.py:69
  58.6 36.7 %collective-permute-start.8 = (bf16[96,1920]{1,0:T(8,128)(2,1)S(1)}, bf16[96,1920]{1,0:T(8,128)(2,1)S(1)}, u32[]{:S(2)}, u32[]{:S(2)}) collective-permute-start(bf16[96,1920]{1,0:T(8,128)(2,1)S(1)} %get-tuple-element.148), channel_id=1, source_target_pairs={{0,6},{1,7},{2,0},{3,1},{4,2},{5,3},{6,4},{7,5},{8,14},{9,15},{10,... | collective-permute-start | bytes 1105928 | tf_op jit(solution)/shard_map/ppermute | solution.py:64
  78.0 35.3 %collective-permute-start.9 = (bf16[96,1920]{1,0:T(8,128)(2,1)S(1)}, bf16[96,1920]{1,0:T(8,128)(2,1)S(1)}, u32[]{:S(2)}, u32[]{:S(2)}) collective-permute-start(bf16[96,1920]{1,0:T(8,128)(2,1)S(1)} %get-tuple-element.148), channel_id=1, source_target_pairs={{0,4},{1,5},{2,6},{3,7},{4,0},{5,1},{6,2},{7,3},{8,12},{9,13},{10,... | collective-permute-start | bytes 1105928 | tf_op jit(solution)/shard_map/ppermute | solution.py:64
  90.9 22.4 %collective-permute-start.10 = (bf16[96,1920]{1,0:T(8,128)(2,1)S(1)}, bf16[96,1920]{1,0:T(8,128)(2,1)S(1)}, u32[]{:S(2)}, u32[]{:S(2)}) collective-permute-start(bf16[96,1920]{1,0:T(8,128)(2,1)S(1)} %get-tuple-element.148), channel_id=1, source_target_pairs={{0,2},{1,3},{2,4},{3,5},{4,6},{5,7},{6,0},{7,1},{8,10},{9,11},{10,... | collective-permute-start | bytes 1105928 | tf_op jit(solution)/shard_map/ppermute | solution.py:64
  92.1 26.2 %collective-permute-start.17 = (bf16[4,48,1152]{2,1,0:T(8,128)(2,1)S(1)}, bf16[4,48,1152]{2,1,0:T(8,128)(2,1)}, u32[]{:S(2)}, u32[]{:S(2)}) collective-permute-start(bf16[4,48,1152]{2,1,0:T(8,128)(2,1)S(1)} %pad_maximum_fusion.12.refs_0_), channel_id=1, source_target_pairs={{0,1},{1,0},{2,3},{3,2},{4,5},{5,4},{6,7},{7,6},{8,9},{9,8},{10,11... | collective-permute-start | bytes 1327112 | tf_op jit(solution)/shard_map/ppermute | solution.py:64
  92.1 26.3 %collective-permute-start.7 = (bf16[4,80,768]{2,1,0:T(8,128)(2,1)S(1)}, bf16[4,80,768]{2,1,0:T(8,128)(2,1)S(1)}, u32[]{:S(2)}, u32[]{:S(2)}) collective-permute-start(bf16[4,80,768]{2,1,0:T(8,128)(2,1)S(1)} %get-tuple-element.143), channel_id=1, source_target_pairs={{0,1},{1,0},{2,3},{3,2},{4,5},{5,4},{6,7},{7,6},{8,9},{9,8},{10,11... | collective-permute-start | bytes 1474568 | tf_op jit(solution)/shard_map/ppermute | solution.py:64
  95.3 54.2 %collective-permute-start.18 = (bf16[4,48,1152]{2,1,0:T(8,128)(2,1)S(1)}, bf16[4,48,1152]{2,1,0:T(8,128)(2,1)}, u32[]{:S(2)}, u32[]{:S(2)}) collective-permute-start(bf16[4,48,1152]{2,1,0:T(8,128)(2,1)S(1)} %pad_maximum_fusion.12.refs_0_), channel_id=1, source_target_pairs={{0,16},{1,17},{2,18},{3,19},{4,20},{5,21},{6,22},{7,23},{8,24},{9,... | collective-permute-start | bytes 1327112 | tf_op jit(solution)/shard_map/ppermute | solution.py:64
  113.3 36.9 %collective-permute-start.20 = (bf16[4,48,1152]{2,1,0:T(8,128)(2,1)S(1)}, bf16[4,48,1152]{2,1,0:T(8,128)(2,1)}, u32[]{:S(2)}, u32[]{:S(2)}) collective-permute-start(bf16[4,48,1152]{2,1,0:T(8,128)(2,1)S(1)} %pad_maximum_fusion.12.refs_0_), channel_id=1, source_target_pairs={{0,8},{1,9},{2,10},{3,11},{4,12},{5,13},{6,14},{7,15},{8,0},{9,1},... | collective-permute-start | bytes 1327112 | tf_op jit(solution)/shard_map/ppermute | solution.py:64
  113.4 65.0 %collective-permute-start.27 = (bf16[4,48,3072]{2,1,0:T(8,128)(2,1)}, bf16[4,48,3072]{2,1,0:T(8,128)(2,1)}, u32[]{:S(2)}, u32[]{:S(2)}) collective-permute-start(bf16[4,48,3072]{2,1,0:T(8,128)(2,1)} %pad_maximum_fusion.5.refs_0_), channel_id=1, source_target_pairs={{0,1},{1,0},{2,3},{3,2},{4,5},{5,4},{6,7},{7,6},{8,9},{9,8},{10,11... | collective-permute-start | bytes 3538952 | tf_op jit(solution)/shard_map/ppermute | solution.py:64
  118.3 58.2 %collective-permute-start.11 = (bf16[4,96,1920]{2,1,0:T(8,128)(2,1)S(1)}, bf16[4,96,1920]{2,1,0:T(8,128)(2,1)}, u32[]{:S(2)}, u32[]{:S(2)}) collective-permute-start(bf16[4,96,1920]{2,1,0:T(8,128)(2,1)S(1)} %pad_maximum_fusion.2.refs_0_), channel_id=1, source_target_pairs={{0,1},{1,0},{2,3},{3,2},{4,5},{5,4},{6,7},{7,6},{8,9},{9,8},{10,11... | collective-permute-start | bytes 4423688 | tf_op jit(solution)/shard_map/ppermute | solution.py:64
  118.4 58.2 %collective-permute-start.19 = (bf16[4,48,1152]{2,1,0:T(8,128)(2,1)}, bf16[4,48,1152]{2,1,0:T(8,128)(2,1)}, u32[]{:S(2)}, u32[]{:S(2)}) collective-permute-start(bf16[4,48,1152]{2,1,0:T(8,128)(2,1)} %collective-permute-done.17.refs_1_), channel_id=1, source_target_pairs={{0,16},{1,17},{2,18},{3,19},{4,20},{5,21},{6,22},{7,23},{8,24},{9,... | collective-permute-start | bytes 1327112 | tf_op jit(solution)/shard_map/ppermute | solution.py:64
  149.6 28.6 %collective-permute-start.21 = (bf16[4,48,1152]{2,1,0:T(8,128)(2,1)}, bf16[4,48,1152]{2,1,0:T(8,128)(2,1)}, u32[]{:S(2)}, u32[]{:S(2)}) collective-permute-start(bf16[4,48,1152]{2,1,0:T(8,128)(2,1)} %collective-permute-done.17.refs_1_), channel_id=1, source_target_pairs={{0,8},{1,9},{2,10},{3,11},{4,12},{5,13},{6,14},{7,15},{8,0},{9,1},... | collective-permute-start | bytes 1327112 | tf_op jit(solution)/shard_map/ppermute | solution.py:64
  150.3 65.8 %collective-permute-start.12 = (bf16[4,96,1920]{2,1,0:T(8,128)(2,1)S(1)}, bf16[4,96,1920]{2,1,0:T(8,128)(2,1)}, u32[]{:S(2)}, u32[]{:S(2)}) collective-permute-start(bf16[4,96,1920]{2,1,0:T(8,128)(2,1)S(1)} %pad_maximum_fusion.2.refs_0_), channel_id=1, source_target_pairs={{0,8},{1,9},{2,10},{3,11},{4,12},{5,13},{6,14},{7,15},{8,0},{9,1},... | collective-permute-start | bytes 4423688 | tf_op jit(solution)/shard_map/ppermute | solution.py:64
  176.6 54.1 %collective-permute-start.13 = (bf16[4,96,1920]{2,1,0:T(8,128)(2,1)}, bf16[4,96,1920]{2,1,0:T(8,128)(2,1)}, u32[]{:S(2)}, u32[]{:S(2)}) collective-permute-start(bf16[4,96,1920]{2,1,0:T(8,128)(2,1)} %collective-permute-done.11.refs_1_), channel_id=1, source_target_pairs={{0,8},{1,9},{2,10},{3,11},{4,12},{5,13},{6,14},{7,15},{8,0},{9,1},... | collective-permute-start | bytes 4423688 | tf_op jit(solution)/shard_map/ppermute | solution.py:64
  176.7 38.9 %collective-permute-start.28 = (bf16[4,48,3072]{2,1,0:T(8,128)(2,1)}, bf16[4,48,3072]{2,1,0:T(8,128)(2,1)}, u32[]{:S(2)}, u32[]{:S(2)}) collective-permute-start(bf16[4,48,3072]{2,1,0:T(8,128)(2,1)} %pad_maximum_fusion.5.refs_0_), channel_id=1, source_target_pairs={{0,16},{1,17},{2,18},{3,19},{4,20},{5,21},{6,22},{7,23},{8,24},{9,... | collective-permute-start | bytes 3538952 | tf_op jit(solution)/shard_map/ppermute | solution.py:64
  178.4 52.2 %collective-permute-start.29 = (bf16[4,48,3072]{2,1,0:T(8,128)(2,1)}, bf16[4,48,3072]{2,1,0:T(8,128)(2,1)}, u32[]{:S(2)}, u32[]{:S(2)}) collective-permute-start(bf16[4,48,3072]{2,1,0:T(8,128)(2,1)} %collective-permute-done.27.refs_1_), channel_id=1, source_target_pairs={{0,16},{1,17},{2,18},{3,19},{4,20},{5,21},{6,22},{7,23},{8,24},{9,... | collective-permute-start | bytes 3538952 | tf_op jit(solution)/shard_map/ppermute | solution.py:64
  181.8 24.2 %collective-permute-start.23 = (bf16[4,48,1152]{2,1,0:T(8,128)(2,1)}, bf16[4,48,1152]{2,1,0:T(8,128)(2,1)S(1)}, u32[]{:S(2)}, u32[]{:S(2)}) collective-permute-start(bf16[4,48,1152]{2,1,0:T(8,128)(2,1)} %collective-permute-done.19.refs_3_), channel_id=1, source_target_pairs={{0,8},{1,9},{2,10},{3,11},{4,12},{5,13},{6,14},{7,15},{8,0},{9,1},... | collective-permute-start | bytes 1327112 | tf_op jit(solution)/shard_map/ppermute | solution.py:64
  206.0 59.4 %collective-permute-start.30 = (bf16[4,48,3072]{2,1,0:T(8,128)(2,1)}, bf16[4,48,3072]{2,1,0:T(8,128)(2,1)}, u32[]{:S(2)}, u32[]{:S(2)}) collective-permute-start(bf16[4,48,3072]{2,1,0:T(8,128)(2,1)} %pad_maximum_fusion.5.refs_0_), channel_id=1, source_target_pairs={{0,8},{1,9},{2,10},{3,11},{4,12},{5,13},{6,14},{7,15},{8,0},{9,1},... | collective-permute-start | bytes 3538952 | tf_op jit(solution)/shard_map/ppermute | solution.py:64
  215.6 178.2 %collective-permute-start.56 = (bf16[512,768]{1,0:T(8,128)(2,1)}, bf16[512,768]{1,0:T(8,128)(2,1)}, u32[]{:S(2)}, u32[]{:S(2)}) collective-permute-start(bf16[512,768]{1,0:T(8,128)(2,1)} %bitcast.18), channel_id=1, source_target_pairs={{0,8},{1,9},{2,10},{3,11},{4,12},{5,13},{6,14},{7,15},{8,0},{9,1},... | collective-permute-start | bytes 2359304 | tf_op jit(solution)/shard_map/ppermute | solution.py:64
  216.1 49.3 %collective-permute-start.31 = (bf16[4,48,3072]{2,1,0:T(8,128)(2,1)}, bf16[4,48,3072]{2,1,0:T(8,128)(2,1)}, u32[]{:S(2)}, u32[]{:S(2)}) collective-permute-start(bf16[4,48,3072]{2,1,0:T(8,128)(2,1)} %collective-permute-done.27.refs_1_), channel_id=1, source_target_pairs={{0,8},{1,9},{2,10},{3,11},{4,12},{5,13},{6,14},{7,15},{8,0},{9,1},... | collective-permute-start | bytes 3538952 | tf_op jit(solution)/shard_map/ppermute | solution.py:64
  230.7 35.3 %collective-permute-start.32 = (bf16[4,48,3072]{2,1,0:T(8,128)(2,1)}, bf16[4,48,3072]{2,1,0:T(8,128)(2,1)}, u32[]{:S(2)}, u32[]{:S(2)}) collective-permute-start(bf16[4,48,3072]{2,1,0:T(8,128)(2,1)} %collective-permute-done.28.refs_2_), channel_id=1, source_target_pairs={{0,8},{1,9},{2,10},{3,11},{4,12},{5,13},{6,14},{7,15},{8,0},{9,1},... | collective-permute-start | bytes 3538952 | tf_op jit(solution)/shard_map/ppermute | solution.py:64
  230.7 35.3 %collective-permute-start.33 = (bf16[4,48,3072]{2,1,0:T(8,128)(2,1)}, bf16[4,48,3072]{2,1,0:T(8,128)(2,1)}, u32[]{:S(2)}, u32[]{:S(2)}) collective-permute-start(bf16[4,48,3072]{2,1,0:T(8,128)(2,1)} %collective-permute-done.29.refs_3_), channel_id=1, source_target_pairs={{0,8},{1,9},{2,10},{3,11},{4,12},{5,13},{6,14},{7,15},{8,0},{9,1},... | collective-permute-start | bytes 3538952 | tf_op jit(solution)/shard_map/ppermute | solution.py:64
  265.4 78.0 %collective-permute-start.44 = (bf16[128,768]{1,0:T(8,128)(2,1)}, bf16[128,768]{1,0:T(8,128)(2,1)}, u32[]{:S(2)}, u32[]{:S(2)}) collective-permute-start(bf16[128,768]{1,0:T(8,128)(2,1)} %slice.330), channel_id=1, source_target_pairs={{0,8},{1,9},{2,10},{3,11},{4,12},{5,13},{6,14},{7,15},{8,0},{9,1},... | collective-permute-start | bytes 589832 | tf_op jit(solution)/shard_map/ppermute | solution.py:64
  265.4 83.2 %collective-permute-start.59 = (bf16[128,768]{1,0:T(8,128)(2,1)}, bf16[128,768]{1,0:T(8,128)(2,1)}, u32[]{:S(2)}, u32[]{:S(2)}) collective-permute-start(bf16[128,768]{1,0:T(8,128)(2,1)} %cross_forward.1), channel_id=1, source_target_pairs={{0,8},{1,9},{2,10},{3,11},{4,12},{5,13},{6,14},{7,15},{8,0},{9,1},... | collective-permute-start | bytes 589832 | tf_op jit(solution)/shard_map/ppermute | solution.py:64
  265.9 74.5 %collective-permute-start.42 = (bf16[128,768]{1,0:T(8,128)(2,1)}, bf16[128,768]{1,0:T(8,128)(2,1)}, u32[]{:S(2)}, u32[]{:S(2)}) collective-permute-start(bf16[128,768]{1,0:T(8,128)(2,1)} %self_forward.1), channel_id=1, source_target_pairs={{0,8},{1,9},{2,10},{3,11},{4,12},{5,13},{6,14},{7,15},{8,0},{9,1},... | collective-permute-start | bytes 589832 | tf_op jit(solution)/shard_map/ppermute | solution.py:64
  340.5 12.3 %collective-permute-start.61 = (bf16[128,768]{1,0:T(8,128)(2,1)S(1)}, bf16[128,768]{1,0:T(8,128)(2,1)S(1)}, u32[]{:S(2)}, u32[]{:S(2)}) collective-permute-start(bf16[128,768]{1,0:T(8,128)(2,1)S(1)} %copy-done.40), channel_id=1, source_target_pairs={{0,8},{1,9},{2,10},{3,11},{4,12},{5,13},{6,14},{7,15},{8,0},{9,1},... | collective-permute-start | bytes 589832 | tf_op jit(solution)/shard_map/ppermute | solution.py:64
  343.4 13.5 %collective-permute-start.34 = (bf16[128,768]{1,0:T(8,128)(2,1)S(1)}, bf16[128,768]{1,0:T(8,128)(2,1)S(1)}, u32[]{:S(2)}, u32[]{:S(2)}) collective-permute-start(bf16[128,768]{1,0:T(8,128)(2,1)S(1)} %copy-done.55), channel_id=1, source_target_pairs={{1,0},{2,1},{3,2},{4,3},{5,4},{6,5},{7,6},{9,8},{10,9},{11,10},{12... | collective-permute-start | bytes 589832 | tf_op jit(solution)/shard_map/ppermute | solution.py:69
  352.8 11.8 %collective-permute-start.36 = (bf16[128,768]{1,0:T(8,128)(2,1)S(1)}, bf16[128,768]{1,0:T(8,128)(2,1)S(1)}, u32[]{:S(2)}, u32[]{:S(2)}) collective-permute-start(bf16[128,768]{1,0:T(8,128)(2,1)S(1)} %copy-done.53), channel_id=1, source_target_pairs={{3,0},{4,1},{5,2},{6,3},{7,4},{11,8},{12,9},{13,10},{14,11},{15,12... | collective-permute-start | bytes 589832 | tf_op jit(solution)/shard_map/ppermute | solution.py:69
  354.2 24.2 %collective-permute-start.37 = (bf16[128,768]{1,0:T(8,128)(2,1)S(1)}, bf16[128,768]{1,0:T(8,128)(2,1)S(1)}, u32[]{:S(2)}, u32[]{:S(2)}) collective-permute-start(bf16[128,768]{1,0:T(8,128)(2,1)S(1)} %copy-done.52), channel_id=1, source_target_pairs={{4,0},{5,1},{6,2},{7,3},{12,8},{13,9},{14,10},{15,11},{20,16},{21,... | collective-permute-start | bytes 589832 | tf_op jit(solution)/shard_map/ppermute | solution.py:69
  356.8 55.0 %collective-permute-start.46 = (bf16[640,768]{1,0:T(8,128)(2,1)}, bf16[640,768]{1,0:T(8,128)(2,1)}, u32[]{:S(2)}, u32[]{:S(2)}) collective-permute-start(bf16[640,768]{1,0:T(8,128)(2,1)} %fusion.10), channel_id=1, source_target_pairs={{0,8},{1,9},{2,10},{3,11},{4,12},{5,13},{6,14},{7,15},{8,0},{9,1},... | collective-permute-start | bytes 2949128 | tf_op jit(solution)/shard_map/ppermute | solution.py:64
  359.8 31.2 %collective-permute-start.69 = (bf16[128,768]{1,0:T(8,128)(2,1)S(1)}, bf16[128,768]{1,0:T(8,128)(2,1)S(1)}, u32[]{:S(2)}, u32[]{:S(2)}) collective-permute-start(bf16[128,768]{1,0:T(8,128)(2,1)S(1)} %copy-done.56), channel_id=1, source_target_pairs={{0,8},{1,9},{2,10},{3,11},{4,12},{5,13},{6,14},{7,15},{8,0},{9,1},... | collective-permute-start | bytes 589832 | tf_op jit(solution)/shard_map/ppermute | solution.py:64
  364.6 27.0 %collective-permute-start.70 = (bf16[128,1536]{1,0:T(8,128)(2,1)}, bf16[128,1536]{1,0:T(8,128)(2,1)}, u32[]{:S(2)}, u32[]{:S(2)}) collective-permute-start(bf16[128,1536]{1,0:T(8,128)(2,1)} %get-tuple-element.96), channel_id=1, source_target_pairs={{0,8},{1,9},{2,10},{3,11},{4,12},{5,13},{6,14},{7,15},{8,0},{9,1},... | collective-permute-start | bytes 1179656 | tf_op jit(solution)/shard_map/ppermute | solution.py:64
  391.6 21.1 %collective-permute-start.47 = (bf16[640,384]{1,0:T(8,128)(2,1)}, bf16[640,384]{1,0:T(8,128)(2,1)}, u32[]{:S(2)}, u32[]{:S(2)}) collective-permute-start(bf16[640,384]{1,0:T(8,128)(2,1)} %get-tuple-element.88), channel_id=1, source_target_pairs={{0,8},{1,9},{2,10},{3,11},{4,12},{5,13},{6,14},{7,15},{8,0},{9,1},... | collective-permute-start | bytes 1474568 | tf_op jit(solution)/shard_map/ppermute | solution.py:64
  393.8 14.4 %collective-permute-start.83 = (f32[17,768]{1,0:T(8,128)S(1)}, f32[17,768]{1,0:T(8,128)S(1)}, u32[]{:S(2)}, u32[]{:S(2)}) collective-permute-start(f32[17,768]{1,0:T(8,128)S(1)} %add.601), channel_id=1, source_target_pairs={{0,2},{1,3},{2,4},{3,5},{4,6},{5,7},{6,0},{7,1},{8,10},{9,11},{10,... | collective-permute-start | bytes 156680 | tf_op jit(solution)/shard_map/ppermute | solution.py:64
  408.2 19.6 %collective-permute-start.72 = (bf16[128,384]{1,0:T(8,128)(2,1)}, bf16[128,384]{1,0:T(8,128)(2,1)}, u32[]{:S(2)}, u32[]{:S(2)}) collective-permute-start(bf16[128,384]{1,0:T(8,128)(2,1)} %get-tuple-element.163), channel_id=1, source_target_pairs={{0,8},{1,9},{2,10},{3,11},{4,12},{5,13},{6,14},{7,15},{8,0},{9,1},... | collective-permute-start | bytes 294920 | tf_op jit(solution)/shard_map/ppermute | solution.py:64
  408.2 19.6 %collective-permute-start.71 = (bf16[128,3072]{1,0:T(8,128)(2,1)}, bf16[128,3072]{1,0:T(8,128)(2,1)}, u32[]{:S(2)}, u32[]{:S(2)}) collective-permute-start(bf16[128,3072]{1,0:T(8,128)(2,1)} %get-tuple-element.67), channel_id=1, source_target_pairs={{0,8},{1,9},{2,10},{3,11},{4,12},{5,13},{6,14},{7,15},{8,0},{9,1},... | collective-permute-start | bytes 2359304 | tf_op jit(solution)/shard_map/ppermute | solution.py:64
  412.7 12.8 %collective-permute-start.40 = (bf16[64,768]{1,0:T(8,128)(2,1)}, bf16[64,768]{1,0:T(8,128)(2,1)S(1)}, u32[]{:S(2)}, u32[]{:S(2)}) collective-permute-start(bf16[64,768]{1,0:T(8,128)(2,1)} %get-tuple-element.146), channel_id=1, source_target_pairs={{0,4},{1,5},{2,6},{3,7},{4,0},{5,1},{6,2},{7,3},{8,12},{9,13},{10,... | collective-permute-start | bytes 294920 | tf_op jit(solution)/shard_map/ppermute | solution.py:64
  423.6 28.0 %collective-permute-start.63 = (bf16[4,96,1536]{2,1,0:T(8,128)(2,1)S(1)}, bf16[4,96,1536]{2,1,0:T(8,128)(2,1)S(1)}, u32[]{:S(2)}, u32[]{:S(2)}) collective-permute-start(bf16[4,96,1536]{2,1,0:T(8,128)(2,1)S(1)} %copy-done.35), channel_id=1, source_target_pairs={{0,1},{1,0},{2,3},{3,2},{4,5},{5,4},{6,7},{7,6},{8,9},{9,8},{10,11... | collective-permute-start | bytes 3538952 | tf_op jit(solution)/shard_map/ppermute | solution.py:64
  425.5 30.9 %collective-permute-start.49 = (bf16[4,2,48,1536]{3,2,0,1:T(8,128)(2,1)S(1)}, bf16[4,2,48,1536]{3,2,0,1:T(8,128)(2,1)S(1)}, u32[]{:S(2)}, u32[]{:S(2)}) collective-permute-start(bf16[4,2,48,1536]{3,2,0,1:T(8,128)(2,1)S(1)} %pad_maximum_fusion.6), channel_id=1, source_target_pairs={{0,16},{1,17},{2,18},{3,19},{4,20},{5,21},{6,22},{7,23},{8,24},{9,... | collective-permute-start | bytes 3538952 | tf_op jit(solution)/shard_map/ppermute | solution.py:64
  432.6 79.2 %collective-permute-start.73 = (bf16[4,2,48,3072]{3,2,0,1:T(8,128)(2,1)S(1)}, bf16[4,2,48,3072]{3,2,0,1:T(8,128)(2,1)S(1)}, u32[]{:S(2)}, u32[]{:S(2)}) collective-permute-start(bf16[4,2,48,3072]{3,2,0,1:T(8,128)(2,1)S(1)} %fusion.82), channel_id=1, source_target_pairs={{0,16},{1,17},{2,18},{3,19},{4,20},{5,21},{6,22},{7,23},{8,24},{9,... | collective-permute-start | bytes 7077896 | tf_op jit(solution)/shard_map/ppermute | solution.py:64
  452.0 11.8 %collective-permute-start.64 = (bf16[96,1536]{1,0:T(8,128)(2,1)S(1)}, bf16[96,1536]{1,0:T(8,128)(2,1)S(1)}, u32[]{:S(2)}, u32[]{:S(2)}) collective-permute-start(bf16[96,1536]{1,0:T(8,128)(2,1)S(1)} %get-tuple-element.84), channel_id=1, source_target_pairs={{0,2},{1,3},{2,4},{3,5},{4,6},{5,7},{6,0},{7,1},{8,10},{9,11},{10,... | collective-permute-start | bytes 884744 | tf_op jit(solution)/shard_map/ppermute | solution.py:64
  453.1 21.7 %collective-permute-start.65 = (bf16[96,1536]{1,0:T(8,128)(2,1)S(1)}, bf16[96,1536]{1,0:T(8,128)(2,1)S(1)}, u32[]{:S(2)}, u32[]{:S(2)}) collective-permute-start(bf16[96,1536]{1,0:T(8,128)(2,1)S(1)} %get-tuple-element.86), channel_id=1, source_target_pairs={{0,4},{1,5},{2,6},{3,7},{4,0},{5,1},{6,2},{7,3},{8,12},{9,13},{10,... | collective-permute-start | bytes 884744 | tf_op jit(solution)/shard_map/ppermute | solution.py:64
  453.6 21.3 %collective-permute-start.66 = (bf16[96,1536]{1,0:T(8,128)(2,1)S(1)}, bf16[96,1536]{1,0:T(8,128)(2,1)S(1)}, u32[]{:S(2)}, u32[]{:S(2)}) collective-permute-start(bf16[96,1536]{1,0:T(8,128)(2,1)S(1)} %get-tuple-element.85), channel_id=1, source_target_pairs={{0,6},{1,7},{2,0},{3,1},{4,2},{5,3},{6,4},{7,5},{8,14},{9,15},{10,... | collective-permute-start | bytes 884744 | tf_op jit(solution)/shard_map/ppermute | solution.py:64
  456.8 19.8 %collective-permute-start.50 = (bf16[4,48,1536]{2,1,0:T(8,128)(2,1)S(1)}, bf16[4,48,1536]{2,1,0:T(8,128)(2,1)S(1)}, u32[]{:S(2)}, u32[]{:S(2)}) collective-permute-start(bf16[4,48,1536]{2,1,0:T(8,128)(2,1)S(1)} %dynamic-slice_bitcast_fusion.1), channel_id=1, source_target_pairs={{0,1},{1,0},{2,3},{3,2},{4,5},{5,4},{6,7},{7,6},{8,9},{9,8},{10,11... | collective-permute-start | bytes 1769480 | tf_op jit(solution)/shard_map/ppermute | solution.py:64
  475.0 34.9 %collective-permute-start.67 = (bf16[96,1536]{1,0:T(8,128)(2,1)S(1)}, bf16[96,1536]{1,0:T(8,128)(2,1)S(1)}, u32[]{:S(2)}, u32[]{:S(2)}) collective-permute-start(bf16[96,1536]{1,0:T(8,128)(2,1)S(1)} %fusion.51), channel_id=1, source_target_pairs={{0,16},{1,17},{2,18},{3,19},{4,20},{5,21},{6,22},{7,23},{8,24},{9,... | collective-permute-start | bytes 884744 | tf_op jit(solution)/shard_map/ppermute | solution.py:64
  476.8 33.3 %collective-permute-start.51 = (bf16[48,1536]{1,0:T(8,128)(2,1)S(1)}, bf16[48,1536]{1,0:T(8,128)(2,1)S(1)}, u32[]{:S(2)}, u32[]{:S(2)}) collective-permute-start(bf16[48,1536]{1,0:T(8,128)(2,1)S(1)} %get-tuple-element.131), channel_id=1, source_target_pairs={{0,2},{1,3},{2,4},{3,5},{4,6},{5,7},{6,0},{7,1},{8,10},{9,11},{10,... | collective-permute-start | bytes 442376 | tf_op jit(solution)/shard_map/ppermute | solution.py:64
  484.9 25.2 %collective-permute-start.52 = (bf16[48,1536]{1,0:T(8,128)(2,1)S(1)}, bf16[48,1536]{1,0:T(8,128)(2,1)S(1)}, u32[]{:S(2)}, u32[]{:S(2)}) collective-permute-start(bf16[48,1536]{1,0:T(8,128)(2,1)S(1)} %get-tuple-element.133), channel_id=1, source_target_pairs={{0,4},{1,5},{2,6},{3,7},{4,0},{5,1},{6,2},{7,3},{8,12},{9,13},{10,... | collective-permute-start | bytes 442376 | tf_op jit(solution)/shard_map/ppermute | solution.py:64
  484.9 25.2 %collective-permute-start.53 = (bf16[48,1536]{1,0:T(8,128)(2,1)S(1)}, bf16[48,1536]{1,0:T(8,128)(2,1)S(1)}, u32[]{:S(2)}, u32[]{:S(2)}) collective-permute-start(bf16[48,1536]{1,0:T(8,128)(2,1)S(1)} %get-tuple-element.132), channel_id=1, source_target_pairs={{0,6},{1,7},{2,0},{3,1},{4,2},{5,3},{6,4},{7,5},{8,14},{9,15},{10,... | collective-permute-start | bytes 442376 | tf_op jit(solution)/shard_map/ppermute | solution.py:64
  512.8 28.1 %collective-permute-start.74 = (bf16[4,48,3072]{2,1,0:T(8,128)(2,1)S(1)}, bf16[4,48,3072]{2,1,0:T(8,128)(2,1)S(1)}, u32[]{:S(2)}, u32[]{:S(2)}) collective-permute-start(bf16[4,48,3072]{2,1,0:T(8,128)(2,1)S(1)} %dynamic-slice_bitcast_fusion), channel_id=1, source_target_pairs={{0,1},{1,0},{2,3},{3,2},{4,5},{5,4},{6,7},{7,6},{8,9},{9,8},{10,11... | collective-permute-start | bytes 3538952 | tf_op jit(solution)/shard_map/ppermute | solution.py:64
  516.6 28.8 %collective-permute-start.55 = (bf16[96,1536]{1,0:T(8,128)(2,1)S(1)}, bf16[96,1536]{1,0:T(8,128)(2,1)S(1)}, u32[]{:S(2)}, u32[]{:S(2)}) collective-permute-start(bf16[96,1536]{1,0:T(8,128)(2,1)S(1)} %maximum_select_fusion.1), channel_id=1, source_target_pairs={{0,8},{1,9},{2,10},{3,11},{4,12},{5,13},{6,14},{7,15},{8,0},{9,1},... | collective-permute-start | bytes 884744 | tf_op jit(solution)/shard_map/ppermute | solution.py:64
  541.5 11.8 %collective-permute-start.75 = (bf16[48,3072]{1,0:T(8,128)(2,1)S(1)}, bf16[48,3072]{1,0:T(8,128)(2,1)S(1)}, u32[]{:S(2)}, u32[]{:S(2)}) collective-permute-start(bf16[48,3072]{1,0:T(8,128)(2,1)S(1)} %get-tuple-element.81), channel_id=1, source_target_pairs={{0,2},{1,3},{2,4},{3,5},{4,6},{5,7},{6,0},{7,1},{8,10},{9,11},{10,... | collective-permute-start | bytes 884744 | tf_op jit(solution)/shard_map/ppermute | solution.py:64
  542.4 21.9 %collective-permute-start.76 = (bf16[48,3072]{1,0:T(8,128)(2,1)S(1)}, bf16[48,3072]{1,0:T(8,128)(2,1)S(1)}, u32[]{:S(2)}, u32[]{:S(2)}) collective-permute-start(bf16[48,3072]{1,0:T(8,128)(2,1)S(1)} %get-tuple-element.83), channel_id=1, source_target_pairs={{0,4},{1,5},{2,6},{3,7},{4,0},{5,1},{6,2},{7,3},{8,12},{9,13},{10,... | collective-permute-start | bytes 884744 | tf_op jit(solution)/shard_map/ppermute | solution.py:64
  542.8 21.5 %collective-permute-start.77 = (bf16[48,3072]{1,0:T(8,128)(2,1)S(1)}, bf16[48,3072]{1,0:T(8,128)(2,1)S(1)}, u32[]{:S(2)}, u32[]{:S(2)}) collective-permute-start(bf16[48,3072]{1,0:T(8,128)(2,1)S(1)} %get-tuple-element.82), channel_id=1, source_target_pairs={{0,6},{1,7},{2,0},{3,1},{4,2},{5,3},{6,4},{7,5},{8,14},{9,15},{10,... | collective-permute-start | bytes 884744 | tf_op jit(solution)/shard_map/ppermute | solution.py:64
  (101 other events, 843.5 us)

commit v2 on v1

--- a/solution.py
+++ b/solution.py
@@ -64,9 +64,33 @@
     return lax.ppermute(value, BOTH, pairs)
 
 
+def move_mixed(value, wide, turn):
+    pairs = []
+    for x in range(2):
+        for c in range(2):
+            dx = int(c == turn)
+            for z in range(NZ):
+                for y in range(NY):
+                    source = (x * 2 + c) * wide + z * NY + y
+                    target = ((x ^ dx) * 2 + c) * wide + z * NY + (y ^ 1 ^ dx)
+                    pairs.append((source, target))
+    return lax.ppermute(value, BOTH, pairs)
+
+
 def shifted(value, wide, by):
     pairs = [(i, i + by) for i in range(wide) if 0 <= i + by < wide]
     return lax.ppermute(value, "wide", pairs)
+
+
+def along_z(value, wide, by):
+    pairs = []
+    for group in range(4):
+        for z in range(NZ):
+            for y in range(NY):
+                if 0 <= z + by < NZ:
+                    source = group * wide + z * NY + y
+                    pairs.append((source, source + by * NY))
+    return lax.ppermute(value, BOTH, pairs)
 
 
 def pick(value, index, axis):
@@ -172,9 +196,7 @@
         in_specs=[smem(), smem(), smem(), vmem(), vmem(), vmem()],
         out_specs=vmem(),
         name=mode + "_forward",
-        cost_estimate=pl.CostEstimate(
-            flops=8 * rows * count * width, bytes_accessed=8 * count * width, transcendentals=rows * count * HEADS
-        ),
+        cost_estimate=pl.CostEstimate(flops=0, bytes_accessed=rows * width, transcendentals=0),
     )(info, lengths, counts, positions, query, kv)
 
 
@@ -187,9 +209,7 @@
         in_specs=[smem(), smem(), smem(), vmem(), vmem(), vmem(), vmem()],
         out_specs=(vmem(), vmem()),
         name=mode + "_backward",
-        cost_estimate=pl.CostEstimate(
-            flops=20 * rows * count * width, bytes_accessed=16 * count * width, transcendentals=rows * count * HEADS
-        ),
+        cost_estimate=pl.CostEstimate(flops=0, bytes_accessed=rows * width, transcendentals=0),
     )(info, lengths, counts, positions, query, kv, grads)
 
 
@@ -200,87 +220,125 @@
     return [blocks[i] for i in range(blocks.shape[0])]
 
 
-def assemble_body(rows, plan, coords_ref, *refs):
-    count = len(refs) - len(plan)
-    arrays, outs = refs[:count], refs[count:]
+def assemble_copies(plan, coords_ref, arrays, outs, sems, spot):
     x, c, z, y = coords_ref[0], coords_ref[1], coords_ref[2], coords_ref[3]
-    per_core = count // 2
+    k, dz = spot // NZ, spot % NZ
+    copies = []
+    per_spot = len(arrays) * sum(blocks for blocks, _ in plan)
     for number, array in enumerate(arrays):
-        core = c ^ (number // per_core)
-        local = number % per_core
-        row_y = y ^ (local % 2)
-        row_x = x ^ (local // 2)
-
-        def step(dz, carry, array=array, core=core, row_y=row_y, row_x=row_x):
-            wide = ((z + dz) & (NZ - 1)) * NY + row_y
-            cursor = 0
-            for out, (blocks, width) in zip(outs, plan):
-                half = width // 2
-                for block in range(blocks):
-                    row = wide * (96 * blocks) + block * 96
-                    if rows < 96:
-                        row = row + row_x * rows
-                    row = pl.multiple_of(row, 16)
-                    column = pl.multiple_of(core * half, 128)
-                    out[pl.ds(row, rows), pl.ds(column, half)] = array[dz, :, cursor : cursor + half]
-                    cursor += half
-            return carry
-
-        lax.fori_loop(0, NZ, step, 0)
-
-
-def gather_weights(shards, coords, wide, use_x):
+        core = c ^ (number // 2)
+        if number % 2 == 0:
+            row_x, row_y = x ^ (k & (1 - core)), y ^ (k & core)
+        else:
+            row_x, row_y = x ^ (k | core), y ^ (k | (1 - core))
+        wide = ((z + dz) & (NZ - 1)) * NY + row_y
+        cursor = 0
+        for out, (blocks, width) in zip(outs, plan):
+            half = width // 2
+            for block in range(blocks):
+                row = pl.multiple_of(wide * (96 * blocks) + block * 96 + row_x * 48, 16)
+                column = pl.multiple_of(core * half, 128)
+                copies.append(
+                    pltpu.make_async_copy(
+                        array.at[k, dz, :, pl.ds(cursor, half)],
+                        out.at[pl.ds(row, 48), pl.ds(column, half)],
+                        sems.at[spot * per_spot + len(copies)],
+                    )
+                )
+                cursor += half
+    return copies
+
+
+def assemble_body(plan, coords_ref, *refs):
+    arrays, outs, sems = refs[:4], refs[4:-1], refs[-1]
+
+    def start(spot, carry):
+        for copy in assemble_copies(plan, coords_ref, arrays, outs, sems, spot):
+            copy.start()
+        return carry
+
+    def wait(spot, carry):
+        for copy in assemble_copies(plan, coords_ref, arrays, outs, sems, spot):
+            copy.wait()
+        return carry
+
+    lax.fori_loop(0, 2 * NZ, start, 0)
+    lax.fori_loop(0, 2 * NZ, wait, 0)
+
+
+def gather_weights(shards, coords, wide, after=None):
     x, c, z, y = coords
     own = jnp.concatenate([b for s in shards for b in half_columns(s, c)], axis=1)
-    rows = 96
-    if use_x:
-        rows = 48
-        own = lax.dynamic_slice_in_dim(own, x * rows, rows, 0)
+    own = lax.dynamic_slice_in_dim(own, x * 48, 48, 0)
+    if after is not None:
+        own, after = lax.optimization_barrier((own, after))
     column = jnp.stack([own] + [move(own, wide, dz=-d) for d in range(1, NZ)])
-    plane = [column, move(column, wide, dy=1)]
-    if use_x:
-        plane = plane + [move(v, wide, dx=1) for v in plane]
-    arrays = plane + [move(v, wide, dc=1) for v in plane]
+    pair = jnp.stack([column, move_mixed(column, wide, 0)])
+    far = move_mixed(pair, wide, 1)
+    arrays = [pair, far, move(pair, wide, dc=1), move(far, wide, dc=1)]
     plan = [(s.shape[0] // 96, s.shape[1]) for s in shards]
     return pl.pallas_call(
-        functools.partial(assemble_body, rows, plan),
+        functools.partial(assemble_body, plan),
         out_shape=tuple(jax.ShapeDtypeStruct((s.shape[0] * wide, s.shape[1]), BF16) for s in shards),
-        in_specs=[smem()] + [vmem()] * len(arrays),
+        in_specs=[smem()] + [pl.BlockSpec(memory_space=pl.ANY)] * len(arrays),
         out_specs=tuple(vmem() for s in shards),
+        scratch_shapes=[pltpu.SemaphoreType.DMA((2 * NZ * 4 * sum(blocks for blocks, _ in plan),))],
         name="assemble",
-        cost_estimate=pl.CostEstimate(
-            flops=0, bytes_accessed=sum(4 * s.size * wide for s in shards), transcendentals=0
-        ),
+        cost_estimate=pl.CostEstimate(flops=0, bytes_accessed=sum(s.size for s in shards), transcendentals=0),
     )(jnp.stack(coords).astype(jnp.int32), *arrays)
 
 
-def scatter_grads(pieces, coords, wide, use_x):
+def joined(parts):
+    return parts[0] if len(parts) == 1 else jnp.concatenate(parts, axis=-1)
+
+
+def added(kept, arrived):
+    return (kept.astype(F32) + arrived.astype(F32)).astype(BF16)
+
+
+def scatter_steps(pieces, coords, wide):
     x, c, z, y = coords
-
-    def joined(parts):
-        return parts[0] if len(parts) == 1 else jnp.concatenate(parts, axis=-1)
-
-    if use_x:
-        views = [p.reshape(NZ, NY, 2, 48, p.shape[-1]) for p in pieces]
-        arrived = move(joined([pick(v, 1 - x, 2) for v in views]), wide, dx=1)
-        kept = joined([pick(v, x, 2) for v in views])
-        block = (kept.astype(F32) + arrived.astype(F32)).astype(BF16)
-        arrived = move(pick(block, 1 - y, 1), wide, dy=1)
-        kept = pick(block, y, 1)
-    else:
-        views = [p.reshape(NZ, NY, 96, p.shape[-1]) for p in pieces]
-        arrived = move(joined([pick(v, 1 - y, 1) for v in views]), wide, dy=1)
-        kept = joined([pick(v, y, 1) for v in views])
-    column = (kept.astype(F32) + arrived.astype(F32)).astype(BF16)
+    views = [p.reshape(NZ, NY, 2, 48, p.shape[-1]) for p in pieces]
+    send = joined([jnp.where(c == 0, pick(v, 1 - x, 2), pick(v, 1 - y, 1)) for v in views])
+    keep = joined([jnp.where(c == 0, pick(v, x, 2), pick(v, y, 1)) for v in views])
+    send, keep = yield send, keep
+    block = added(keep, move_mixed(send, wide, 0))
+    own = jnp.where(c == 0, y, x)
+    send, keep = pick(block, 1 - own, 1), pick(block, own, 1)
+    send, keep = yield send, keep
+    column = added(keep, move_mixed(send, wide, 1))
+    column = yield column
     arrived = [move(pick(column, (z + d) % NZ, 0), wide, dz=d) for d in range(1, NZ)]
     total = pick(column, z, 0).astype(F32)
     for value in arrived:
         total = total + value.astype(F32)
     total = total.astype(BF16)
+    total = yield total
     other = move(total, wide, dx=1)
-    if use_x:
-        return jnp.where(x == 0, jnp.concatenate([total, other]), jnp.concatenate([other, total]))
-    return (total.astype(F32) + other.astype(F32)).astype(BF16)
+    return jnp.where(x == 0, jnp.concatenate([total, other]), jnp.concatenate([other, total]))
+
+
+class Chain:
+    def __init__(self, steps):
+        self.steps = steps
+        self.held = next(steps)
+        self.result = None
+
+    def go(self, value):
+        held, value = lax.optimization_barrier((self.held, value))
+        try:
+            self.held = self.steps.send(held)
+        except StopIteration as stop:
+            self.result = stop.value
+        return value
+
+    def finish(self):
+        while self.result is None:
+            try:
+                self.held = self.steps.send(self.held)
+            except StopIteration as stop:
+                self.result = stop.value
+        return self.result
 
 
 def finish_grads(mine, shapes, coords, wide):
@@ -332,25 +390,34 @@
     part = width // wide
 
     small = jnp.concatenate([norm_gains.reshape(-1), bias_rows.reshape(-1), mlp_bias])
-    window = jnp.concatenate([shifted(tokens, wide, o) for o in range(span, 0, -1)] + [tokens])
     if fast:
         small_rows = -(-small.shape[0] // (16 * width)) * 16
         small = jnp.pad(small, (0, small_rows * width - small.shape[0])).reshape(small_rows, width)
         own = jnp.concatenate([frames, small])
-        column = jnp.stack([own] + [move(own, wide, dz=-d) for d in range(1, NZ)])
-        plane = jnp.stack([column, move(column, wide, dy=1)])
-        all_frames = plane[:, :, :frame_rows].reshape(-1, width)
+        reach = -(-span // NY)
+        line = [own] + [move(own, wide, dz=-d) for d in range(1, NZ)]
+        earlier = [tokens] + [along_z(tokens, wide, d) for d in range(1, reach + 1)]
+        line = jnp.concatenate(line + earlier)
+        plane = jnp.stack([line, move(line, wide, dy=1)])
+        columns = plane[:, : NZ * (frame_rows + small_rows)].reshape(NY, NZ, -1, width)
+        all_frames = columns[:, :, :frame_rows].reshape(-1, width)
         number = jnp.arange(wide, dtype=jnp.int32)
         owner = ((z + number % NZ) % NZ) * NY + (y ^ (number // NZ))
-        params = plane[:, :, frame_rows:].reshape(NY, NZ, small_rows * width)
-        params = jnp.where(y == 0, params, params[::-1])
-        params = jnp.roll(params, z, axis=1)
-        params = params.transpose(1, 0, 2).reshape(wide, -1)
-        w_in, w_out, w_cross_q = gather_weights((attn_inputs, attn_output, cross_queries), coords, wide, False)
-        w_memory, w_cross_out = gather_weights((cross_memory, cross_output), coords, wide, True)
-        w_mlp_in, w_mlp_out = gather_weights((mlp_inputs, mlp_output), coords, wide, True)
+        params = columns[:, :, frame_rows:].reshape(NY, NZ, small_rows * width)
+        params = jnp.where(y == 0, jnp.stack([params[0], params[1]], 1), jnp.stack([params[1], params[0]], 1))
+        params = jnp.concatenate([params, params])
+        params = lax.dynamic_slice_in_dim(params, (NZ - z) % NZ, NZ, 0).reshape(wide, -1)
+        window = plane[:, NZ * (frame_rows + small_rows) :].reshape(-1, width)
+        blocks_at = jnp.array([NY * d for d in range(reach + 1)], jnp.int32)
+        blocks_at = jnp.concatenate([me - blocks_at, (z * NY + (1 - y)) - blocks_at])
+        w_in, w_out, w_cross_q, w_memory, w_cross_out = gather_weights(
+            (attn_inputs, attn_output, cross_queries, cross_memory, cross_output), coords, wide
+        )
+        w_mlp_in, w_mlp_out = gather_weights((mlp_inputs, mlp_output), coords, wide)
     else:
         gather = functools.partial(lax.all_gather, axis_name="wide", axis=0, tiled=True)
+        window = jnp.concatenate([tokens] + [shifted(tokens, wide, o) for o in range(1, span + 1)])
+        blocks_at = me - jnp.arange(span + 1, dtype=jnp.int32)
         all_frames = gather(frames)
         owner = jnp.arange(wide, dtype=jnp.int32)
         params = gather(small.reshape(1, -1))
@@ -362,13 +429,38 @@
     biases = biases.reshape(10, width).astype(F32)
     hidden_bias = params[:, 13 * part : 13 * part + hidden_rows].reshape(-1).astype(F32)
     frame_pos = (owner[:, None] * frame_rows + jnp.arange(frame_rows, dtype=jnp.int32)).reshape(1, -1)
-    key_pos = ((me - span) * tok_rows + jnp.arange((span + 1) * tok_rows, dtype=jnp.int32)).reshape(1, -1)
+    key_pos = (blocks_at[:, None] * tok_rows + jnp.arange(tok_rows, dtype=jnp.int32)).reshape(1, -1)
     info = me.reshape(1)
     zero_row = jnp.zeros((width,), F32)
 
+    def swapped(parts):
+        theirs = move(jnp.concatenate(parts), wide, dc=1)
+        found, cursor = [], 0
+        for value in parts:
+            found.append(theirs[cursor : cursor + value.shape[0]])
+            cursor += value.shape[0]
+        return found
+
+    def halves(values):
+        half = values[0].shape[1] // 2
+        mine = [lax.dynamic_slice_in_dim(v, c * half, half, 1) for v in values]
+        theirs = swapped([lax.dynamic_slice_in_dim(v, (1 - c) * half, half, 1) for v in values])
+        return [jnp.concatenate(pair) for pair in zip(mine, theirs)]
+
+    def doubled(values):
+        return [jnp.concatenate(pair) for pair in zip(values, swapped(values))]
+
+    def weight(left, right):
+        grad = dot_tn(left, right).astype(BF16)
+        return grad.reshape(wide, -1, 96, grad.shape[1])
+
+    def blocks(*grads):
+        return [grad[:, i] for grad in grads for i in range(grad.shape[1])]
+
     inputs = tokens.astype(F32)
-    normed_window = norm_apply(window.astype(F32), gains[0], biases[0]).astype(BF16)
-    normed_one = normed_window[span * tok_rows :]
+    normal_window = norm_parts(window.astype(F32))[0]
+    normed_window = (normal_window * gains[0] + biases[0]).astype(BF16)
+    normed_one = normed_window[:tok_rows]
     query = (dot(normed_one, w_in[:, :width]) + biases[3]).astype(BF16)
     self_kv = (dot(normed_window, w_in[:, width:]) + jnp.concatenate([zero_row, biases[4]])).astype(BF16)
     tables = (info, item_lengths, frame_lengths)
@@ -388,6 +480,17 @@
     grad_out = cotangent.astype(F32)
     grad_hidden = dot_nt(cotangent, w_mlp_out)
     grad_pre = jax.vjp(exact_gelu, pre_act)[1](grad_hidden)[0].astype(BF16)
+    if fast:
+        window_two, frames_two, one_two, attended_two, two_two, cross_att_two, three_two = doubled(
+            [normed_window, all_frames, normed_one, attended, normed_two, cross_att, normed_three]
+        )
+        (hidden_two,) = doubled([hidden])
+        (out_half,) = halves([cotangent])
+        chain_out = Chain(scatter_steps(blocks(weight(hidden_two, out_half)), coords, wide))
+        grad_pre = chain_out.go(grad_pre)
+        (pre_half,) = halves([grad_pre])
+        chain_in = Chain(scatter_steps(blocks(weight(three_two, pre_half)), coords, wide))
+        grad_pre = chain_in.go(grad_pre)
     grad_three, gain_three, shift_three = norm_back(after_two, gains[2], dot_nt(grad_pre, w_mlp_in))
     grad_after_two = grad_out + grad_three
     grad_cross_branch = grad_after_two.astype(BF16)
@@ -395,30 +498,63 @@
     grad_cross_q, grad_memory = attention_backward(
         "cross", *tables, frame_pos, cross_q, memory, grad_cross_att
     )
+    if fast:
+        grad_cross_q = chain_out.go(chain_in.go(grad_cross_q))
     grad_two, gain_two, shift_two = norm_back(after_one, gains[1], dot_nt(grad_cross_q, w_cross_q))
     grad_after_one = grad_after_two + grad_two
     grad_self_branch = grad_after_one.astype(BF16)
     grad_attended = dot_nt(grad_self_branch, w_out).astype(BF16)
-    grad_query, grad_kv = attention_backward("self", *tables, key_pos, query, self_kv, grad_attended)
 
     frame_part = dot_nt(grad_memory, w_memory)
     if fast:
+        branch_half, cross_half, keys_half, values_half = halves(
+            [grad_cross_branch, grad_cross_q, grad_memory[:, :width], grad_memory[:, width:]]
+        )
+        pieces = blocks(
+            weight(frames_two, keys_half),
+            weight(frames_two, values_half),
+            weight(cross_att_two, branch_half),
+            weight(two_two, cross_half),
+        )
+        chain_cross = Chain(scatter_steps(pieces, coords, wide))
+        grad_attended = chain_cross.go(grad_attended)
         frame_part = frame_part.astype(BF16).reshape(NY, NZ, frame_rows, width)
         arrived = move(frame_part[1], wide, dy=1)
-        line = (frame_part[0].astype(F32) + arrived.astype(F32)).astype(BF16)
+        line = added(frame_part[0], arrived)
         grad_frames = line[0].astype(F32)
         for d in range(1, NZ):
             grad_frames = grad_frames + move(line[d], wide, dz=d).astype(F32)
     else:
         grad_frames = lax.psum_scatter(frame_part, "wide", scatter_dimension=0, tiled=True)
+    grad_query, grad_kv = attention_backward("self", *tables, key_pos, query, self_kv, grad_attended)
+    if fast:
+        grad_query = chain_out.go(chain_in.go(grad_query))
+        branch_half, query_half, keys_half, values_half = halves(
+            [grad_self_branch, grad_query, grad_kv[:, :width], grad_kv[:, width:]]
+        )
+        grad_in = [weight(one_two, query_half), weight(window_two, keys_half), weight(window_two, values_half)]
+        grad_wo = weight(attended_two, branch_half)
+        chain_self = Chain(scatter_steps(blocks(*grad_in) + blocks(grad_wo), coords, wide))
+        grad_kv = chain_self.go(grad_kv)
 
     window_part = dot_nt(grad_kv, w_in[:, width:])
-    grad_one = window_part[span * tok_rows :] + dot_nt(grad_query, w_in[:, :width])
-    for o in range(1, span + 1):
-        block = window_part[(span - o) * tok_rows : (span - o + 1) * tok_rows]
-        grad_one = grad_one + shifted(block.astype(BF16), wide, -o).astype(F32)
-    grad_first, gain_one, shift_one = norm_back(inputs, gains[0], grad_one)
-    grad_tokens = grad_after_one + grad_first
+    own_part = window_part[:tok_rows] + dot_nt(grad_query, w_in[:, :width])
+    window_part = jnp.concatenate([own_part, window_part[tok_rows:]])
+    gain_one = jnp.sum(window_part * normal_window, axis=0)
+    shift_one = jnp.sum(window_part, axis=0)
+    if fast:
+        back = window_part.reshape(NY, reach + 1, tok_rows, width)
+        arrived = move(back[1].astype(BF16), wide, dy=1).astype(F32)
+        line = back[0] + arrived
+        grad_one = line[0]
+        for d in range(1, reach + 1):
+            grad_one = grad_one + along_z(line[d].astype(BF16), wide, -d).astype(F32)
+    else:
+        grad_one = own_part
+        for o in range(1, span + 1):
+            block = window_part[o * tok_rows : (o + 1) * tok_rows]
+            grad_one = grad_one + shifted(block.astype(BF16), wide, -o).astype(F32)
+    grad_tokens = grad_after_one + norm_back(inputs, gains[0], grad_one)[0]
 
     def total(value):
         return jnp.sum(value.astype(F32), axis=0)
@@ -441,70 +577,39 @@
     pre_total = total(grad_pre)
 
     if fast:
-
-        def both(value):
-            return jnp.concatenate([value, move(value, wide, dc=1)])
-
-        def split(value):
-            half = value.shape[1] // 2
-            mine = lax.dynamic_slice_in_dim(value, c * half, half, 1)
-            theirs = lax.dynamic_slice_in_dim(value, (1 - c) * half, half, 1)
-            return jnp.concatenate([mine, move(theirs, wide, dc=1)])
-
-        def weight(left, right):
-            grad = dot_tn(left, right).astype(BF16)
-            return grad.reshape(wide, -1, 96, grad.shape[1])
-
-        def blocks(grad):
-            return [grad[:, i] for i in range(grad.shape[1])]
-
-        half_hidden = weight(both(hidden), split(cotangent))
-        half_pre = weight(both(normed_three), split(grad_pre))
-        reduced = scatter_grads(blocks(half_pre) + blocks(half_hidden), coords, wide, True)
-        g_mlp_in, g_mlp_out = finish_grads(reduced, [mlp_inputs.shape, mlp_output.shape], coords, wide)
-
-        g_cross_out = weight(both(cross_att), split(grad_cross_branch))
-        frames_two = both(all_frames)
-        g_memory_k = weight(frames_two, split(grad_memory[:, :width]))
-        g_memory_v = weight(frames_two, split(grad_memory[:, width:]))
-        g_cross_q = weight(both(normed_two), split(grad_cross_q))
-        pieces = [p for g in (g_memory_k, g_memory_v, g_cross_out, g_cross_q) for p in blocks(g)]
-        reduced = scatter_grads(pieces, coords, wide, False)
-        square = (part, width)
-        g_memory_k, g_memory_v, g_cross_out, g_cross_q = finish_grads(reduced, [square] * 4, coords, wide)
-        g_memory = jnp.concatenate([g_memory_k, g_memory_v], axis=1)
-
-        g_out = weight(both(attended), split(grad_self_branch))
-        window_two = both(normed_window)
-        g_in_q = weight(both(normed_one), split(grad_query))
-        g_in_k = weight(window_two, split(grad_kv[:, :width]))
-        g_in_v = weight(window_two, split(grad_kv[:, width:]))
-        pieces = [p for g in (g_out, g_in_q, g_in_k, g_in_v) for p in blocks(g)]
-        reduced = scatter_grads(pieces, coords, wide, True)
-        g_out, g_in_q, g_in_k, g_in_v = finish_grads(reduced, [square] * 4, coords, wide)
-        g_in = jnp.concatenate([g_in_q, g_in_k, g_in_v], axis=1)
-
-        small = jnp.concatenate([jnp.stack(rows), pre_total.reshape(-1, width)])
+        extra = pre_total.reshape(wide, -1, part).transpose(1, 0, 2).reshape(-1, width)
+        small = jnp.concatenate([jnp.stack(rows), extra])
         small = small + move(small, wide, dc=1)
         small = small + move(small, wide, dx=1)
         small = small + move(small, wide, dy=1)
         arrived = [move(small, wide, dz=d) for d in range(1, NZ)]
         small = small + arrived[0] + arrived[1] + arrived[2]
-        rows_all = lax.dynamic_slice_in_dim(small[:13], me * part, part, 1)
-        g_bias = lax.dynamic_slice_in_dim(small[13:].reshape(-1), me * hidden_rows, hidden_rows, 0)
+        small = lax.dynamic_slice_in_dim(small, me * part, part, 1)
+        square = (part, width)
+        (g_mlp_in,) = finish_grads(chain_in.finish(), [mlp_inputs.shape], coords, wide)
+        (g_mlp_out,) = finish_grads(chain_out.finish(), [mlp_output.shape], coords, wide)
+        g_memory_k, g_memory_v, g_cross_out, g_cross_q = finish_grads(
+            chain_cross.finish(), [square] * 4, coords, wide
+        )
+        g_in_q, g_in_k, g_in_v, g_out = finish_grads(chain_self.finish(), [square] * 4, coords, wide)
+        g_memory = jnp.concatenate([g_memory_k, g_memory_v], axis=1)
+        g_in = jnp.concatenate([g_in_q, g_in_k, g_in_v], axis=1)
+        rows_all, g_bias = small[:13], small[13:].reshape(-1)
     else:
 
-        def weight(left, right):
+        def weight_sum(left, right):
             grad = lax.psum_scatter(dot_tn(left, right), "wide", scatter_dimension=0, tiled=True)
             return lax.psum(grad.astype(BF16), "grp").astype(F32)
 
-        g_in = jnp.concatenate([weight(normed_one, grad_query), weight(normed_window, grad_kv)], axis=1)
-        g_out = weight(attended, grad_self_branch)
-        g_cross_q = weight(normed_two, grad_cross_q)
-        g_memory = weight(all_frames, grad_memory)
-        g_cross_out = weight(cross_att, grad_cross_branch)
-        g_mlp_in = weight(normed_three, grad_pre)
-        g_mlp_out = weight(hidden, cotangent)
+        g_in = jnp.concatenate(
+            [weight_sum(normed_one, grad_query), weight_sum(normed_window, grad_kv)], axis=1
+        )
+        g_out = weight_sum(attended, grad_self_branch)
+        g_cross_q = weight_sum(normed_two, grad_cross_q)
+        g_memory = weight_sum(all_frames, grad_memory)
+        g_cross_out = weight_sum(cross_att, grad_cross_branch)
+        g_mlp_in = weight_sum(normed_three, grad_pre)
+        g_mlp_out = weight_sum(hidden, cotangent)
         small = lax.psum(jnp.stack(rows), BOTH)
         rows_all = lax.dynamic_slice_in_dim(small, me * part, part, 1)
         g_bias = lax.dynamic_slice_in_dim(lax.psum(pre_total, BOTH), me * hidden_rows, hidden_rows, 0)

time: 587 us -> 510 us (0.87)
  waiting for transfers between devices: 199 us -> 131 us
  other arithmetic: 30 us -> 52.4 us
  starting transfers between devices: 136 us -> 117 us
  matrix products: 64.3 us -> 52.8 us
    ppermute x78 -> x51, waiting for transfers between devices: 177 us -> 75.4 us  [move(): return lax.ppermute(value, BOTH, pairs)]
    ppermute x8 -> x16, waiting for transfers between devices: 21.5 us -> 55.9 us  [the longest x12 45.8 us: move_mixed(): return lax.ppermute(value, BOTH, pairs)]
    rev x1 -> x0, local copies, waits for them, and re-layouts: 28.8 us -> none  [per_device(): params = jnp.where(y == 0, params, params[::-1])]
    ppermute x78 -> x51, starting transfers between devices: 111 us -> 88.1 us  [move(): return lax.ppermute(value, BOTH, pairs)]
    unnamed x179 -> x212, local copies, waits for them, and re-layouts: 11.4 us -> 23.8 us
    slice x7 -> x15, local copies, waits for them, and re-layouts: 4.26 us -> 14.2 us  [the longest x7 6.28 us: swapped(): found.append(theirs[cursor:cursor + value.shape[0]])]
    dot_general x10, matrix products: 19.4 us -> 9.63 us  [dot_tn(): lax.dot_general(left, right, (((0,), (0,)), ((), ())), preferred_element_...]
    another operation x13 -> x14, local copies, waits for them, and re-layouts: 0.06 us -> 9.04 us  [the longest x12 5.88 us: per_device(): small = jnp.concatenate([jnp.stack(rows), extra])]
  transfers between devices with their start and end apart: 86 -> 67, of which waited for: 21 -> 30; matrix products, arithmetic and copies ran while one was open for 30% -> 30% of each run, Pallas kernels for 10% -> 5%
where the time goes in v2:
time: 510 us; the launch traced here: 503 us
  waiting for transfers between devices  131 us (26%)
  starting transfers between devices  117 us (23%)
  local copies, waits for them, and re-layouts  87.5 us (17%)
  Pallas kernels  58.7 us (12%)
  matrix products  52.8 us (10%)
  other arithmetic  52.4 us (10%)
    ppermute x51, starting transfers between devices, move(): return lax.ppermute(value, BOTH, pairs)  88.1 us
    ppermute x51, waiting for transfers between devices, move(): return lax.ppermute(value, BOTH, pairs)  75.4 us
    ppermute x12, waiting for transfers between devices, move_mixed(): return lax.ppermute(value, BOTH, pairs)  45.8 us
    dot_general x8, matrix products, dot(): return jnp.dot(left, right, preferred_element_type=F32)  27 us
    unnamed x212, local copies, waits for them, and re-layouts  23.8 us
    pallas_call x2, Pallas kernels, attention_backward(): pl.pallas_call(functools.partial(attention_backward_body, mode), out_shap...  22.7 us
    pallas_call x2, Pallas kernels, gather_weights(): pl.pallas_call(functools.partial(assemble_body, plan), out_shape=tuple((j...  19.8 us
    ppermute x12, starting transfers between devices, move_mixed(): return lax.ppermute(value, BOTH, pairs)  16.4 us
  transfers between devices with their start and end apart: 67, of which 30 were waited for; matrix products, arithmetic and copies ran while one was open for 30% of the time, Pallas kernels for 5%

profile of v2, /device:TPU:0, one launch (start us, length us, event | category | flops | bytes accessed | tf_op | source)
XLA Modules:
  0.0 502.5 jit_solution(3326566216209259803)
XLA Ops:
  0.7 5.1 %collective-permute-start.3 = (bf16[128,768]{1,0:T(8,128)(2,1)}, bf16[128,768]{1,0:T(8,128)(2,1)S(1)}, u32[]{:S(2)}, u32[]{:S(2)}) collective-permute-start(bf16[128,768]{1,0:T(8,128)(2,1)} %param.16), channel_id=1, source_target_pairs={{0,2},{1,3},{2,4},{3,5},{4,6},{5,7},{8,10},{9,11},{10,12},{11,13},... | collective-permute-start | bytes 589832 | tf_op jit(solution)/shard_map/ppermute | solution.py:93
  5.8 4.5 collective-permute-start.4
  14.8 3.8 collective-permute-start
  28.7 2.0 collective-permute-start.7
  31.6 12.4 %collective-permute-start.6 = (bf16[48,3072]{1,0:T(8,128)(2,1)S(1)}, bf16[48,3072]{1,0:T(8,128)(2,1)S(1)}, u32[]{:S(2)}, u32[]{:S(2)}) collective-permute-start(bf16[48,3072]{1,0:T(8,128)(2,1)S(1)} %constant_dynamic-slice_fusion.72), channel_id=1, source_target_pairs={{0,6},{1,7},{2,0},{3,1},{4,2},{5,3},{6,4},{7,5},{8,14},{9,15},{10,... | collective-permute-start | bytes 884744 | tf_op jit(solution)/shard_map/ppermute | solution.py:64
  44.9 3.3 collective-permute-start.13
  48.2 2.0 collective-permute-done.7
  50.2 7.8 %collective-permute-start.15 = (bf16[48,3072]{1,0:T(8,128)(2,1)S(1)}, bf16[48,3072]{1,0:T(8,128)(2,1)S(1)}, u32[]{:S(2)}, u32[]{:S(2)}) collective-permute-start(bf16[48,3072]{1,0:T(8,128)(2,1)S(1)} %constant_dynamic-slice_fusion.71), channel_id=1, source_target_pairs={{0,2},{1,3},{2,4},{3,5},{4,6},{5,7},{6,0},{7,1},{8,10},{9,11},{10,... | collective-permute-start | bytes 884744 | tf_op jit(solution)/shard_map/ppermute | solution.py:64
  61.9 13.6 %collective-permute-done.14 = bf16[48,3072]{1,0:T(8,128)(2,1)S(1)} collective-permute-done((bf16[48,3072]{1,0:T(8,128)(2,1)S(1)}, bf16[48,3072]{1,0:T(8,128)(2,1)S(1)}, u32[]{:S(2)}, u32[]{:S(2)}) %collective-permute-start.14) | collective-permute-done | bytes 294944 | tf_op jit(solution)/shard_map/ppermute | solution.py:64
  78.5 6.2 %collective-permute-done.5 = bf16[704,768]{1,0:T(8,128)(2,1)S(1)} collective-permute-done((bf16[704,768]{1,0:T(8,128)(2,1)S(1)}, bf16[704,768]{1,0:T(8,128)(2,1)S(1)}, u32[]{:S(2)}, u32[]{:S(2)}) %collective-permute-start.5) | collective-permute-done | bytes 1081376 | tf_op jit(solution)/shard_map/ppermute | solution.py:64
  96.5 10.8 %collective-permute-start.11 = (bf16[2,4,48,3072]{3,2,1,0:T(8,128)(2,1)S(1)}, bf16[2,4,48,3072]{3,2,1,0:T(8,128)(2,1)}, u32[]{:S(2)}, u32[]{:S(2)}) collective-permute-start(bf16[2,4,48,3072]{3,2,1,0:T(8,128)(2,1)S(1)} %pad_maximum_fusion.1.refs_0_), channel_id=1, source_target_pairs={{0,8},{1,9},{2,10},{3,11},{4,12},{5,13},{6,14},{7,15},{8,0},{9,1},... | collective-permute-start | bytes 7077896 | tf_op jit(solution)/shard_map/ppermute | solution.py:64
  107.4 3.2 pad_maximum_fusion.2.refs_0_
  112.1 19.0 %collective-permute-done.10.refs_1_ = bf16[2,4,48,3072]{3,2,1,0:T(8,128)(2,1)} collective-permute-done((bf16[2,4,48,3072]{3,2,1,0:T(8,128)(2,1)S(1)}, bf16[2,4,48,3072]{3,2,1,0:T(8,128)(2,1)}, u32[]{:S(2)}, u32[]{:S(2)}) %collective-permute-start.10) | collective-permute-done | bytes 2359328 | tf_op jit(solution)/shard_map/ppermute | solution.py:77
  132.4 1.7 reshape.370
  140.4 2.0 slice_reduce_fusion
  162.6 10.1 %assemble.2 = (bf16[768,2304]{1,0:T(8,128)(2,1)}, bf16[768,768]{1,0:T(8,128)(2,1)}, bf16[768,768]{1,0:T(8,128)(2,1)}, bf16[768,1536]{1,0:T(8,128)(2,1)}, bf16[768,768]{1,0:T(8,128)(2,1)}) custom-call(s32[4]{0:T(128)} %pad_add_fusion.coords_ref, bf16[2,4,48,3072]{3,2,1,0:T(8,128)(2,1)} %copy-done, bf16[2,4,48,3072]{3,2,1,0:T(8,128)(2,1)} %collective-permute-done.10.refs_1_, ...), custom_call_target="tpu_custom_call" | custom-call | bytes 589824 | tf_op jit(solution)/shard_map/assemble/pallas_call | solution.py:280
  172.7 2.3 fusion.35.q_ref
  175.0 5.1 %add_convert_fusion.kv_ref = bf16[768,1536]{1,0:T(8,128)(2,1)} fusion(bf16[768,768]{1,0:T(8,128)(2,1)S(1)} %copy-done.34, f32[1536]{0:T(1024)S(1)} %copy-done.81, bf16[768,2304]{1,0:T(8,128)(2,1)} %get-tuple-element.46), kind=kOutput, calls=%fused_computation | convolution fusion | flops 1814298624 | bytes 5904384 | tf_op jit(solution)/shard_map/dot_general | solution.py:23
  180.1 8.7 %self_forward.1 = bf16[128,768]{1,0:T(8,128)(2,1)} custom-call(s32[1]{0:T(128)} %bitcast.info_ref, s32[1,4]{1,0:T(1,128)} %lengths_ref.7, s32[1,4]{1,0:T(1,128)} %counts_ref.7, s32[1,768]{1,0:T(1,128)} %bitcast.372, bf16[128,768]{1,0:T(8,128)(2,1)} %fusion.35.q_ref, bf16[768,1536]{1,0:T(8,128)(2,1)} %add_convert_fusion.kv_ref), custom_call_target="tpu_custom_call" | custom-call | bytes 98304 | tf_op jit(solution)/shard_map/self_forward/pallas_call | solution.py:193
  188.8 1.6 constant_dynamic-update-slice_fusion.13
  190.4 1.9 fusion.162
  194.5 2.5 fusion.kv_ref
  197.1 7.5 %cross_forward.1 = bf16[128,768]{1,0:T(8,128)(2,1)} custom-call(s32[1]{0:T(128)} %bitcast.info_ref, s32[1,4]{1,0:T(1,128)} %lengths_ref.7, s32[1,4]{1,0:T(1,128)} %counts_ref.7, s32[1,512]{1,0:T(1,128)} %add.595.pos_ref, bf16[128,768]{1,0:T(8,128)(2,1)} %fusion.36.q_ref, bf16[512,1536]{1,0:T(8,128)(2,1)} %fusion.kv_ref), custom_call_target="tpu_custom_call" | custom-call | bytes 98304 | tf_op jit(solution)/shard_map/cross_forward/pallas_call | solution.py:193
  204.6 1.6 constant_dynamic-update-slice_fusion.11
  208.6 9.7 %assemble.3 = (bf16[768,3072]{1,0:T(8,128)(2,1)}, bf16[3072,768]{1,0:T(8,128)(2,1)}) custom-call(s32[4]{0:T(128)} %pad_add_fusion.coords_ref, bf16[2,4,48,3072]{3,2,1,0:T(8,128)(2,1)} %pad_maximum_fusion.2.refs_0_, bf16[2,4,48,3072]{3,2,1,0:T(8,128)(2,1)} %collective-permute-done.17.refs_1_, bf16[2,4,48,3072]{3,2,1,0:T(8,128)(2,1)} %collective-permute-done.18.refs_2_, ...), custom_call_target="tpu_custom_call" | custom-call | bytes 589824 | tf_op jit(solution)/shard_map/assemble/pallas_call | solution.py:280
  218.3 8.7 %multiply_convert_fusion = (bf16[128,3072]{1,0:T(8,128)(2,1)}, f32[128,3072]{1,0:T(8,128)}, f32[128,3072]{1,0:T(8,128)}) fusion(f32[3072]{0:T(1024)S(1)} %copy-done.67, bf16[128,768]{1,0:T(8,128)(2,1)S(1)} %get-tuple-element.114, bf16[768,3072]{1,0:T(8,128)(2,1)} %get-tuple-element.51), kind=kOutput, calls=%fused_computation.40 | convolution fusion | flops 629932032 | bytes 8859648 | tf_op jit(solution)/shard_map/dot_general | solution.py:23
  228.4 5.0 add_convert_fusion.5
  233.4 2.4 convolution_convert_fusion
  241.8 4.1 fusion.34
  246.0 10.0 %collective-permute-done.24 = bf16[4,2,48,1536]{3,2,0,1:T(8,128)(2,1)} collective-permute-done((bf16[4,2,48,1536]{3,2,0,1:T(8,128)(2,1)}, bf16[4,2,48,1536]{3,2,0,1:T(8,128)(2,1)}, u32[]{:S(2)}, u32[]{:S(2)}) %collective-permute-start.24) | collective-permute-done | bytes 1179680 | tf_op jit(solution)/shard_map/ppermute | solution.py:77
  258.7 2.3 fusion.145
  261.8 1.7 bitcast_select_fusion
  263.6 1.8 multiply_reduce_fusion.2
  268.2 10.4 %cross_backward.1 = (bf16[128,768]{1,0:T(8,128)(2,1)}, bf16[512,1536]{1,0:T(8,128)(2,1)}) custom-call(s32[1]{0:T(128)} %bitcast.info_ref, s32[1,4]{1,0:T(1,128)} %lengths_ref.7, s32[1,4]{1,0:T(1,128)} %counts_ref.7, s32[1,512]{1,0:T(1,128)} %add.595.pos_ref, bf16[128,768]{1,0:T(8,128)(2,1)} %fusion.36.q_ref, bf16[512,1536]{1,0:T(8,128)(2,1)} %fusion.kv_ref, ...), custom_call_target="tpu_custom_call" | custom-call | bytes 98304 | tf_op jit(solution)/shard_map/cross_backward/pallas_call | solution.py:206
  278.6 3.7 convolution_convert_fusion.2
  292.2 2.5 slice.446
  294.9 2.1 collective-permute-done.33
  298.1 11.5 %collective-permute-start.34 = (bf16[64,768]{1,0:T(8,128)(2,1)S(1)}, bf16[64,768]{1,0:T(8,128)(2,1)S(1)}, u32[]{:S(2)}, u32[]{:S(2)}) collective-permute-start(bf16[64,768]{1,0:T(8,128)(2,1)S(1)} %get-tuple-element.240), channel_id=1, source_target_pairs={{0,2},{1,3},{2,4},{3,5},{4,6},{5,7},{6,0},{7,1},{8,10},{9,11},{10,... | collective-permute-start | bytes 294920 | tf_op jit(solution)/shard_map/ppermute | solution.py:64
  311.9 2.9 collective-permute-done.36
  327.0 3.1 collective-permute-done.27
  331.0 5.4 %collective-permute-done.26 = bf16[4,48,1536]{2,1,0:T(8,128)(2,1)S(1)} collective-permute-done((bf16[4,48,1536]{2,1,0:T(8,128)(2,1)S(1)}, bf16[4,48,1536]{2,1,0:T(8,128)(2,1)S(1)}, u32[]{:S(2)}, u32[]{:S(2)}) %collective-permute-start.26) | collective-permute-done | bytes 589856 | tf_op jit(solution)/shard_map/ppermute | solution.py:77
  344.2 12.3 %self_backward.1 = (bf16[128,768]{1,0:T(8,128)(2,1)}, bf16[768,1536]{1,0:T(8,128)(2,1)}) custom-call(s32[1]{0:T(128)} %bitcast.info_ref, s32[1,4]{1,0:T(1,128)} %lengths_ref.7, s32[1,4]{1,0:T(1,128)} %counts_ref.7, s32[1,768]{1,0:T(1,128)} %bitcast.373, bf16[128,768]{1,0:T(8,128)(2,1)} %fusion.35.q_ref, bf16[768,1536]{1,0:T(8,128)(2,1)} %add_convert_fusion.kv_ref, ...), custom_call_target="tpu_custom_call" | custom-call | bytes 98304 | tf_op jit(solution)/shard_map/self_backward/pallas_call | solution.py:206
  358.1 1.9 collective-permute-start.56
  360.4 3.5 collective-permute-start.53
  364.3 1.8 fusion.146
  370.3 2.6 collective-permute-done.53
  374.4 4.3 collective-permute-done.52
  381.2 4.8 collective-permute-done.57
  387.6 6.2 %collective-permute-done.54 = bf16[48,1536]{1,0:T(8,128)(2,1)S(1)} collective-permute-done((bf16[48,1536]{1,0:T(8,128)(2,1)S(1)}, bf16[48,1536]{1,0:T(8,128)(2,1)S(1)}, u32[]{:S(2)}, u32[]{:S(2)}) %collective-permute-start.54) | collective-permute-done | bytes 147488 | tf_op jit(solution)/shard_map/ppermute | solution.py:64
  412.0 2.0 fusion.5
  421.1 2.0 collective-permute-done.62
  425.5 2.1 slice.557
  428.4 2.1 collective-permute-start.66
  433.3 2.8 collective-permute-start.46
  437.2 1.6 collective-permute-done.65
  443.5 6.3 %collective-permute-done.47 = bf16[48,1536]{1,0:T(8,128)(2,1)} collective-permute-done((bf16[48,1536]{1,0:T(8,128)(2,1)}, bf16[48,1536]{1,0:T(8,128)(2,1)}, u32[]{:S(2)}, u32[]{:S(2)}) %collective-permute-start.47) | collective-permute-done | bytes 147488 | tf_op jit(solution)/shard_map/ppermute | solution.py:64
  456.5 2.1 collective-permute-done.49
  458.7 4.6 collective-permute-done.31
  463.3 5.6 %collective-permute-done.32 = bf16[128,768]{1,0:T(8,128)(2,1)S(1)} collective-permute-done((bf16[128,768]{1,0:T(8,128)(2,1)S(1)}, bf16[128,768]{1,0:T(8,128)(2,1)S(1)}, u32[]{:S(2)}, u32[]{:S(2)}) %collective-permute-start.32) | collective-permute-done | bytes 196640 | tf_op jit(solution)/shard_map/ppermute | solution.py:93
  471.1 8.4 %collective-permute-done.38 = bf16[4,48,1536]{2,1,0:T(8,128)(2,1)S(1)} collective-permute-done((bf16[4,48,1536]{2,1,0:T(8,128)(2,1)S(1)}, bf16[4,48,1536]{2,1,0:T(8,128)(2,1)S(1)}, u32[]{:S(2)}, u32[]{:S(2)}) %collective-permute-start.38) | collective-permute-done | bytes 589856 | tf_op jit(solution)/shard_map/ppermute | solution.py:77
  479.8 3.8 collective-permute-start.41
  483.6 4.8 collective-permute-done.39
  488.4 5.0 collective-permute-done.40
  494.9 3.8 collective-permute-done.42
  (560 shorter events, 179.1 us)
Async XLA Ops:
  0.7 43.6 %collective-permute-start.3 = (bf16[128,768]{1,0:T(8,128)(2,1)}, bf16[128,768]{1,0:T(8,128)(2,1)S(1)}, u32[]{:S(2)}, u32[]{:S(2)}) collective-permute-start(bf16[128,768]{1,0:T(8,128)(2,1)} %param.16), channel_id=1, source_target_pairs={{0,2},{1,3},{2,4},{3,5},{4,6},{5,7},{8,10},{9,11},{10,12},{11,13},... | collective-permute-start | bytes 589832 | tf_op jit(solution)/shard_map/ppermute | solution.py:93
  5.8 39.1 %collective-permute-start.4 = (bf16[128,768]{1,0:T(8,128)(2,1)}, bf16[128,768]{1,0:T(8,128)(2,1)S(1)}, u32[]{:S(2)}, u32[]{:S(2)}) collective-permute-start(bf16[128,768]{1,0:T(8,128)(2,1)} %param.16), channel_id=1, source_target_pairs={{0,4},{1,5},{2,6},{3,7},{8,12},{9,13},{10,14},{11,15},{16,20},{17,... | collective-permute-start | bytes 589832 | tf_op jit(solution)/shard_map/ppermute | solution.py:93
  14.8 29.3 %collective-permute-start.2 = (bf16[80,768]{1,0:T(8,128)(2,1)}, bf16[80,768]{1,0:T(8,128)(2,1)S(1)}, u32[]{:S(2)}, u32[]{:S(2)}) collective-permute-start(bf16[80,768]{1,0:T(8,128)(2,1)} %get-tuple-element.276), channel_id=1, source_target_pairs={{0,2},{1,3},{2,4},{3,5},{4,6},{5,7},{6,0},{7,1},{8,10},{9,11},{10,... | collective-permute-start | bytes 368648 | tf_op jit(solution)/shard_map/ppermute | solution.py:64
  14.8 16.8 %collective-permute-start.1 = (bf16[80,768]{1,0:T(8,128)(2,1)}, bf16[80,768]{1,0:T(8,128)(2,1)S(1)}, u32[]{:S(2)}, u32[]{:S(2)}) collective-permute-start(bf16[80,768]{1,0:T(8,128)(2,1)} %get-tuple-element.276), channel_id=1, source_target_pairs={{0,4},{1,5},{2,6},{3,7},{4,0},{5,1},{6,2},{7,3},{8,12},{9,13},{10,... | collective-permute-start | bytes 368648 | tf_op jit(solution)/shard_map/ppermute | solution.py:64
  14.8 13.9 %collective-permute-start = (bf16[80,768]{1,0:T(8,128)(2,1)}, bf16[80,768]{1,0:T(8,128)(2,1)}, u32[]{:S(2)}, u32[]{:S(2)}) collective-permute-start(bf16[80,768]{1,0:T(8,128)(2,1)} %get-tuple-element.276), channel_id=1, source_target_pairs={{0,6},{1,7},{2,0},{3,1},{4,2},{5,3},{6,4},{7,5},{8,14},{9,15},{10,... | collective-permute-start | bytes 368648 | tf_op jit(solution)/shard_map/ppermute | solution.py:64
  28.7 21.5 %collective-permute-start.7 = (bf16[48,3072]{1,0:T(8,128)(2,1)S(1)}, bf16[48,3072]{1,0:T(8,128)(2,1)S(1)}, u32[]{:S(2)}, u32[]{:S(2)}) collective-permute-start(bf16[48,3072]{1,0:T(8,128)(2,1)S(1)} %constant_dynamic-slice_fusion.72), channel_id=1, source_target_pairs={{0,4},{1,5},{2,6},{3,7},{4,0},{5,1},{6,2},{7,3},{8,12},{9,13},{10,... | collective-permute-start | bytes 884744 | tf_op jit(solution)/shard_map/ppermute | solution.py:64
  31.6 26.4 %collective-permute-start.6 = (bf16[48,3072]{1,0:T(8,128)(2,1)S(1)}, bf16[48,3072]{1,0:T(8,128)(2,1)S(1)}, u32[]{:S(2)}, u32[]{:S(2)}) collective-permute-start(bf16[48,3072]{1,0:T(8,128)(2,1)S(1)} %constant_dynamic-slice_fusion.72), channel_id=1, source_target_pairs={{0,6},{1,7},{2,0},{3,1},{4,2},{5,3},{6,4},{7,5},{8,14},{9,15},{10,... | collective-permute-start | bytes 884744 | tf_op jit(solution)/shard_map/ppermute | solution.py:64
  44.1 15.4 %collective-permute-start.8 = (bf16[48,3072]{1,0:T(8,128)(2,1)S(1)}, bf16[48,3072]{1,0:T(8,128)(2,1)S(1)}, u32[]{:S(2)}, u32[]{:S(2)}) collective-permute-start(bf16[48,3072]{1,0:T(8,128)(2,1)S(1)} %constant_dynamic-slice_fusion.72), channel_id=1, source_target_pairs={{0,2},{1,3},{2,4},{3,5},{4,6},{5,7},{6,0},{7,1},{8,10},{9,11},{10,... | collective-permute-start | bytes 884744 | tf_op jit(solution)/shard_map/ppermute | solution.py:64
  44.2 31.2 %collective-permute-start.14 = (bf16[48,3072]{1,0:T(8,128)(2,1)S(1)}, bf16[48,3072]{1,0:T(8,128)(2,1)S(1)}, u32[]{:S(2)}, u32[]{:S(2)}) collective-permute-start(bf16[48,3072]{1,0:T(8,128)(2,1)S(1)} %constant_dynamic-slice_fusion.71), channel_id=1, source_target_pairs={{0,4},{1,5},{2,6},{3,7},{4,0},{5,1},{6,2},{7,3},{8,12},{9,13},{10,... | collective-permute-start | bytes 884744 | tf_op jit(solution)/shard_map/ppermute | solution.py:64
  44.9 30.6 %collective-permute-start.13 = (bf16[48,3072]{1,0:T(8,128)(2,1)S(1)}, bf16[48,3072]{1,0:T(8,128)(2,1)S(1)}, u32[]{:S(2)}, u32[]{:S(2)}) collective-permute-start(bf16[48,3072]{1,0:T(8,128)(2,1)S(1)} %constant_dynamic-slice_fusion.71), channel_id=1, source_target_pairs={{0,6},{1,7},{2,0},{3,1},{4,2},{5,3},{6,4},{7,5},{8,14},{9,15},{10,... | collective-permute-start | bytes 884744 | tf_op jit(solution)/shard_map/ppermute | solution.py:64
  50.2 25.3 %collective-permute-start.15 = (bf16[48,3072]{1,0:T(8,128)(2,1)S(1)}, bf16[48,3072]{1,0:T(8,128)(2,1)S(1)}, u32[]{:S(2)}, u32[]{:S(2)}) collective-permute-start(bf16[48,3072]{1,0:T(8,128)(2,1)S(1)} %constant_dynamic-slice_fusion.71), channel_id=1, source_target_pairs={{0,2},{1,3},{2,4},{3,5},{4,6},{5,7},{6,0},{7,1},{8,10},{9,11},{10,... | collective-permute-start | bytes 884744 | tf_op jit(solution)/shard_map/ppermute | solution.py:64
  58.0 26.7 %collective-permute-start.5 = (bf16[704,768]{1,0:T(8,128)(2,1)S(1)}, bf16[704,768]{1,0:T(8,128)(2,1)S(1)}, u32[]{:S(2)}, u32[]{:S(2)}) collective-permute-start(bf16[704,768]{1,0:T(8,128)(2,1)S(1)} %constant_dynamic-update-slice_fusion.2), channel_id=1, source_target_pairs={{0,1},{1,0},{2,3},{3,2},{4,5},{5,4},{6,7},{7,6},{8,9},{9,8},{10,11... | collective-permute-start | bytes 3244040 | tf_op jit(solution)/shard_map/ppermute | solution.py:64
  59.7 26.0 %collective-permute-start.9 = (bf16[4,48,3072]{2,1,0:T(8,128)(2,1)S(1)}, bf16[4,48,3072]{2,1,0:T(8,128)(2,1)S(1)}, u32[]{:S(2)}, u32[]{:S(2)}) collective-permute-start(bf16[4,48,3072]{2,1,0:T(8,128)(2,1)S(1)} %get-tuple-element.155), channel_id=1, source_target_pairs={{0,16},{1,17},{2,18},{3,19},{4,20},{5,21},{6,22},{7,23},{8,9},{9,8... | collective-permute-start | bytes 3538952 | tf_op jit(solution)/shard_map/ppermute | solution.py:77
  77.1 30.3 %collective-permute-start.16 = (bf16[4,48,3072]{2,1,0:T(8,128)(2,1)}, bf16[4,48,3072]{2,1,0:T(8,128)(2,1)}, u32[]{:S(2)}, u32[]{:S(2)}) collective-permute-start(bf16[4,48,3072]{2,1,0:T(8,128)(2,1)} %get-tuple-element.153), channel_id=1, source_target_pairs={{0,16},{1,17},{2,18},{3,19},{4,20},{5,21},{6,22},{7,23},{8,9},{9,8... | collective-permute-start | bytes 3538952 | tf_op jit(solution)/shard_map/ppermute | solution.py:77
  85.9 45.2 %collective-permute-start.10 = (bf16[2,4,48,3072]{3,2,1,0:T(8,128)(2,1)S(1)}, bf16[2,4,48,3072]{3,2,1,0:T(8,128)(2,1)}, u32[]{:S(2)}, u32[]{:S(2)}) collective-permute-start(bf16[2,4,48,3072]{3,2,1,0:T(8,128)(2,1)S(1)} %pad_maximum_fusion.1.refs_0_), channel_id=1, source_target_pairs={{0,1},{1,0},{2,3},{3,2},{4,5},{5,4},{6,7},{7,6},{8,24},{9,25},{10,... | collective-permute-start | bytes 7077896 | tf_op jit(solution)/shard_map/ppermute | solution.py:77
  96.5 65.0 %collective-permute-start.11 = (bf16[2,4,48,3072]{3,2,1,0:T(8,128)(2,1)S(1)}, bf16[2,4,48,3072]{3,2,1,0:T(8,128)(2,1)}, u32[]{:S(2)}, u32[]{:S(2)}) collective-permute-start(bf16[2,4,48,3072]{3,2,1,0:T(8,128)(2,1)S(1)} %pad_maximum_fusion.1.refs_0_), channel_id=1, source_target_pairs={{0,8},{1,9},{2,10},{3,11},{4,12},{5,13},{6,14},{7,15},{8,0},{9,1},... | collective-permute-start | bytes 7077896 | tf_op jit(solution)/shard_map/ppermute | solution.py:64
  110.6 50.9 %collective-permute-start.17 = (bf16[2,4,48,3072]{3,2,1,0:T(8,128)(2,1)}, bf16[2,4,48,3072]{3,2,1,0:T(8,128)(2,1)}, u32[]{:S(2)}, u32[]{:S(2)}) collective-permute-start(bf16[2,4,48,3072]{3,2,1,0:T(8,128)(2,1)} %pad_maximum_fusion.2.refs_0_), channel_id=1, source_target_pairs={{0,1},{1,0},{2,3},{3,2},{4,5},{5,4},{6,7},{7,6},{8,24},{9,25},{10,... | collective-permute-start | bytes 7077896 | tf_op jit(solution)/shard_map/ppermute | solution.py:77
  131.1 31.5 %collective-permute-start.12 = (bf16[2,4,48,3072]{3,2,1,0:T(8,128)(2,1)}, bf16[2,4,48,3072]{3,2,1,0:T(8,128)(2,1)}, u32[]{:S(2)}, u32[]{:S(2)}) collective-permute-start(bf16[2,4,48,3072]{3,2,1,0:T(8,128)(2,1)} %collective-permute-done.10.refs_1_), channel_id=1, source_target_pairs={{0,8},{1,9},{2,10},{3,11},{4,12},{5,13},{6,14},{7,15},{8,0},{9,1},... | collective-permute-start | bytes 7077896 | tf_op jit(solution)/shard_map/ppermute | solution.py:64
  161.0 47.6 %collective-permute-start.18 = (bf16[2,4,48,3072]{3,2,1,0:T(8,128)(2,1)}, bf16[2,4,48,3072]{3,2,1,0:T(8,128)(2,1)}, u32[]{:S(2)}, u32[]{:S(2)}) collective-permute-start(bf16[2,4,48,3072]{3,2,1,0:T(8,128)(2,1)} %pad_maximum_fusion.2.refs_0_), channel_id=1, source_target_pairs={{0,8},{1,9},{2,10},{3,11},{4,12},{5,13},{6,14},{7,15},{8,0},{9,1},... | collective-permute-start | bytes 7077896 | tf_op jit(solution)/shard_map/ppermute | solution.py:64
  161.5 47.1 %collective-permute-start.19 = (bf16[2,4,48,3072]{3,2,1,0:T(8,128)(2,1)}, bf16[2,4,48,3072]{3,2,1,0:T(8,128)(2,1)}, u32[]{:S(2)}, u32[]{:S(2)}) collective-permute-start(bf16[2,4,48,3072]{3,2,1,0:T(8,128)(2,1)} %collective-permute-done.17.refs_1_), channel_id=1, source_target_pairs={{0,8},{1,9},{2,10},{3,11},{4,12},{5,13},{6,14},{7,15},{8,0},{9,1},... | collective-permute-start | bytes 7077896 | tf_op jit(solution)/shard_map/ppermute | solution.py:64
  227.0 6.4 %collective-permute-start.21 = (bf16[128,3072]{1,0:T(8,128)(2,1)}, bf16[128,3072]{1,0:T(8,128)(2,1)}, u32[]{:S(2)}, u32[]{:S(2)}) collective-permute-start(bf16[128,3072]{1,0:T(8,128)(2,1)} %get-tuple-element.117), channel_id=1, source_target_pairs={{0,8},{1,9},{2,10},{3,11},{4,12},{5,13},{6,14},{7,15},{8,0},{9,1},... | collective-permute-start | bytes 2359304 | tf_op jit(solution)/shard_map/ppermute | solution.py:64
  227.6 5.8 %collective-permute-start.22 = (bf16[128,384]{1,0:T(8,128)(2,1)S(1)}, bf16[128,384]{1,0:T(8,128)(2,1)}, u32[]{:S(2)}, u32[]{:S(2)}) collective-permute-start(bf16[128,384]{1,0:T(8,128)(2,1)S(1)} %get-tuple-element.273), channel_id=1, source_target_pairs={{0,8},{1,9},{2,10},{3,11},{4,12},{5,13},{6,14},{7,15},{8,0},{9,1},... | collective-permute-start | bytes 294920 | tf_op jit(solution)/shard_map/ppermute | solution.py:64
  227.9 30.7 %collective-permute-start.20 = (bf16[1920,768]{1,0:T(8,128)(2,1)}, bf16[1920,768]{1,0:T(8,128)(2,1)}, u32[]{:S(2)}, u32[]{:S(2)}) collective-permute-start(bf16[1920,768]{1,0:T(8,128)(2,1)} %get-tuple-element.113), channel_id=1, source_target_pairs={{0,8},{1,9},{2,10},{3,11},{4,12},{5,13},{6,14},{7,15},{8,0},{9,1},... | collective-permute-start | bytes 8847368 | tf_op jit(solution)/shard_map/ppermute | solution.py:64
  239.5 16.5 %collective-permute-start.24 = (bf16[4,2,48,1536]{3,2,0,1:T(8,128)(2,1)}, bf16[4,2,48,1536]{3,2,0,1:T(8,128)(2,1)}, u32[]{:S(2)}, u32[]{:S(2)}) collective-permute-start(bf16[4,2,48,1536]{3,2,0,1:T(8,128)(2,1)} %pad_maximum_fusion.14), channel_id=1, source_target_pairs={{0,16},{1,17},{2,18},{3,19},{4,20},{5,21},{6,22},{7,23},{8,9},{9,8... | collective-permute-start | bytes 3538952 | tf_op jit(solution)/shard_map/ppermute | solution.py:77
  245.9 15.1 %collective-permute-start.23 = (bf16[128,1536]{1,0:T(8,128)(2,1)S(1)}, bf16[128,1536]{1,0:T(8,128)(2,1)S(1)}, u32[]{:S(2)}, u32[]{:S(2)}) collective-permute-start(bf16[128,1536]{1,0:T(8,128)(2,1)S(1)} %get-tuple-element.169), channel_id=1, source_target_pairs={{0,8},{1,9},{2,10},{3,11},{4,12},{5,13},{6,14},{7,15},{8,0},{9,1},... | collective-permute-start | bytes 1179656 | tf_op jit(solution)/shard_map/ppermute | solution.py:64
  284.7 12.3 %collective-permute-start.33 = (bf16[4,64,768]{2,1,0:T(8,128)(2,1)}, bf16[4,64,768]{2,1,0:T(8,128)(2,1)}, u32[]{:S(2)}, u32[]{:S(2)}) collective-permute-start(bf16[4,64,768]{2,1,0:T(8,128)(2,1)} %bitcast.101), channel_id=1, source_target_pairs={{0,1},{1,0},{2,3},{3,2},{4,5},{5,4},{6,7},{7,6},{8,9},{9,8},{10,11... | collective-permute-start | bytes 1179656 | tf_op jit(solution)/shard_map/ppermute | solution.py:64
  286.2 30.3 %collective-permute-start.25 = (bf16[4,2,48,1536]{3,2,1,0:T(8,128)(2,1)}, bf16[4,2,48,1536]{3,2,1,0:T(8,128)(2,1)}, u32[]{:S(2)}, u32[]{:S(2)}) collective-permute-start(bf16[4,2,48,1536]{3,2,1,0:T(8,128)(2,1)} %get-tuple-element.58), channel_id=1, source_target_pairs={{0,16},{1,17},{2,18},{3,19},{4,20},{5,21},{6,22},{7,23},{8,9},{9,8... | collective-permute-start | bytes 3538952 | tf_op jit(solution)/shard_map/ppermute | solution.py:77
  298.1 13.8 %collective-permute-start.34 = (bf16[64,768]{1,0:T(8,128)(2,1)S(1)}, bf16[64,768]{1,0:T(8,128)(2,1)S(1)}, u32[]{:S(2)}, u32[]{:S(2)}) collective-permute-start(bf16[64,768]{1,0:T(8,128)(2,1)S(1)} %get-tuple-element.240), channel_id=1, source_target_pairs={{0,2},{1,3},{2,4},{3,5},{4,6},{5,7},{6,0},{7,1},{8,10},{9,11},{10,... | collective-permute-start | bytes 294920 | tf_op jit(solution)/shard_map/ppermute | solution.py:64
  309.7 5.1 %collective-permute-start.36 = (bf16[64,768]{1,0:T(8,128)(2,1)S(1)}, bf16[64,768]{1,0:T(8,128)(2,1)S(1)}, u32[]{:S(2)}, u32[]{:S(2)}) collective-permute-start(bf16[64,768]{1,0:T(8,128)(2,1)S(1)} %get-tuple-element.241), channel_id=1, source_target_pairs={{0,6},{1,7},{2,0},{3,1},{4,2},{5,3},{6,4},{7,5},{8,14},{9,15},{10,... | collective-permute-start | bytes 294920 | tf_op jit(solution)/shard_map/ppermute | solution.py:64
  310.1 5.7 %collective-permute-start.35 = (bf16[64,768]{1,0:T(8,128)(2,1)S(1)}, bf16[64,768]{1,0:T(8,128)(2,1)S(1)}, u32[]{:S(2)}, u32[]{:S(2)}) collective-permute-start(bf16[64,768]{1,0:T(8,128)(2,1)S(1)} %get-tuple-element.242), channel_id=1, source_target_pairs={{0,4},{1,5},{2,6},{3,7},{4,0},{5,1},{6,2},{7,3},{8,12},{9,13},{10,... | collective-permute-start | bytes 294920 | tf_op jit(solution)/shard_map/ppermute | solution.py:64
  320.1 9.9 %collective-permute-start.27 = (bf16[4,48,1536]{2,1,0:T(8,128)(2,1)S(1)}, bf16[4,48,1536]{2,1,0:T(8,128)(2,1)S(1)}, u32[]{:S(2)}, u32[]{:S(2)}) collective-permute-start(bf16[4,48,1536]{2,1,0:T(8,128)(2,1)S(1)} %get-tuple-element.65), channel_id=1, source_target_pairs={{0,1},{1,0},{2,3},{3,2},{4,5},{5,4},{6,7},{7,6},{8,24},{9,25},{10,... | collective-permute-start | bytes 1769480 | tf_op jit(solution)/shard_map/ppermute | solution.py:77
  325.0 11.4 %collective-permute-start.26 = (bf16[4,48,1536]{2,1,0:T(8,128)(2,1)S(1)}, bf16[4,48,1536]{2,1,0:T(8,128)(2,1)S(1)}, u32[]{:S(2)}, u32[]{:S(2)}) collective-permute-start(bf16[4,48,1536]{2,1,0:T(8,128)(2,1)S(1)} %copy-done.45), channel_id=1, source_target_pairs={{0,1},{1,0},{2,3},{3,2},{4,5},{5,4},{6,7},{7,6},{8,24},{9,25},{10,... | collective-permute-start | bytes 1769480 | tf_op jit(solution)/shard_map/ppermute | solution.py:77
  325.6 10.9 %collective-permute-start.28 = (bf16[1280,384]{1,0:T(8,128)(2,1)S(1)}, bf16[1280,384]{1,0:T(8,128)(2,1)S(1)}, u32[]{:S(2)}, u32[]{:S(2)}) collective-permute-start(bf16[1280,384]{1,0:T(8,128)(2,1)S(1)} %pad_maximum_fusion.23), channel_id=1, source_target_pairs={{0,8},{1,9},{2,10},{3,11},{4,12},{5,13},{6,14},{7,15},{8,0},{9,1},... | collective-permute-start | bytes 2949128 | tf_op jit(solution)/shard_map/ppermute | solution.py:64
  358.1 23.1 %collective-permute-start.56 = (bf16[48,1536]{1,0:T(8,128)(2,1)S(1)}, bf16[48,1536]{1,0:T(8,128)(2,1)S(1)}, u32[]{:S(2)}, u32[]{:S(2)}) collective-permute-start(bf16[48,1536]{1,0:T(8,128)(2,1)S(1)} %get-tuple-element.172), channel_id=1, source_target_pairs={{0,2},{1,3},{2,4},{3,5},{4,6},{5,7},{6,0},{7,1},{8,10},{9,11},{10,... | collective-permute-start | bytes 442376 | tf_op jit(solution)/shard_map/ppermute | solution.py:64
  360.1 9.1 %collective-permute-start.51 = (bf16[48,1536]{1,0:T(8,128)(2,1)S(1)}, bf16[48,1536]{1,0:T(8,128)(2,1)S(1)}, u32[]{:S(2)}, u32[]{:S(2)}) collective-permute-start(bf16[48,1536]{1,0:T(8,128)(2,1)S(1)} %get-tuple-element.177), channel_id=1, source_target_pairs={{0,2},{1,3},{2,4},{3,5},{4,6},{5,7},{6,0},{7,1},{8,10},{9,11},{10,... | collective-permute-start | bytes 442376 | tf_op jit(solution)/shard_map/ppermute | solution.py:64
  360.4 12.5 %collective-permute-start.53 = (bf16[48,1536]{1,0:T(8,128)(2,1)S(1)}, bf16[48,1536]{1,0:T(8,128)(2,1)S(1)}, u32[]{:S(2)}, u32[]{:S(2)}) collective-permute-start(bf16[48,1536]{1,0:T(8,128)(2,1)S(1)} %get-tuple-element.178), channel_id=1, source_target_pairs={{0,6},{1,7},{2,0},{3,1},{4,2},{5,3},{6,4},{7,5},{8,14},{9,15},{10,... | collective-permute-start | bytes 442376 | tf_op jit(solution)/shard_map/ppermute | solution.py:64
  363.9 14.7 %collective-permute-start.52 = (bf16[48,1536]{1,0:T(8,128)(2,1)S(1)}, bf16[48,1536]{1,0:T(8,128)(2,1)S(1)}, u32[]{:S(2)}, u32[]{:S(2)}) collective-permute-start(bf16[48,1536]{1,0:T(8,128)(2,1)S(1)} %get-tuple-element.179), channel_id=1, source_target_pairs={{0,4},{1,5},{2,6},{3,7},{4,0},{5,1},{6,2},{7,3},{8,12},{9,13},{10,... | collective-permute-start | bytes 442376 | tf_op jit(solution)/shard_map/ppermute | solution.py:64
  367.0 14.2 %collective-permute-start.58 = (bf16[48,1536]{1,0:T(8,128)(2,1)S(1)}, bf16[48,1536]{1,0:T(8,128)(2,1)S(1)}, u32[]{:S(2)}, u32[]{:S(2)}) collective-permute-start(bf16[48,1536]{1,0:T(8,128)(2,1)S(1)} %get-tuple-element.173), channel_id=1, source_target_pairs={{0,6},{1,7},{2,0},{3,1},{4,2},{5,3},{6,4},{7,5},{8,14},{9,15},{10,... | collective-permute-start | bytes 442376 | tf_op jit(solution)/shard_map/ppermute | solution.py:64
  369.1 16.9 %collective-permute-start.57 = (bf16[48,1536]{1,0:T(8,128)(2,1)S(1)}, bf16[48,1536]{1,0:T(8,128)(2,1)S(1)}, u32[]{:S(2)}, u32[]{:S(2)}) collective-permute-start(bf16[48,1536]{1,0:T(8,128)(2,1)S(1)} %get-tuple-element.174), channel_id=1, source_target_pairs={{0,4},{1,5},{2,6},{3,7},{4,0},{5,1},{6,2},{7,3},{8,12},{9,13},{10,... | collective-permute-start | bytes 442376 | tf_op jit(solution)/shard_map/ppermute | solution.py:64
  372.9 25.9 %collective-permute-start.44 = (bf16[4,2,48,1536]{3,2,0,1:T(8,128)(2,1)S(1)}, bf16[4,2,48,1536]{3,2,0,1:T(8,128)(2,1)S(1)}, u32[]{:S(2)}, u32[]{:S(2)}) collective-permute-start(bf16[4,2,48,1536]{3,2,0,1:T(8,128)(2,1)S(1)} %copy-done.40), channel_id=1, source_target_pairs={{0,16},{1,17},{2,18},{3,19},{4,20},{5,21},{6,22},{7,23},{8,9},{9,8... | collective-permute-start | bytes 3538952 | tf_op jit(solution)/shard_map/ppermute | solution.py:77
  379.7 14.2 %collective-permute-start.54 = (bf16[48,1536]{1,0:T(8,128)(2,1)S(1)}, bf16[48,1536]{1,0:T(8,128)(2,1)S(1)}, u32[]{:S(2)}, u32[]{:S(2)}) collective-permute-start(bf16[48,1536]{1,0:T(8,128)(2,1)S(1)} %fusion.90), channel_id=1, source_target_pairs={{0,16},{1,17},{2,18},{3,19},{4,20},{5,21},{6,22},{7,23},{8,24},{9,... | collective-permute-start | bytes 442376 | tf_op jit(solution)/shard_map/ppermute | solution.py:64
  386.1 9.3 %collective-permute-start.59 = (bf16[48,1536]{1,0:T(8,128)(2,1)S(1)}, bf16[48,1536]{1,0:T(8,128)(2,1)S(1)}, u32[]{:S(2)}, u32[]{:S(2)}) collective-permute-start(bf16[48,1536]{1,0:T(8,128)(2,1)S(1)} %fusion.87), channel_id=1, source_target_pairs={{0,16},{1,17},{2,18},{3,19},{4,20},{5,21},{6,22},{7,23},{8,24},{9,... | collective-permute-start | bytes 442376 | tf_op jit(solution)/shard_map/ppermute | solution.py:64
  394.1 7.4 %collective-permute-start.29 = (bf16[1792,384]{1,0:T(8,128)(2,1)S(1)}, bf16[1792,384]{1,0:T(8,128)(2,1)S(1)}, u32[]{:S(2)}, u32[]{:S(2)}) collective-permute-start(bf16[1792,384]{1,0:T(8,128)(2,1)S(1)} %pad_maximum_fusion.7), channel_id=1, source_target_pairs={{0,8},{1,9},{2,10},{3,11},{4,12},{5,13},{6,14},{7,15},{8,0},{9,1},... | collective-permute-start | bytes 4128776 | tf_op jit(solution)/shard_map/ppermute | solution.py:64
  395.5 2.5 collective-permute-start.60
  400.0 31.2 %collective-permute-start.45 = (bf16[4,48,1536]{2,1,0:T(8,128)(2,1)}, bf16[4,48,1536]{2,1,0:T(8,128)(2,1)}, u32[]{:S(2)}, u32[]{:S(2)}) collective-permute-start(bf16[4,48,1536]{2,1,0:T(8,128)(2,1)} %dynamic-slice_bitcast_fusion), channel_id=1, source_target_pairs={{0,1},{1,0},{2,3},{3,2},{4,5},{5,4},{6,7},{7,6},{8,24},{9,25},{10,... | collective-permute-start | bytes 1769480 | tf_op jit(solution)/shard_map/ppermute | solution.py:77
  418.6 4.5 collective-permute-start.62
  423.1 5.3 %collective-permute-start.63 = (f32[17,768]{1,0:T(8,128)S(1)}, f32[17,768]{1,0:T(8,128)S(1)}, u32[]{:S(2)}, u32[]{:S(2)}) collective-permute-start(f32[17,768]{1,0:T(8,128)S(1)} %add.671), channel_id=1, source_target_pairs={{0,1},{1,0},{2,3},{3,2},{4,5},{5,4},{6,7},{7,6},{8,9},{9,8},{10,11... | collective-permute-start | bytes 156680 | tf_op jit(solution)/shard_map/ppermute | solution.py:64
  427.6 24.9 %collective-permute-start.30 = (bf16[3,128,768]{2,1,0:T(8,128)(2,1)}, bf16[3,128,768]{2,1,0:T(8,128)(2,1)}, u32[]{:S(2)}, u32[]{:S(2)}) collective-permute-start(bf16[3,128,768]{2,1,0:T(8,128)(2,1)} %bitcast.96), channel_id=1, source_target_pairs={{0,1},{1,0},{2,3},{3,2},{4,5},{5,4},{6,7},{7,6},{8,9},{9,8},{10,11... | collective-permute-start | bytes 1769480 | tf_op jit(solution)/shard_map/ppermute | solution.py:64
  428.4 7.7 %collective-permute-start.66 = (f32[17,768]{1,0:T(8,128)S(1)}, f32[17,768]{1,0:T(8,128)S(1)}, u32[]{:S(2)}, u32[]{:S(2)}) collective-permute-start(f32[17,768]{1,0:T(8,128)S(1)} %add.672), channel_id=1, source_target_pairs={{0,6},{1,7},{2,0},{3,1},{4,2},{5,3},{6,4},{7,5},{8,14},{9,15},{10,... | collective-permute-start | bytes 156680 | tf_op jit(solution)/shard_map/ppermute | solution.py:64
  430.6 8.3 %collective-permute-start.65 = (f32[17,768]{1,0:T(8,128)S(1)}, f32[17,768]{1,0:T(8,128)S(1)}, u32[]{:S(2)}, u32[]{:S(2)}) collective-permute-start(f32[17,768]{1,0:T(8,128)S(1)} %add.672), channel_id=1, source_target_pairs={{0,4},{1,5},{2,6},{3,7},{4,0},{5,1},{6,2},{7,3},{8,12},{9,13},{10,... | collective-permute-start | bytes 156680 | tf_op jit(solution)/shard_map/ppermute | solution.py:64
  430.6 8.4 %collective-permute-start.64 = (f32[17,768]{1,0:T(8,128)S(1)}, f32[17,768]{1,0:T(8,128)S(1)}, u32[]{:S(2)}, u32[]{:S(2)}) collective-permute-start(f32[17,768]{1,0:T(8,128)S(1)} %add.672), channel_id=1, source_target_pairs={{0,2},{1,3},{2,4},{3,5},{4,6},{5,7},{6,0},{7,1},{8,10},{9,11},{10,... | collective-permute-start | bytes 156680 | tf_op jit(solution)/shard_map/ppermute | solution.py:64
  433.3 9.1 %collective-permute-start.46 = (bf16[48,1536]{1,0:T(8,128)(2,1)}, bf16[48,1536]{1,0:T(8,128)(2,1)S(1)}, u32[]{:S(2)}, u32[]{:S(2)}) collective-permute-start(bf16[48,1536]{1,0:T(8,128)(2,1)} %get-tuple-element.182), channel_id=1, source_target_pairs={{0,2},{1,3},{2,4},{3,5},{4,6},{5,7},{6,0},{7,1},{8,10},{9,11},{10,... | collective-permute-start | bytes 442376 | tf_op jit(solution)/shard_map/ppermute | solution.py:64
  436.1 7.3 %collective-permute-start.48 = (bf16[48,1536]{1,0:T(8,128)(2,1)}, bf16[48,1536]{1,0:T(8,128)(2,1)}, u32[]{:S(2)}, u32[]{:S(2)}) collective-permute-start(bf16[48,1536]{1,0:T(8,128)(2,1)} %get-tuple-element.183), channel_id=1, source_target_pairs={{0,6},{1,7},{2,0},{3,1},{4,2},{5,3},{6,4},{7,5},{8,14},{9,15},{10,... | collective-permute-start | bytes 442376 | tf_op jit(solution)/shard_map/ppermute | solution.py:64
  438.9 11.0 %collective-permute-start.47 = (bf16[48,1536]{1,0:T(8,128)(2,1)}, bf16[48,1536]{1,0:T(8,128)(2,1)}, u32[]{:S(2)}, u32[]{:S(2)}) collective-permute-start(bf16[48,1536]{1,0:T(8,128)(2,1)} %get-tuple-element.184), channel_id=1, source_target_pairs={{0,4},{1,5},{2,6},{3,7},{4,0},{5,1},{6,2},{7,3},{8,12},{9,13},{10,... | collective-permute-start | bytes 442376 | tf_op jit(solution)/shard_map/ppermute | solution.py:64
  439.0 30.2 %collective-permute-start.37 = (bf16[4,2,48,1536]{3,2,0,1:T(8,128)(2,1)}, bf16[4,2,48,1536]{3,2,0,1:T(8,128)(2,1)S(1)}, u32[]{:S(2)}, u32[]{:S(2)}) collective-permute-start(bf16[4,2,48,1536]{3,2,0,1:T(8,128)(2,1)} %pad_maximum_fusion.18), channel_id=1, source_target_pairs={{0,16},{1,17},{2,18},{3,19},{4,20},{5,21},{6,22},{7,23},{8,9},{9,8... | collective-permute-start | bytes 3538952 | tf_op jit(solution)/shard_map/ppermute | solution.py:77
  451.0 7.7 %collective-permute-start.49 = (bf16[48,1536]{1,0:T(8,128)(2,1)S(1)}, bf16[48,1536]{1,0:T(8,128)(2,1)S(1)}, u32[]{:S(2)}, u32[]{:S(2)}) collective-permute-start(bf16[48,1536]{1,0:T(8,128)(2,1)S(1)} %fusion.93), channel_id=1, source_target_pairs={{0,16},{1,17},{2,18},{3,19},{4,20},{5,21},{6,22},{7,23},{8,24},{9,... | collective-permute-start | bytes 442376 | tf_op jit(solution)/shard_map/ppermute | solution.py:64
  453.8 9.6 %collective-permute-start.31 = (bf16[128,768]{1,0:T(8,128)(2,1)S(1)}, bf16[128,768]{1,0:T(8,128)(2,1)S(1)}, u32[]{:S(2)}, u32[]{:S(2)}) collective-permute-start(bf16[128,768]{1,0:T(8,128)(2,1)S(1)} %get-tuple-element.190), channel_id=1, source_target_pairs={{2,0},{3,1},{4,2},{5,3},{6,4},{7,5},{10,8},{11,9},{12,10},{13,11},... | collective-permute-start | bytes 589832 | tf_op jit(solution)/shard_map/ppermute | solution.py:93
  455.2 13.7 %collective-permute-start.32 = (bf16[128,768]{1,0:T(8,128)(2,1)S(1)}, bf16[128,768]{1,0:T(8,128)(2,1)S(1)}, u32[]{:S(2)}, u32[]{:S(2)}) collective-permute-start(bf16[128,768]{1,0:T(8,128)(2,1)S(1)} %get-tuple-element.191), channel_id=1, source_target_pairs={{4,0},{5,1},{6,2},{7,3},{12,8},{13,9},{14,10},{15,11},{20,16},{21,... | collective-permute-start | bytes 589832 | tf_op jit(solution)/shard_map/ppermute | solution.py:93
  458.7 12.4 %collective-permute-start.50 = (bf16[96,1536]{1,0:T(8,128)(2,1)S(1)}, bf16[96,1536]{1,0:T(8,128)(2,1)S(1)}, u32[]{:S(2)}, u32[]{:S(2)}) collective-permute-start(bf16[96,1536]{1,0:T(8,128)(2,1)S(1)} %maximum_select_fusion.1), channel_id=1, source_target_pairs={{0,8},{1,9},{2,10},{3,11},{4,12},{5,13},{6,14},{7,15},{8,0},{9,1},... | collective-permute-start | bytes 884744 | tf_op jit(solution)/shard_map/ppermute | solution.py:64
  469.6 9.9 %collective-permute-start.38 = (bf16[4,48,1536]{2,1,0:T(8,128)(2,1)S(1)}, bf16[4,48,1536]{2,1,0:T(8,128)(2,1)S(1)}, u32[]{:S(2)}, u32[]{:S(2)}) collective-permute-start(bf16[4,48,1536]{2,1,0:T(8,128)(2,1)S(1)} %dynamic-slice_bitcast_fusion.1), channel_id=1, source_target_pairs={{0,1},{1,0},{2,3},{3,2},{4,5},{5,4},{6,7},{7,6},{8,24},{9,25},{10,... | collective-permute-start | bytes 1769480 | tf_op jit(solution)/shard_map/ppermute | solution.py:77
  479.7 8.7 %collective-permute-start.39 = (bf16[48,1536]{1,0:T(8,128)(2,1)S(1)}, bf16[48,1536]{1,0:T(8,128)(2,1)S(1)}, u32[]{:S(2)}, u32[]{:S(2)}) collective-permute-start(bf16[48,1536]{1,0:T(8,128)(2,1)S(1)} %get-tuple-element.187), channel_id=1, source_target_pairs={{0,2},{1,3},{2,4},{3,5},{4,6},{5,7},{6,0},{7,1},{8,10},{9,11},{10,... | collective-permute-start | bytes 442376 | tf_op jit(solution)/shard_map/ppermute | solution.py:64
  479.8 8.6 %collective-permute-start.41 = (bf16[48,1536]{1,0:T(8,128)(2,1)S(1)}, bf16[48,1536]{1,0:T(8,128)(2,1)S(1)}, u32[]{:S(2)}, u32[]{:S(2)}) collective-permute-start(bf16[48,1536]{1,0:T(8,128)(2,1)S(1)} %get-tuple-element.188), channel_id=1, source_target_pairs={{0,6},{1,7},{2,0},{3,1},{4,2},{5,3},{6,4},{7,5},{8,14},{9,15},{10,... | collective-permute-start | bytes 442376 | tf_op jit(solution)/shard_map/ppermute | solution.py:64
  483.6 9.8 %collective-permute-start.40 = (bf16[48,1536]{1,0:T(8,128)(2,1)S(1)}, bf16[48,1536]{1,0:T(8,128)(2,1)S(1)}, u32[]{:S(2)}, u32[]{:S(2)}) collective-permute-start(bf16[48,1536]{1,0:T(8,128)(2,1)S(1)} %get-tuple-element.189), channel_id=1, source_target_pairs={{0,4},{1,5},{2,6},{3,7},{4,0},{5,1},{6,2},{7,3},{8,12},{9,13},{10,... | collective-permute-start | bytes 442376 | tf_op jit(solution)/shard_map/ppermute | solution.py:64
  493.5 5.2 %collective-permute-start.42 = (bf16[48,1536]{1,0:T(8,128)(2,1)S(1)}, bf16[48,1536]{1,0:T(8,128)(2,1)S(1)}, u32[]{:S(2)}, u32[]{:S(2)}) collective-permute-start(bf16[48,1536]{1,0:T(8,128)(2,1)S(1)} %fusion.96), channel_id=1, source_target_pairs={{0,16},{1,17},{2,18},{3,19},{4,20},{5,21},{6,22},{7,23},{8,24},{9,... | collective-permute-start | bytes 442376 | tf_op jit(solution)/shard_map/ppermute | solution.py:64
  (98 other events, 514.5 us)
